TPU v7x, 256 devices: a whole 4x4x8 slice. The times are simulated.
256 devices in a mesh: leaf: 16 (over y, x), row: 16 (over z, core).
Axes of the slice: x: 4, y: 4, z: 8, core: 2. Of those that a mesh axis runs over, the one named last changes fastest.
Arguments:
- sigma_root: float32 [2048, 2048], P(None, 'row')
- linv_one: bfloat16 [16, 2048, 2048], P('leaf', None, 'row'), as said below
- panel_one: bfloat16 [16, 512, 2048], P('leaf', None, 'row'), may hold values from -1.25 to 1.25
- tiles_one: int32 [16, 4], replicated, may hold values from 0 to 15, as said below
- mask_one: int32 [16, 4, 16], P('leaf', None, 'row'), may hold values 0 or 1
- linv_two: bfloat16 [16, 2048, 2048], P('leaf', None, 'row'), as said below
- panel_two: bfloat16 [16, 512, 2048], P('leaf', None, 'row'), may hold values from -1.25 to 1.25
- tiles_two: int32 [16, 4], replicated, may hold values from 0 to 15, as said below
- mask_two: int32 [16, 4, 16], P('leaf', None, 'row'), may hold values 0 or 1
- parent: int32 [16], replicated, may hold values from 0 to 15
Outputs:
- sigma_one: float32 [16, 2048, 2048], P('leaf', None, 'row')
- cross_one: float32 [16, 512, 2048], P('leaf', None, 'row')
- sigma_two: float32 [16, 2048, 2048], P('leaf', None, 'row')
- cross_two: float32 [16, 512, 2048], P('leaf', None, 'row')
Inputs may be any that keep to these rules, and one draw needn't show every extreme that they name: `tiles_one`: each row holds 4 different tile numbers in increasing order. `tiles_two`: each row holds 4 different tile numbers in increasing order. `linv_one`: each block is lower triangular with a positive diagonal. `sigma_root`: symmetric. `linv_two`: each block is lower triangular with a positive diagonal.
All inputs are finite; a program needn't handle non-finite values. No bound on the sum of `mask_one` or of `mask_two` on one device may be relied on, other than what follows from the above.
Results may differ from a plain program's by a relative error of at most 0.00045.
Values may be sent and summed in bfloat16 or wider, within the bound.
No kernel may reach another device: no remote copies, remote signals or barrier semaphores. Data moves between devices by JAX's collectives and lax.ppermute only.
A program may use at most 64 MiB of HBM per device.

v0:
```python
import jax
import jax.numpy as jnp
from jax import lax
from jax.sharding import PartitionSpec as P

TILE = 128


def pattern_rows(tile_list):
    offsets = jnp.arange(TILE, dtype=jnp.int32)
    return (tile_list[..., None] * TILE + offsets).reshape(tile_list.shape[:-1] + (-1,))


def expand_mask(tile_mask):
    return jnp.repeat(jnp.repeat(tile_mask, TILE, axis=0), TILE, axis=1)


def assemble(selected, row_list):
    gathered = lax.all_gather(selected, "row", axis=1, tiled=True)
    return jnp.take(gathered, row_list, axis=1)


def solve_block(selected, row_list, linv_local, panel_local, mask_local):
    select = assemble(selected, row_list)
    masked = panel_local * expand_mask(mask_local).astype(jnp.bfloat16)
    linv_wide = linv_local.astype(jnp.float32)
    whole_panel = lax.all_gather(masked, "row", axis=1, tiled=True)
    upper_part = jnp.dot(whole_panel, linv_local, preferred_element_type=jnp.float32)
    cross = -jnp.dot(select, upper_part, precision=lax.Precision.HIGHEST)
    middle = linv_wide - jnp.dot(
        whole_panel.astype(jnp.float32).T, cross, precision=lax.Precision.HIGHEST
    )
    sigma = jnp.dot(
        lax.all_gather(linv_local, "row", axis=1, tiled=True).astype(jnp.float32).T,
        middle,
        precision=lax.Precision.HIGHEST,
    )
    return (sigma, cross)


def body(
    sigma_root,
    linv_one,
    panel_one,
    tiles_one,
    mask_one,
    linv_two,
    panel_two,
    tiles_two,
    mask_two,
    parent,
):
    leaf_id = lax.axis_index("leaf")
    width = sigma_root.shape[1]
    own_tiles = lax.dynamic_index_in_dim(tiles_one, leaf_id, 0, keepdims=False)
    rows_first = pattern_rows(own_tiles)
    selected_first = jnp.take(sigma_root, rows_first, axis=0)
    sigma_first, cross_first = solve_block(
        selected_first, rows_first, linv_one[0], panel_one[0], mask_one[0]
    )
    rows_every = pattern_rows(tiles_two)
    count = rows_every.shape[0]
    block_rows = rows_every.shape[1]
    owned = (parent == leaf_id).astype(jnp.float32)
    slots = jnp.take(sigma_first, rows_every.reshape(-1), axis=0).reshape(count, block_rows, width)
    slots = slots * owned[:, None, None]
    arrived = lax.all_to_all(slots, "leaf", split_axis=0, concat_axis=0, tiled=True)
    selected_second = jnp.sum(arrived, axis=0)
    rows_second = lax.dynamic_index_in_dim(rows_every, leaf_id, 0, keepdims=False)
    sigma_second, cross_second = solve_block(
        selected_second, rows_second, linv_two[0], panel_two[0], mask_two[0]
    )
    return (sigma_first[None], cross_first[None], sigma_second[None], cross_second[None])


def solution(mesh):
    return jax.shard_map(
        body,
        mesh=mesh,
        in_specs=(
            P(None, "row"),
            P("leaf", None, "row"),
            P("leaf", None, "row"),
            P(),
            P("leaf", None, "row"),
            P("leaf", None, "row"),
            P("leaf", None, "row"),
            P(),
            P("leaf", None, "row"),
            P(),
        ),
        out_specs=(
            P("leaf", None, "row"),
            P("leaf", None, "row"),
            P("leaf", None, "row"),
            P("leaf", None, "row"),
        ),
        check_vma=False,
    )
```

profile of v0, /device:TPU:1, one launch (start us, length us, event | category | flops | bytes accessed | tf_op | source)
XLA Modules:
  0.0 404.3 jit_solution(16791441184361963141)
XLA Ops:
  8.1 1.7 bitcast_multiply_fusion.1
  16.1 39.5 %all-gather.9.cloned.1.call-done = bf16[512,2048]{1,0:T(8,128)(2,1)} async-done(((bf16[512,128]{1,0:T(8,128)(2,1)}), bf16[512,2048]{1,0:T(8,128)(2,1)}) %all-gather.9.cloned.1.call-update) | async-done | bytes 2097168 | tf_op jit(solution)/shard_map/all_gather | solution.py:27
  55.5 2.3 fusion.13
  57.8 48.6 %all-gather.11.cloned.1.call-done = f32[512,2048]{1,0:T(8,128)} async-done(((f32[512,128]{1,0:T(8,128)}), f32[512,2048]{1,0:T(8,128)}) %all-gather.11.cloned.1.call-update) | async-done | bytes 4194320 | tf_op jit(solution)/shard_map/all_gather | solution.py:19
  106.5 5.3 %copy.19 = f32[512,2048]{0,1:T(8,128)} copy(f32[512,2048]{1,0:T(8,128)} %all-gather.11.cloned.1.call-done) | data formatting | bytes 8388608 | tf_op jit(solution)/shard_map/all_gather | solution.py:19
  111.8 4.2 %gather_fusion.2 = f32[512,512]{1,0:T(8,128)S(1)} fusion(f32[512,2048]{0,1:T(8,128)} %copy.19, s32[1024]{0:T(1024)S(1)} %pad_clamp_fusion.1), kind=kCustom, calls=%fused_computation.clone | custom fusion | bytes 2099200 | tf_op jit(solution)/shard_map/jit(_take)/gather | solution.py:20
  116.0 1.9 convolution_negate_fusion.1
  118.6 3.9 convolution_subtract_fusion.1
  122.6 50.3 %all-gather.17.cloned.1.call-done = bf16[1,2048,2048]{2,1,0:T(8,128)(2,1)} async-done(((bf16[1,2048,128]{2,1,0:T(8,128)(2,1)}), bf16[1,2048,2048]{2,1,0:T(8,128)(2,1)}) %all-gather.17.cloned.1.call-update) | async-done | bytes 8388624 | tf_op jit(solution)/shard_map/all_gather | solution.py:34
  172.9 6.3 %fusion.2 = f32[128,2048]{1,0:T(8,128)S(1)} fusion(f32[2048,128]{1,0:T(8,128)S(1)} %convolution_subtract_fusion.1, bf16[1,2048,2048]{2,1,0:T(8,128)(2,1)} %all-gather.17.cloned.1.call-done), kind=kOutput, calls=%fused_computation.6 | convolution fusion | flops 6442450944 | bytes 10485760 | tf_op jit(solution)/shard_map/dot_general | solution.py:33
  179.5 27.8 %gather_fusion.1 = f32[8192,128]{1,0:T(8,128)} fusion(f32[2048,128]{1,0:T(8,128)S(1)} %copy.21, s32[8192]{0:T(1024)S(1)} %broadcast_clamp_fusion), kind=kCustom, calls=%fused_computation.3 | custom fusion | bytes 8421376 | tf_op jit(solution)/shard_map/jit(_take)/gather | solution.py:65
  207.3 5.3 %select_multiply_fusion = f32[16,512,128]{2,1,0:T(8,128)} fusion(f32[16,512,128]{2,1,0:T(8,128)} %bitcast.84, f32[16]{0:T(128)S(1)} %compare_convert_fusion, pred[16,512]{1,0:T(8,128)(4,1)S(1)} %compare_and_fusion), kind=kLoop, calls=%fused_computation.8 | loop fusion | flops 2097152 | bytes 8396864 | tf_op jit(solution)/shard_map/mul | solution.py:66
  212.5 4.7 %all-to-all-start = ((f32[16,512,128]{2,1,0:T(8,128)}), f32[16,512,128]{2,1,0:T(8,128)}, u32[]{:S(2)}, u32[]{:S(2)}) async-start(f32[16,512,128]{2,1,0:T(8,128)} %select_multiply_fusion), calls=%async_computation | async-start | bytes 8388608 | tf_op jit(solution)/shard_map/all_to_all | solution.py:67
  218.2 62.3 %all-to-all-done = f32[16,512,128]{2,1,0:T(8,128)} async-done(((f32[16,512,128]{2,1,0:T(8,128)}), f32[16,512,128]{2,1,0:T(8,128)}, u32[]{:S(2)}, u32[]{:S(2)}) %all-to-all-start) | async-done | bytes 4194336 | tf_op jit(solution)/shard_map/all_to_all | solution.py:67
  280.5 2.4 reduce_sum.9
  284.4 2.3 fusion.11
  286.7 1.3 copy.23
  288.0 35.5 %all-gather.15.cloned.1.call-done = f32[512,2048]{0,1:T(8,128)} async-done(((f32[512,128]{0,1:T(8,128)}), f32[512,2048]{0,1:T(8,128)}) %all-gather.15.cloned.1.call-update) | async-done | bytes 4194320 | tf_op jit(solution)/shard_map/all_gather | solution.py:19
  323.6 4.2 %gather_fusion.3 = f32[512,512]{1,0:T(8,128)S(1)} fusion(f32[512,2048]{0,1:T(8,128)} %all-gather.15.cloned.1.call-done, s32[1024]{0:T(1024)S(1)} %pad_clamp_fusion), kind=kCustom, calls=%fused_computation.1.clone | custom fusion | bytes 2099200 | tf_op jit(solution)/shard_map/jit(_take)/gather | solution.py:20
  327.8 1.9 convolution_negate_fusion
  329.7 4.0 convolution_subtract_fusion
  333.7 56.2 %all-gather.19.cloned.1.call-done = bf16[1,2048,2048]{2,1,0:T(8,128)(2,1)} async-done(((bf16[1,2048,128]{2,1,0:T(8,128)(2,1)}), bf16[1,2048,2048]{2,1,0:T(8,128)(2,1)}) %all-gather.19.cloned.1.call-update) | async-done | bytes 8388624 | tf_op jit(solution)/shard_map/all_gather | solution.py:34
  389.9 6.3 %fusion.4 = f32[1,2048,128]{1,2,0:T(8,128)S(1)} fusion(f32[2048,128]{1,0:T(8,128)S(1)} %convolution_subtract_fusion, bf16[1,2048,2048]{2,1,0:T(8,128)(2,1)} %all-gather.19.cloned.1.call-done), kind=kOutput, calls=%fused_computation.9 | convolution fusion | flops 6442450944 | bytes 10485760 | tf_op jit(solution)/shard_map/dot_general | solution.py:33
  396.2 1.3 copy.24
  (58 shorter events, 10.5 us)
Async XLA Ops:
  7.2 3.6 copy-start
  7.2 48.4 %copy-start.1 = (bf16[1,2048,128]{2,1,0:T(8,128)(2,1)S(1)}, bf16[1,2048,128]{2,1,0:T(8,128)(2,1)}, u32[]{:S(2)}) copy-start(bf16[1,2048,128]{2,1,0:T(8,128)(2,1)} %param.13) | copy-start | bytes 1572868
  7.2 48.3 %all-gather.9.cloned.1.call-start = ((), (), s32[]{:S(2)}) async-start(), calls=%async_computation.1 | async-start | bytes 2228224 | tf_op jit(solution)/shard_map/all_gather | solution.py:27
  9.8 96.7 %all-gather.11.cloned.1.call-start = ((), (), s32[]{:S(2)}) async-start(), calls=%async_computation.2 | async-start | bytes 4456448 | tf_op jit(solution)/shard_map/all_gather | solution.py:19
  12.8 160.1 %all-gather.17.cloned.1.call-start = ((), (), s32[]{:S(2)}) async-start(), calls=%async_computation.5 | async-start | bytes 8912896 | tf_op jit(solution)/shard_map/all_gather | solution.py:34
  117.9 0.7 copy-start.4
  212.5 4.8 %copy-start.6 = (bf16[1,512,128]{2,1,0:T(8,128)(2,1)S(1)}, bf16[1,512,128]{2,1,0:T(8,128)(2,1)}, u32[]{:S(2)}) copy-start(bf16[1,512,128]{2,1,0:T(8,128)(2,1)} %param.18) | copy-start | bytes 393220
  212.5 67.9 %all-to-all-start = ((f32[16,512,128]{2,1,0:T(8,128)}), f32[16,512,128]{2,1,0:T(8,128)}, u32[]{:S(2)}, u32[]{:S(2)}) async-start(f32[16,512,128]{2,1,0:T(8,128)} %select_multiply_fusion), calls=%async_computation | async-start | bytes 8388608 | tf_op jit(solution)/shard_map/all_to_all | solution.py:67
  217.2 67.2 %copy-start.2 = (bf16[1,2048,128]{2,1,0:T(8,128)(2,1)S(1)}, bf16[1,2048,128]{2,1,0:T(8,128)(2,1)}, u32[]{:S(2)}) copy-start(bf16[1,2048,128]{2,1,0:T(8,128)(2,1)} %param.17) | copy-start | bytes 1572868
  217.2 67.2 %all-gather.13.cloned.1.call-start = ((), (), s32[]{:S(2)}) async-start(), calls=%async_computation.3 | async-start | bytes 2228224 | tf_op jit(solution)/shard_map/all_gather | solution.py:27
  218.1 105.4 %all-gather.15.cloned.1.call-start = ((), (), s32[]{:S(2)}) async-start(), calls=%async_computation.4 | async-start | bytes 4456448 | tf_op jit(solution)/shard_map/all_gather | solution.py:19
  283.7 106.2 %all-gather.19.cloned.1.call-start = ((), (), s32[]{:S(2)}) async-start(), calls=%async_computation.6 | async-start | bytes 8912896 | tf_op jit(solution)/shard_map/all_gather | solution.py:34
  288.0 41.6 %copy-start.3 = (bf16[1,2048,128]{2,1,0:T(8,128)(2,1)S(1)}, bf16[1,2048,128]{2,1,0:T(8,128)(2,1)}, u32[]{:S(2)}) copy-start(bf16[1,2048,128]{2,1,0:T(8,128)(2,1)} %param.17) | copy-start | bytes 1572868
  329.7 4.0 copy-start.5
Sparse Core Ops, SparseCore 0:
  10.4 45.1 all-gather.8
  57.9 48.5 all-gather.10
  108.2 64.6 all-gather.16
  220.1 40.0 all-gather.12
  283.9 39.6 all-gather.14
  325.2 64.6 all-gather.18
where the time goes:
time: 405 us; the launch traced here: 404 us
  waiting for transfers between devices  294 us (73%)
  local copies, waits for them, and re-layouts  47.4 us (12%)
  matrix products  28.8 us (7%)
  other arithmetic  15.1 us (4%)
  between operations  14.4 us (4%)
  starting transfers between devices  5.12 us (1%)
    all_gather x2, waiting for transfers between devices, solve_block(): lax.all_gather(linv_local, 'row', axis=1, tiled=True).astype(jnp.float32)  107 us
    all_gather x2, waiting for transfers between devices, assemble(): gathered = lax.all_gather(selected, 'row', axis=1, tiled=True)  84.1 us
    all_to_all x1, waiting for transfers between devices, body(): lax.all_to_all(slots, 'leaf', split_axis=0, concat_axis=0, tiled=True)  62.3 us
    all_gather x2, waiting for transfers between devices, solve_block(): whole_panel = lax.all_gather(masked, 'row', axis=1, tiled=True)  39.5 us
    gather x1, local copies, waits for them, and re-layouts, body(): jnp.take(sigma_first, rows_every.reshape(-1), axis=0)  27.8 us
    dot_general x2, matrix products, solve_block(): jnp.dot(lax.all_gather(linv_local, 'row', axis=1, tiled=True).astype(jnp....  12.5 us
    gather x2, local copies, waits for them, and re-layouts, assemble(): return jnp.take(gathered, row_list, axis=1)  8.43 us
  transfers between devices with their start and end apart: 7, of which 6 were waited for; matrix products, arithmetic and copies ran while one was open for 10% of the time, Pallas kernels for 0%

commit v1 on v0

v1 whole, which is shorter than its diff:
```python
import functools

import jax
import jax.numpy as jnp
from jax import lax
from jax.experimental import pallas as pl
from jax.experimental.pallas import tpu as pltpu
from jax.sharding import PartitionSpec as P

TILE = 128
BF = jnp.bfloat16
F32 = jnp.float32
VMEM_SPEC = pl.BlockSpec(memory_space=pltpu.VMEM)
SMEM_SPEC = pl.BlockSpec(memory_space=pltpu.SMEM)
HBM_SPEC = pl.BlockSpec(memory_space=pltpu.HBM)
VMEM_LIMIT = 40 << 20
SOLVE_LIMIT = 60 << 20
SENT = 3


def split(x):
    high = x.astype(BF)
    return high, (x - high.astype(F32)).astype(BF)


def dot(a, b):
    return jnp.dot(a, b, preferred_element_type=F32)


def sent_tiles(tiles_ref, block, row_id):
    count = tiles_ref.shape[1]
    place = jnp.int32(0)
    for a in range(1, count):
        place = jnp.where(tiles_ref[block, a] == row_id, jnp.int32(a), place)
    picks = []
    for j in range(SENT):
        index = place + j
        picks.append(tiles_ref[block, jnp.where(index >= count, index - count, index)])
    return picks


def pack_kernel(with_select, mask_ref, panel_ref, linv_ref, *rest):
    if with_select:
        tiles_ref, select_ref, out_ref = rest
    else:
        (out_ref,) = rest
    kb = panel_ref.shape[0]
    ns = linv_ref.shape[0]
    for a in range(kb // TILE):
        rows = pl.ds(a * TILE, TILE)
        weight = mask_ref[a, 0].astype(F32)
        out_ref[rows, :] = (panel_ref[rows, :].astype(F32) * weight).astype(BF)
    out_ref[pl.ds(kb, ns), :] = linv_ref[...]
    if with_select:
        picks = sent_tiles(tiles_ref, lax.axis_index("leaf"), lax.axis_index("row"))
        for j in range(SENT):
            start = pl.multiple_of(picks[j] * TILE, TILE)
            high, low = split(select_ref[pl.ds(start, TILE), :])
            out_ref[pl.ds(kb + ns + j * TILE, TILE), :] = high
            out_ref[pl.ds(kb + ns + (SENT + j) * TILE, TILE), :] = low


def pack(mask, panel, linv, tiles=None, select=None):
    kb, width = panel.shape
    ns = linv.shape[0]
    extra = 0 if select is None else 2 * SENT * TILE
    operands = [mask, panel, linv]
    in_specs = [SMEM_SPEC, VMEM_SPEC, VMEM_SPEC]
    if select is not None:
        operands += [tiles, select]
        in_specs += [SMEM_SPEC, VMEM_SPEC]
    return pl.pallas_call(
        functools.partial(pack_kernel, select is not None),
        out_shape=jax.ShapeDtypeStruct((kb + ns + extra, width), BF),
        in_specs=in_specs,
        out_specs=VMEM_SPEC,
        compiler_params=pltpu.CompilerParams(vmem_limit_bytes=VMEM_LIMIT),
        cost_estimate=pl.CostEstimate(
            flops=0, transcendentals=0, bytes_accessed=2 * 2 * (kb + ns + extra) * width
        ),
        name="pack",
    )(*operands)


def solve_kernel(
    first, blocks, kb, tiles_ref, gath_ref, own_ref, *rest
):
    if first:
        slot_ref, sigma_ref, cross_ref, slots_ref = rest[:4]
        lm, lv, raw, sh, sl, mt, lm_sem, s_sem, lv_sem, out_sem = rest[4:]
    else:
        ancestor_ref, sigma_ref, cross_ref = rest[:3]
        lm, lv, raw, sh, sl, mt, lm_sem, s_sem, lv_sem = rest[3:]
    ns = blocks * TILE
    wide = 2 * TILE
    pairs = blocks // 2
    k = kb // TILE
    leaf_id = lax.axis_index("leaf")
    copies = [pltpu.make_async_copy(gath_ref.at[:, pl.ds(0, kb), :], lm, lm_sem)]
    for b in range(k):
        tile = tiles_ref[leaf_id, b]
        if first:
            source = gath_ref.at[tile, pl.ds(kb + ns, 2 * SENT * TILE), :]
        else:
            source = ancestor_ref.at[tile]
        copies.append(pltpu.make_async_copy(source, raw.at[b], s_sem.at[b]))
    lv_copies = []
    for j in range(pairs):
        lv_copies.append(
            pltpu.make_async_copy(
                gath_ref.at[pl.ds(2 * j, 2), pl.ds(kb + wide * j, ns - wide * j), :],
                lv.at[pl.ds(2 * j, 2), pl.ds(wide * j, ns - wide * j), :],
                lv_sem.at[j],
            )
        )
    for copy in copies + lv_copies:
        copy.start()

    def panel(j):
        return jnp.concatenate([lm[2 * j], lm[2 * j + 1]], axis=1)

    copies[0].wait()
    upper = jnp.zeros((kb, TILE), F32)
    for j in range(pairs):
        upper = upper + dot(panel(j), own_ref[pl.ds(wide * j, wide), :])
    upper_high, upper_low = split(upper)
    for b in range(k):
        copies[1 + b].wait()
        for j in range(SENT):
            if first:
                high = raw[b, pl.ds(j * TILE, TILE), :]
                low = raw[b, pl.ds((SENT + j) * TILE, TILE), :]
            else:
                high, low = split(raw[b, pl.ds(j * TILE, TILE), :])
            a = (b + j) % k
            sh[pl.ds(a * TILE, TILE), pl.ds(b * TILE, TILE)] = high
            sl[pl.ds(a * TILE, TILE), pl.ds(b * TILE, TILE)] = low
            if j == 1:
                sh[pl.ds(b * TILE, TILE), pl.ds(a * TILE, TILE)] = high.astype(F32).T.astype(BF)
                sl[pl.ds(b * TILE, TILE), pl.ds(a * TILE, TILE)] = low.astype(F32).T.astype(BF)
    both = dot(sh[...], jnp.concatenate([upper_high, upper_low], axis=1))
    cross = -(both[:, :TILE] + both[:, TILE:] + dot(sl[...], upper_high))
    cross_ref[...] = cross
    cross_high, cross_low = split(cross.T)
    stacked = jnp.concatenate([cross_high, cross_low], axis=0)
    for j in range(pairs):
        rows = pl.ds(wide * j, wide)
        part = dot(stacked, panel(j))
        middle = own_ref[rows, :].astype(F32).T - (part[:TILE] + part[TILE:])
        middle_high, middle_low = split(middle)
        mt[pl.ds(0, TILE), rows] = middle_high
        mt[pl.ds(TILE, TILE), rows] = middle_low
    for j in range(pairs):
        lv_copies[j].wait()
        total = jnp.zeros((wide, wide), F32)
        for i in range(j, pairs):
            rows = pl.ds(wide * i, wide)
            total = total + dot(
                mt[:, rows], jnp.concatenate([lv[2 * j, rows, :], lv[2 * j + 1, rows, :]], axis=1)
            )
        sigma_ref[pl.ds(wide * j, wide), :] = (total[:TILE] + total[TILE:]).T
    if first:
        out_copies = []
        row_id = lax.axis_index("row")
        for p in range(slots_ref.shape[0]):
            picks = sent_tiles(slot_ref, p, row_id)
            for j in range(SENT):
                start = pl.multiple_of(picks[j] * TILE, TILE)
                out_copies.append(
                    pltpu.make_async_copy(
                        sigma_ref.at[pl.ds(start, TILE), :],
                        slots_ref.at[p, pl.ds(j * TILE, TILE), :],
                        out_sem.at[p * SENT + j],
                    )
                )
        for copy in out_copies:
            copy.start()
        for copy in out_copies:
            copy.wait()


def solve(tiles, gathered, own, kb, slot_tiles=None, ancestor=None):
    first = ancestor is None
    blocks = gathered.shape[0]
    ns, width = own.shape
    k = kb // TILE
    outs = [
        jax.ShapeDtypeStruct((ns, width), F32),
        jax.ShapeDtypeStruct((kb, width), F32),
    ]
    out_specs = [VMEM_SPEC, VMEM_SPEC]
    scratch = [
        pltpu.VMEM((blocks, kb, width), BF),
        pltpu.VMEM((blocks, ns, width), BF),
        pltpu.VMEM((k, 2 * SENT * TILE, width), BF)
        if first
        else pltpu.VMEM((k, SENT * TILE, width), F32),
        pltpu.VMEM((kb, kb), BF),
        pltpu.VMEM((kb, kb), BF),
        pltpu.VMEM((2 * TILE, ns), BF),
        pltpu.SemaphoreType.DMA,
        pltpu.SemaphoreType.DMA((k,)),
        pltpu.SemaphoreType.DMA((blocks // 2,)),
    ]
    operands = [tiles, gathered, own]
    in_specs = [SMEM_SPEC, HBM_SPEC, VMEM_SPEC]
    if first:
        operands.append(slot_tiles)
        in_specs.append(SMEM_SPEC)
        count = slot_tiles.shape[0]
        outs.append(jax.ShapeDtypeStruct((count, SENT * TILE, width), F32))
        out_specs.append(HBM_SPEC)
        scratch.append(pltpu.SemaphoreType.DMA((count * SENT,)))
    else:
        operands.append(ancestor)
        in_specs.append(HBM_SPEC)
    return pl.pallas_call(
        functools.partial(solve_kernel, first, blocks, kb),
        out_shape=outs,
        in_specs=in_specs,
        out_specs=out_specs,
        scratch_shapes=scratch,
        compiler_params=pltpu.CompilerParams(vmem_limit_bytes=SOLVE_LIMIT),
        cost_estimate=pl.CostEstimate(
            flops=4 * ns * ns * width, transcendentals=0, bytes_accessed=14 << 20
        ),
        name="solve_first" if first else "solve_second",
    )(*operands)


def body(
    sigma_root,
    linv_one,
    panel_one,
    tiles_one,
    mask_one,
    linv_two,
    panel_two,
    tiles_two,
    mask_two,
    parent,
):
    leaf_id = lax.axis_index("leaf")
    kb = panel_one.shape[1]
    source = lax.dynamic_index_in_dim(parent, leaf_id, 0, keepdims=False)
    packed_one = pack(mask_one[0], panel_one[0], linv_one[0], tiles_one, sigma_root)
    packed_two = pack(mask_two[0], panel_two[0], linv_two[0])
    gathered_one = lax.all_gather(packed_one, "row", axis=0)
    gathered_one, packed_two = lax.optimization_barrier((gathered_one, packed_two))
    gathered_two = lax.all_gather(packed_two, "row", axis=0)
    sigma_first, cross_first, slots = solve(
        tiles_one, gathered_one, linv_one[0], kb, slot_tiles=tiles_two
    )
    arrived = lax.all_to_all(slots, "leaf", split_axis=0, concat_axis=0, tiled=True)
    chosen = lax.dynamic_index_in_dim(arrived, source, 0, keepdims=False)
    chosen, gathered_two = lax.optimization_barrier((chosen, gathered_two))
    ancestor = lax.all_gather(chosen, "row", axis=0)
    sigma_second, cross_second = solve(
        tiles_two, gathered_two, linv_two[0], kb, ancestor=ancestor
    )
    return (sigma_first[None], cross_first[None], sigma_second[None], cross_second[None])


def solution(mesh):
    return jax.shard_map(
        body,
        mesh=mesh,
        in_specs=(
            P(None, "row"),
            P("leaf", None, "row"),
            P("leaf", None, "row"),
            P(),
            P("leaf", None, "row"),
            P("leaf", None, "row"),
            P("leaf", None, "row"),
            P(),
            P("leaf", None, "row"),
            P(),
        ),
        out_specs=(
            P("leaf", None, "row"),
            P("leaf", None, "row"),
            P("leaf", None, "row"),
            P("leaf", None, "row"),
        ),
        check_vma=False,
    )
```

time: 405 us -> 227 us (0.56)
  waiting for transfers between devices: 294 us -> 167 us
  local copies, waits for them, and re-layouts: 47.4 us -> 6.8 us
  Pallas kernels: 0 us -> 30.9 us
  matrix products: 28.8 us -> 0 us
  other arithmetic: 15.1 us -> 0 us
    all_gather x6 -> x3, waiting for transfers between devices: 230 us -> 122 us  [the longest x1 83.3 us: body(): gathered_one = lax.all_gather(packed_one, 'row', axis=0)]
    gather x4 -> x0, local copies, waits for them, and re-layouts: 37.2 us -> none  [the longest x1 27.8 us: body(): jnp.take(sigma_first, rows_every.reshape(-1), axis=0)]
    pallas_call x0 -> x4, Pallas kernels: none -> 30.9 us  [the longest x2 27.7 us: solve(): pl.pallas_call(functools.partial(solve_kernel, first, blocks, kb), out_sh...]
    dot_general x8 -> x0, matrix products: 28.8 us -> none  [the longest x2 12.5 us: solve_block(): jnp.dot(lax.all_gather(linv_local, 'row', axis=1, tiled=True).astype(jnp....]
    all_to_all x1, waiting for transfers between devices: 62.3 us -> 45.2 us  [body(): lax.all_to_all(slots, 'leaf', split_axis=0, concat_axis=0, tiled=True)]
    mul x5 -> x0, other arithmetic: 9.31 us -> none  [the longest x1 5.27 us: body(): slots = slots * owned[:, None, None]]
    all_gather x1 -> x0, local copies, waits for them, and re-layouts: 5.34 us -> none  [assemble(): gathered = lax.all_gather(selected, 'row', axis=1, tiled=True)]
  transfers between devices with their start and end apart: 7 -> 4, of which waited for: 6 -> 3; matrix products, arithmetic and copies ran while one was open for 10% -> 1% of each run, Pallas kernels for 0% -> 7%
where the time goes in v1:
time: 227 us
  waiting for transfers between devices  167 us (74%)
  Pallas kernels  30.9 us (14%)
  between operations  15.8 us (7%)
  local copies, waits for them, and re-layouts  6.8 us (3%)
  starting transfers between devices  6.66 us (3%)
    all_gather x1, waiting for transfers between devices, body(): gathered_one = lax.all_gather(packed_one, 'row', axis=0)  83.3 us
    all_to_all x1, waiting for transfers between devices, body(): lax.all_to_all(slots, 'leaf', split_axis=0, concat_axis=0, tiled=True)  45.2 us
    all_gather x1, waiting for transfers between devices, body(): ancestor = lax.all_gather(chosen, 'row', axis=0)  38.4 us
    pallas_call x2, Pallas kernels, solve(): pl.pallas_call(functools.partial(solve_kernel, first, blocks, kb), out_sh...  27.7 us
    all_to_all x1, starting transfers between devices, body(): lax.all_to_all(slots, 'leaf', split_axis=0, concat_axis=0, tiled=True)  6.54 us
    unnamed x20, local copies, waits for them, and re-layouts  4.68 us
  transfers between devices with their start and end apart: 4, of which 3 were waited for; matrix products, arithmetic and copies ran while one was open for 1% of the time, Pallas kernels for 7%

profile of v1, /device:TPU:1, one launch (start us, length us, event | category | flops | bytes accessed | tf_op | source)
XLA Modules:
  0.0 227.1 jit_solution(2334988459512481446)
XLA Ops:
  7.2 0.0 copy-start
  7.2 0.0 all-gather.7.cloned.1.call-start
  7.2 0.8 copy.17.rest_0_.tiles_ref
  8.0 0.7 copy.14.mask_ref
  8.8 1.0 copy-done.1
  9.8 1.2 copy-done.2
  11.1 0.9 copy-done.3
  12.0 1.7 pack.2
  13.6 0.0 all-gather.7.cloned.1.call-update
  13.6 0.0 all-gather.9.cloned.1.call-start
  13.7 0.1 copy.16.mask_ref
  13.8 1.5 pack.3
  15.3 83.3 %all-gather.7.cloned.1.call-done = bf16[53248,128]{1,0:T(8,128)(2,1)} async-done(((bf16[3328,128]{1,0:T(8,128)(2,1)}), bf16[53248,128]{1,0:T(8,128)(2,1)}) %all-gather.7.cloned.1.call-update) | async-done | bytes 13631504 | tf_op jit(solution)/shard_map/all_gather | solution.py:248
  98.6 0.0 all-gather.9.cloned.1.call-update
  98.6 0.7 copy.18.rest_0_.tiles_ref
  99.3 15.0 %solve_first.1 = (f32[2048,128]{1,0:T(8,128)}, f32[512,128]{1,0:T(8,128)}, f32[16,384,128]{2,1,0:T(8,128)}) custom-call(s32[16,4]{1,0:T(8,128)} %copy-done.5, bf16[16,3328,128]{2,1,0:T(8,128)(2,1)} %bitcast.22, bf16[2048,128]{1,0:T(8,128)(2,1)} %bitcast.18, s32[16,4]{1,0:T(8,128)} %copy.18.rest_0_.tiles_ref), custom_call_target="tpu_custom_call" | custom-call | flops 2147483648 | bytes 14680064 | tf_op jit(solution)/shard_map/solve_first/pallas_call | solution.py:217
  114.3 6.5 %all-to-all-start = ((f32[16,384,128]{2,1,0:T(8,128)}), f32[16,384,128]{2,1,0:T(8,128)S(1)}, u32[]{:S(2)}, u32[]{:S(2)}) async-start(f32[16,384,128]{2,1,0:T(8,128)} %get-tuple-element.16), calls=%async_computation | async-start | bytes 6291456 | tf_op jit(solution)/shard_map/all_to_all | solution.py:254
  120.9 0.0 all-gather.11.cloned.1.call-start
  121.0 0.6 dynamic_slice.8
  123.5 45.2 %all-to-all-done = f32[16,384,128]{2,1,0:T(8,128)S(1)} async-done(((f32[16,384,128]{2,1,0:T(8,128)}), f32[16,384,128]{2,1,0:T(8,128)S(1)}, u32[]{:S(2)}, u32[]{:S(2)}) %all-to-all-start) | async-done | bytes 3145760 | tf_op jit(solution)/shard_map/all_to_all | solution.py:254
  168.7 0.7 dynamic-slice_bitcast_fusion
  169.4 0.0 all-gather.11.cloned.1.call-update
  169.4 38.4 %all-gather.11.cloned.1.call-done = f32[6144,128]{1,0:T(8,128)} async-done(((f32[384,128]{1,0:T(8,128)}), f32[6144,128]{1,0:T(8,128)}) %all-gather.11.cloned.1.call-update) | async-done | bytes 3145744 | tf_op jit(solution)/shard_map/all_gather | solution.py:257
  207.8 12.7 %solve_second.1 = (f32[2048,128]{1,0:T(8,128)}, f32[512,128]{1,0:T(8,128)}) custom-call(s32[16,4]{1,0:T(8,128)} %copy.18.rest_0_.tiles_ref, bf16[16,2560,128]{2,1,0:T(8,128)(2,1)} %bitcast.23, bf16[2048,128]{1,0:T(8,128)(2,1)} %bitcast.16, f32[16,384,128]{2,1,0:T(8,128)} %bitcast.24), custom_call_target="tpu_custom_call" | custom-call | flops 2147483648 | bytes 14680064 | tf_op jit(solution)/shard_map/solve_second/pallas_call | solution.py:217
  (15 shorter events, 0.0 us)
Async XLA Ops:
  7.2 6.6 %copy-start = (bf16[1,2048,128]{2,1,0:T(8,128)(2,1)S(1)}, bf16[1,2048,128]{2,1,0:T(8,128)(2,1)}, u32[]{:S(2)}) copy-start(bf16[1,2048,128]{2,1,0:T(8,128)(2,1)} %param.15) | copy-start | bytes 1572868
  7.2 91.4 %all-gather.7.cloned.1.call-start = ((), (), s32[]{:S(2)}) async-start(), calls=%async_computation.1 | async-start | bytes 14483456 | tf_op jit(solution)/shard_map/all_gather | solution.py:248
  8.0 91.3 %copy-start.5 = (s32[16,4]{1,0:T(8,128)}, s32[16,4]{1,0:T(8,128)S(1)}, u32[]{:S(2)}) copy-start(s32[16,4]{1,0:T(8,128)S(1)} %copy.17.rest_0_.tiles_ref) | copy-start | bytes 772
  8.8 1.0 copy-start.1
  9.8 1.2 copy-start.2
  11.0 0.9 copy-start.3
  12.0 1.7 copy-start.7
  12.0 1.8 copy-start.4
  12.0 86.7 %copy-start.6 = (s32[16,4]{0,1:T(4,128)S(1)}, s32[16,4]{0,1:T(4,128)}, u32[]{:S(2)}) copy-start(s32[16,4]{0,1:T(4,128)} %param.17) | copy-start | bytes 772
  13.6 155.8 %all-gather.9.cloned.1.call-start = ((), (), s32[]{:S(2)}) async-start(), calls=%async_computation.2 | async-start | bytes 11141120 | tf_op jit(solution)/shard_map/all_gather | solution.py:250
  114.3 6.6 %copy-start.8 = (s32[16]{0:T(128)S(1)}, s32[16]{0:T(128)}, u32[]{:S(2)}) copy-start(s32[16]{0:T(128)} %param.19) | copy-start | bytes 196
  114.3 54.4 %all-to-all-start = ((f32[16,384,128]{2,1,0:T(8,128)}), f32[16,384,128]{2,1,0:T(8,128)S(1)}, u32[]{:S(2)}, u32[]{:S(2)}) async-start(f32[16,384,128]{2,1,0:T(8,128)} %get-tuple-element.16), calls=%async_computation | async-start | bytes 6291456 | tf_op jit(solution)/shard_map/all_to_all | solution.py:254
  120.9 86.9 %all-gather.11.cloned.1.call-start = ((), (), s32[]{:S(2)}) async-start(), calls=%async_computation.3 | async-start | bytes 3342336 | tf_op jit(solution)/shard_map/all_gather | solution.py:257
Sparse Core Ops, SparseCore 0:
  13.8 84.8 all-gather.6
  100.4 64.3 all-gather.8
  169.6 38.2 all-gather.10

commit v2 on v1

--- a/solution.py
+++ b/solution.py
@@ -16,11 +16,21 @@
 VMEM_LIMIT = 40 << 20
 SOLVE_LIMIT = 60 << 20
 SENT = 3
+SCALES = 16
+STEPS = 256.0
+TOP = 32512.0
 
 
 def split(x):
     high = x.astype(BF)
     return high, (x - high.astype(F32)).astype(BF)
+
+
+def code_tile(x):
+    peak = jnp.max(jnp.abs(x), axis=0, keepdims=True)
+    code = jnp.clip(jnp.ceil(jnp.log2(peak) * STEPS), -110.0 * STEPS, 127.0 * STEPS)
+    levels = jnp.round(x * (TOP / jnp.exp2(code * (1.0 / STEPS))))
+    return levels.astype(jnp.int32), code
 
 
 def dot(a, b):
@@ -87,7 +97,7 @@
 ):
     if first:
         slot_ref, sigma_ref, cross_ref, slots_ref = rest[:4]
-        lm, lv, raw, sh, sl, mt, lm_sem, s_sem, lv_sem, out_sem = rest[4:]
+        lm, lv, raw, sh, sl, mt, lm_sem, s_sem, lv_sem, levels_ref, out_sem = rest[4:]
     else:
         ancestor_ref, sigma_ref, cross_ref = rest[:3]
         lm, lv, raw, sh, sl, mt, lm_sem, s_sem, lv_sem = rest[3:]
@@ -126,12 +136,22 @@
     upper_high, upper_low = split(upper)
     for b in range(k):
         copies[1 + b].wait()
+        if not first:
+            codes = raw[b, pl.ds(SENT * TILE, SCALES), :].astype(jnp.int32).astype(F32)
+            code_row = lax.broadcasted_iota(jnp.int32, codes.shape, 0)
         for j in range(SENT):
             if first:
                 high = raw[b, pl.ds(j * TILE, TILE), :]
                 low = raw[b, pl.ds((SENT + j) * TILE, TILE), :]
             else:
-                high, low = split(raw[b, pl.ds(j * TILE, TILE), :])
+                code = jnp.sum(
+                    jnp.where(code_row == tiles_ref[leaf_id, (b + j) % k], codes, 0.0),
+                    axis=0,
+                    keepdims=True,
+                )
+                scale = jnp.exp2(code * (1.0 / STEPS)) * (1.0 / TOP)
+                levels = raw[b, pl.ds(j * TILE, TILE), :].astype(jnp.int32).astype(F32)
+                high, low = split(levels * scale)
             a = (b + j) % k
             sh[pl.ds(a * TILE, TILE), pl.ds(b * TILE, TILE)] = high
             sl[pl.ds(a * TILE, TILE), pl.ds(b * TILE, TILE)] = low
@@ -150,6 +170,7 @@
         middle_high, middle_low = split(middle)
         mt[pl.ds(0, TILE), rows] = middle_high
         mt[pl.ds(TILE, TILE), rows] = middle_low
+    codes = []
     for j in range(pairs):
         lv_copies[j].wait()
         total = jnp.zeros((wide, wide), F32)
@@ -158,19 +179,28 @@
             total = total + dot(
                 mt[:, rows], jnp.concatenate([lv[2 * j, rows, :], lv[2 * j + 1, rows, :]], axis=1)
             )
-        sigma_ref[pl.ds(wide * j, wide), :] = (total[:TILE] + total[TILE:]).T
+        block = (total[:TILE] + total[TILE:]).T
+        sigma_ref[pl.ds(wide * j, wide), :] = block
+        if first:
+            for i in range(2):
+                levels, code = code_tile(block[i * TILE : (i + 1) * TILE])
+                levels_ref[pl.ds(wide * j + i * TILE, TILE), :] = levels.astype(jnp.int16)
+                codes.append(code)
     if first:
+        row_id = lax.axis_index("row")
+        levels_ref[pl.ds(ns, SCALES), :] = (
+            jnp.concatenate(codes, axis=0).astype(jnp.int32).astype(jnp.int16)
+        )
         out_copies = []
-        row_id = lax.axis_index("row")
         for p in range(slots_ref.shape[0]):
-            picks = sent_tiles(slot_ref, p, row_id)
-            for j in range(SENT):
-                start = pl.multiple_of(picks[j] * TILE, TILE)
+            starts = [pl.multiple_of(pick * TILE, TILE) for pick in sent_tiles(slot_ref, p, row_id)]
+            moves = [(start, j * TILE, TILE) for j, start in enumerate(starts)]
+            for j, (start, place, size) in enumerate(moves + [(ns, SENT * TILE, SCALES)]):
                 out_copies.append(
                     pltpu.make_async_copy(
-                        sigma_ref.at[pl.ds(start, TILE), :],
-                        slots_ref.at[p, pl.ds(j * TILE, TILE), :],
-                        out_sem.at[p * SENT + j],
+                        levels_ref.at[pl.ds(start, size), :],
+                        slots_ref.at[p, pl.ds(place, size), :],
+                        out_sem.at[p * (SENT + 1) + j],
                     )
                 )
         for copy in out_copies:
@@ -194,7 +224,7 @@
         pltpu.VMEM((blocks, ns, width), BF),
         pltpu.VMEM((k, 2 * SENT * TILE, width), BF)
         if first
-        else pltpu.VMEM((k, SENT * TILE, width), F32),
+        else pltpu.VMEM((k, SENT * TILE + SCALES, width), jnp.int16),
         pltpu.VMEM((kb, kb), BF),
         pltpu.VMEM((kb, kb), BF),
         pltpu.VMEM((2 * TILE, ns), BF),
@@ -208,9 +238,10 @@
         operands.append(slot_tiles)
         in_specs.append(SMEM_SPEC)
         count = slot_tiles.shape[0]
-        outs.append(jax.ShapeDtypeStruct((count, SENT * TILE, width), F32))
+        outs.append(jax.ShapeDtypeStruct((count, SENT * TILE + SCALES, width), jnp.int16))
         out_specs.append(HBM_SPEC)
-        scratch.append(pltpu.SemaphoreType.DMA((count * SENT,)))
+        scratch.append(pltpu.VMEM((ns + SCALES, width), jnp.int16))
+        scratch.append(pltpu.SemaphoreType.DMA((count * (SENT + 1),)))
     else:
         operands.append(ancestor)
         in_specs.append(HBM_SPEC)
@@ -253,7 +284,6 @@
     )
     arrived = lax.all_to_all(slots, "leaf", split_axis=0, concat_axis=0, tiled=True)
     chosen = lax.dynamic_index_in_dim(arrived, source, 0, keepdims=False)
-    chosen, gathered_two = lax.optimization_barrier((chosen, gathered_two))
     ancestor = lax.all_gather(chosen, "row", axis=0)
     sigma_second, cross_second = solve(
         tiles_two, gathered_two, linv_two[0], kb, ancestor=ancestor

time: 227 us -> 195 us (0.86)
  waiting for transfers between devices: 167 us -> 106 us
  blocking collectives: 0 us -> 29.1 us
    all_gather x1 -> x0, waiting for transfers between devices: 38.4 us -> none  [body(): ancestor = lax.all_gather(chosen, 'row', axis=0)]
    all_gather x0 -> x1, blocking collectives: none -> 29.1 us  [body(): ancestor = lax.all_gather(chosen, 'row', axis=0)]
    all_to_all x1, waiting for transfers between devices: 45.2 us -> 23 us  [body(): lax.all_to_all(slots, 'leaf', split_axis=0, concat_axis=0, tiled=True)]
  transfers between devices with their start and end apart: 4 -> 3, of which waited for: 3 -> 2; matrix products, arithmetic and copies ran while one was open for 1% -> 1% of each run, Pallas kernels for 7% -> 8%
where the time goes in v2:
time: 195 us
  waiting for transfers between devices  106 us (54%)
  Pallas kernels  30.9 us (16%)
  blocking collectives  29.1 us (15%)
  between operations  16.1 us (8%)
  starting transfers between devices  6.62 us (3%)
  local copies, waits for them, and re-layouts  6.07 us (3%)
    all_gather x1, waiting for transfers between devices, body(): gathered_one = lax.all_gather(packed_one, 'row', axis=0)  83.4 us
    all_gather x1, blocking collectives, body(): ancestor = lax.all_gather(chosen, 'row', axis=0)  29.1 us
    pallas_call x2, Pallas kernels, solve(): pl.pallas_call(functools.partial(solve_kernel, first, blocks, kb), out_sh...  27.8 us
    all_to_all x1, waiting for transfers between devices, body(): lax.all_to_all(slots, 'leaf', split_axis=0, concat_axis=0, tiled=True)  23 us
    all_to_all x1, starting transfers between devices, body(): lax.all_to_all(slots, 'leaf', split_axis=0, concat_axis=0, tiled=True)  6.54 us
    unnamed x20, local copies, waits for them, and re-layouts  4.63 us
  transfers between devices with their start and end apart: 3, of which 2 were waited for; matrix products, arithmetic and copies ran while one was open for 1% of the time, Pallas kernels for 8%

profile of v2, /device:TPU:1, one launch (start us, length us, event | category | flops | bytes accessed | tf_op | source)
XLA Modules:
  0.0 195.1 jit_solution(10147704973225580081)
XLA Ops:
  7.2 0.0 all-gather.6.cloned.1.call-start
  7.2 0.8 copy.23.rest_0_.tiles_ref
  8.0 0.7 copy.20.mask_ref
  8.7 1.0 copy-done.1
  9.8 1.2 copy-done.2
  11.0 0.9 copy-done.3
  11.9 1.7 pack.2
  13.6 0.0 all-gather.6.cloned.1.call-update
  13.6 0.0 copy-done.5
  13.6 0.0 all-gather.8.cloned.1.call-start
  13.6 0.0 copy-done.7
  13.7 0.1 copy.22.mask_ref
  13.7 0.0 copy-done.4
  13.8 1.4 pack.3
  15.2 83.4 %all-gather.6.cloned.1.call-done = bf16[53248,128]{1,0:T(8,128)(2,1)} async-done(((bf16[3328,128]{1,0:T(8,128)(2,1)}), bf16[53248,128]{1,0:T(8,128)(2,1)}) %all-gather.6.cloned.1.call-update) | async-done | bytes 13631504 | tf_op jit(solution)/shard_map/all_gather | solution.py:279
  98.6 0.0 all-gather.8.cloned.1.call-update
  98.6 0.7 copy.24.rest_0_.tiles_ref
  99.3 15.0 %solve_first.1 = (f32[2048,128]{1,0:T(8,128)}, f32[512,128]{1,0:T(8,128)}, s16[16,400,128]{2,1,0:T(8,128)(2,1)}) custom-call(s32[16,4]{1,0:T(8,128)} %copy-done.5, bf16[16,3328,128]{2,1,0:T(8,128)(2,1)} %bitcast.19, bf16[2048,128]{1,0:T(8,128)(2,1)} %bitcast.15, s32[16,4]{1,0:T(8,128)} %copy.24.rest_0_.tiles_ref), custom_call_target="tpu_custom_call" | custom-call | flops 2147483648 | bytes 14680064 | tf_op jit(solution)/shard_map/solve_first/pallas_call | solution.py:248
  114.3 0.0 copy-start.8
  114.3 6.5 %all-to-all-start = ((s16[16,400,128]{2,1,0:T(8,128)(2,1)}), s16[16,400,128]{2,1,0:T(8,128)(2,1)S(1)}, u32[]{:S(2)}, u32[]{:S(2)}) async-start(s16[16,400,128]{2,1,0:T(8,128)(2,1)} %get-tuple-element.15), calls=%async_computation | async-start | bytes 3276800 | tf_op jit(solution)/shard_map/all_to_all | solution.py:285
  120.9 0.6 dynamic_slice.8
  123.4 23.0 %all-to-all-done = s16[16,400,128]{2,1,0:T(8,128)(2,1)S(1)} async-done(((s16[16,400,128]{2,1,0:T(8,128)(2,1)}), s16[16,400,128]{2,1,0:T(8,128)(2,1)S(1)}, u32[]{:S(2)}, u32[]{:S(2)}) %all-to-all-start) | async-done | bytes 1638432 | tf_op jit(solution)/shard_map/all_to_all | solution.py:285
  146.4 29.1 %all-gather.9.rest_0_ = s16[16,400,128]{2,1,0:T(8,128)(2,1)} all-gather(s16[1,400,128]{2,1,0:T(8,128)(2,1)S(1)} %constant_dynamic-slice_fusion), channel_id=1, replica_groups=mesh['leaf'=16,'row'=16] {'row'}, dimensions={0}, use_global_device_ids=true | all-gather | bytes 1740800 | tf_op jit(solution)/shard_map/all_gather | solution.py:287
  175.5 12.7 %solve_second.1 = (f32[2048,128]{1,0:T(8,128)}, f32[512,128]{1,0:T(8,128)}) custom-call(s32[16,4]{1,0:T(8,128)} %copy.24.rest_0_.tiles_ref, bf16[16,2560,128]{2,1,0:T(8,128)(2,1)} %bitcast.20, bf16[2048,128]{1,0:T(8,128)(2,1)} %bitcast.13, s16[16,400,128]{2,1,0:T(8,128)(2,1)} %all-gather.9.rest_0_), custom_call_target="tpu_custom_call" | custom-call | flops 2147483648 | bytes 14680064 | tf_op jit(solution)/shard_map/solve_second/pallas_call | solution.py:248
  (13 shorter events, 0.0 us)
Async XLA Ops:
  7.2 91.4 %all-gather.6.cloned.1.call-start = ((), (), s32[]{:S(2)}) async-start(), calls=%async_computation.1 | async-start | bytes 14483456 | tf_op jit(solution)/shard_map/all_gather | solution.py:279
  8.0 5.6 %copy-start.5 = (s32[16,4]{1,0:T(8,128)}, s32[16,4]{1,0:T(8,128)S(1)}, u32[]{:S(2)}) copy-start(s32[16,4]{1,0:T(8,128)S(1)} %copy.23.rest_0_.tiles_ref) | copy-start | bytes 772
  8.7 1.0 copy-start.1
  9.8 1.2 copy-start.2
  11.0 0.9 copy-start.3
  11.9 1.8 copy-start.7
  11.9 1.9 copy-start
  11.9 1.9 copy-start.4
  13.6 85.0 %copy-start.6 = (s32[16,4]{0,1:T(4,128)S(1)}, s32[16,4]{0,1:T(4,128)}, u32[]{:S(2)}) copy-start(s32[16,4]{0,1:T(4,128)} %param.17) | copy-start | bytes 772
  13.6 161.9 %all-gather.8.cloned.1.call-start = ((), (), s32[]{:S(2)}) async-start(), calls=%async_computation.2 | async-start | bytes 11141120 | tf_op jit(solution)/shard_map/all_gather | solution.py:281
  114.3 6.6 %copy-start.8 = (s32[16]{0:T(128)S(1)}, s32[16]{0:T(128)}, u32[]{:S(2)}) copy-start(s32[16]{0:T(128)} %param.19) | copy-start | bytes 196
  114.3 32.1 %all-to-all-start = ((s16[16,400,128]{2,1,0:T(8,128)(2,1)}), s16[16,400,128]{2,1,0:T(8,128)(2,1)S(1)}, u32[]{:S(2)}, u32[]{:S(2)}) async-start(s16[16,400,128]{2,1,0:T(8,128)(2,1)} %get-tuple-element.15), calls=%async_computation | async-start | bytes 3276800 | tf_op jit(solution)/shard_map/all_to_all | solution.py:285
Sparse Core Ops, SparseCore 0:
  13.7 84.8 all-gather.5
  100.4 70.9 all-gather.7

commit v3 on v2

v3 whole, which is shorter than its diff:
```python
import functools

import jax
import jax.numpy as jnp
from jax import lax
from jax.experimental import pallas as pl
from jax.experimental.pallas import tpu as pltpu
from jax.sharding import PartitionSpec as P

TILE = 128
BF = jnp.bfloat16
F32 = jnp.float32
I16 = jnp.int16
VMEM_SPEC = pl.BlockSpec(memory_space=pltpu.VMEM)
SMEM_SPEC = pl.BlockSpec(memory_space=pltpu.SMEM)
HBM_SPEC = pl.BlockSpec(memory_space=pltpu.HBM)
VMEM_LIMIT = 40 << 20
SOLVE_LIMIT = 60 << 20
SENT = 3
SCALES = 16
STEPS = 256.0
TOP = 32512.0


def split(x):
    high = x.astype(BF)
    return high, (x - high.astype(F32)).astype(BF)


def code_tile(x):
    peak = jnp.max(jnp.abs(x), axis=0, keepdims=True)
    code = jnp.clip(jnp.ceil(jnp.log2(peak) * STEPS), -110.0 * STEPS, 127.0 * STEPS)
    levels = jnp.round(x * (TOP / jnp.exp2(code * (1.0 / STEPS))))
    return levels.astype(jnp.int32).astype(I16), code


def dot(a, b):
    return jnp.dot(a, b, preferred_element_type=F32)


def sent_tiles(tiles_ref, block, row_id):
    count = tiles_ref.shape[1]
    place = jnp.int32(0)
    for a in range(1, count):
        place = jnp.where(tiles_ref[block, a] == row_id, jnp.int32(a), place)
    picks = []
    for j in range(SENT):
        index = place + j
        picks.append(tiles_ref[block, jnp.where(index >= count, index - count, index)])
    return picks


def code_kernel(tiles_ref, select_ref, out_ref):
    picks = sent_tiles(tiles_ref, lax.axis_index("leaf"), lax.axis_index("row"))
    shape = (SCALES, select_ref.shape[1])
    row = lax.broadcasted_iota(jnp.int32, shape, 0)
    codes = jnp.zeros(shape, F32)
    for j in range(SENT):
        start = pl.multiple_of(picks[j] * TILE, TILE)
        levels, code = code_tile(select_ref[pl.ds(start, TILE), :])
        out_ref[pl.ds(j * TILE, TILE), :] = levels
        codes = jnp.where(row == picks[j], code, codes)
    out_ref[pl.ds(SENT * TILE, SCALES), :] = codes.astype(jnp.int32).astype(I16)


def code(tiles, select):
    return pl.pallas_call(
        code_kernel,
        out_shape=jax.ShapeDtypeStruct((SENT * TILE + SCALES, select.shape[1]), I16),
        in_specs=[SMEM_SPEC, VMEM_SPEC],
        out_specs=VMEM_SPEC,
        compiler_params=pltpu.CompilerParams(vmem_limit_bytes=VMEM_LIMIT),
        cost_estimate=pl.CostEstimate(flops=1 << 20, transcendentals=0, bytes_accessed=1 << 20),
        name="code",
    )(tiles, select)


def pack_kernel(blocks, mask_ref, panel_ref, linv_ref, other_ref, out_ref):
    kb = panel_ref.shape[0]
    ns = linv_ref.shape[0]
    cut = other_ref.shape[0]
    half = blocks // 2
    row_id = lax.axis_index("row")
    for a in range(kb // TILE):
        rows = pl.ds(a * TILE, TILE)
        weight = mask_ref[a, 0].astype(F32)
        out_ref[rows, :] = (panel_ref[rows, :].astype(F32) * weight).astype(BF)

    @pl.when(row_id < half)
    def _():
        out_ref[pl.ds(kb, ns - cut), :] = linv_ref[pl.ds(cut, ns - cut), :]

    @pl.when(row_id >= half)
    def _():
        out_ref[pl.ds(kb, cut), :] = other_ref[...]
        for i in range(half - 1):

            @pl.when(i < blocks - 1 - row_id)
            def _():
                start = pl.multiple_of(lax.min(row_id + i, blocks - 1) * TILE, TILE)
                out_ref[pl.ds(kb + i * TILE, TILE), :] = linv_ref[pl.ds(start, TILE), :]

        out_ref[pl.ds(kb + cut, TILE), :] = linv_ref[pl.ds(ns - TILE, TILE), :]


def turn_kernel(linv_ref, turned_ref):
    for c in range(linv_ref.shape[0] // TILE):
        rows = pl.ds(c * TILE, TILE)
        turned_ref[:, rows] = linv_ref[rows, :].astype(F32).T.astype(BF)


def turn(linv):
    ns, width = linv.shape
    return pl.pallas_call(
        turn_kernel,
        out_shape=jax.ShapeDtypeStruct((width, ns), BF),
        in_specs=[VMEM_SPEC],
        out_specs=VMEM_SPEC,
        compiler_params=pltpu.CompilerParams(vmem_limit_bytes=VMEM_LIMIT),
        cost_estimate=pl.CostEstimate(
            flops=0, transcendentals=0, bytes_accessed=2 * 2 * ns * width
        ),
        name="turn",
    )(linv)


def pack(blocks, mask, panel, linv, other):
    kb, width = panel.shape
    ns = linv.shape[0]
    rows = kb + ns - other.shape[0]
    return pl.pallas_call(
        functools.partial(pack_kernel, blocks),
        out_shape=jax.ShapeDtypeStruct((rows, width), BF),
        in_specs=[SMEM_SPEC, VMEM_SPEC, VMEM_SPEC, VMEM_SPEC],
        out_specs=VMEM_SPEC,
        compiler_params=pltpu.CompilerParams(vmem_limit_bytes=VMEM_LIMIT),
        cost_estimate=pl.CostEstimate(
            flops=0, transcendentals=0, bytes_accessed=2 * 2 * rows * width
        ),
        name="pack",
    )(mask, panel, linv, other)


def column_parts(c, blocks, kb):
    ns = blocks * TILE
    cut = (blocks - 1) * TILE // 2
    if c < blocks // 2:
        return [
            (c, kb, ns - cut, cut),
            (blocks - 1 - c, kb + TILE * c, cut - TILE * c, TILE * c),
        ]
    parts = [(c, kb + cut, TILE, ns - TILE)]
    if c < blocks - 1:
        parts.append((c, kb, TILE * (blocks - 1 - c), TILE * c))
    return parts


def solve_kernel(first, blocks, kb, tiles_ref, gath_ref, own_ref, turned_ref, ancestor_ref, *rest):
    if first:
        slot_ref, sigma_ref, cross_ref, slots_ref = rest[:4]
        lm, lv, raw, sh, sl, mt, lm_sem, s_sem, lv_sem, levels_ref, out_sem = rest[4:]
    else:
        sigma_ref, cross_ref = rest[:2]
        lm, lv, raw, sh, sl, mt, lm_sem, s_sem, lv_sem = rest[2:]
    ns = blocks * TILE
    wide = 2 * TILE
    pairs = blocks // 2
    k = kb // TILE
    leaf_id = lax.axis_index("leaf")
    lm_copies = [
        pltpu.make_async_copy(
            gath_ref.at[c, pl.ds(0, kb), :], lm.at[:, pl.ds(c * TILE, TILE)], lm_sem.at[c]
        )
        for c in range(blocks)
    ]
    s_copies = [
        pltpu.make_async_copy(ancestor_ref.at[tiles_ref[leaf_id, b]], raw.at[b], s_sem.at[b])
        for b in range(k)
    ]
    lv_copies = []
    for c in range(blocks):
        for block, start, size, place in column_parts(c, blocks, kb):
            lv_copies.append(
                pltpu.make_async_copy(
                    gath_ref.at[block, pl.ds(start, size), :],
                    lv.at[pl.ds(place, size), pl.ds(c * TILE, TILE)],
                    lv_sem.at[len(lv_copies)],
                )
            )
    for copy in lm_copies + s_copies + lv_copies:
        copy.start()
    for j in range(pairs):
        lv[pl.ds(wide * j, TILE), pl.ds(wide * j + TILE, TILE)] = jnp.zeros((TILE, TILE), BF)

    for copy in s_copies:
        copy.wait()
    for b in range(k):
        codes = raw[b, pl.ds(SENT * TILE, SCALES), :].astype(jnp.int32).astype(F32)
        code_row = lax.broadcasted_iota(jnp.int32, codes.shape, 0)
        for j in range(SENT):
            a = (b + j) % k
            code = jnp.sum(
                jnp.where(code_row == tiles_ref[leaf_id, a], codes, 0.0), axis=0, keepdims=True
            )
            scale = jnp.exp2(code * (1.0 / STEPS)) * (1.0 / TOP)
            values = raw[b, pl.ds(j * TILE, TILE), :].astype(jnp.int32).astype(F32) * scale
            high, low = split(values)
            sh[pl.ds(a * TILE, TILE), pl.ds(b * TILE, TILE)] = high
            sl[pl.ds(a * TILE, TILE), pl.ds(b * TILE, TILE)] = low
            if j == 1:
                high, low = split(values.T)
                sh[pl.ds(b * TILE, TILE), pl.ds(a * TILE, TILE)] = high
                sl[pl.ds(b * TILE, TILE), pl.ds(a * TILE, TILE)] = low
    for copy in lm_copies:
        copy.wait()
    upper_high, upper_low = split(dot(lm[...], own_ref[...]))
    both = dot(sh[...], jnp.concatenate([upper_high, upper_low], axis=1))
    cross = -(both[:, :TILE] + both[:, TILE:] + dot(sl[...], upper_high))
    cross_ref[...] = cross
    cross_high, cross_low = split(cross.T)
    stacked = jnp.concatenate([cross_high, cross_low], axis=0)
    for j in range(pairs):
        rows = pl.ds(wide * j, wide)
        part = dot(stacked, lm[:, rows])
        middle = turned_ref[:, rows].astype(F32) - (part[:TILE] + part[TILE:])
        middle_high, middle_low = split(middle)
        mt[pl.ds(0, TILE), rows] = middle_high
        mt[pl.ds(TILE, TILE), rows] = middle_low
    for copy in lv_copies:
        copy.wait()
    codes = []
    for j in range(pairs):
        rest_rows = pl.ds(wide * j, ns - wide * j)
        total = dot(mt[:, rest_rows], lv[rest_rows, pl.ds(wide * j, wide)])
        block = (total[:TILE] + total[TILE:]).T
        sigma_ref[pl.ds(wide * j, wide), :] = block
        if first:
            for i in range(2):
                levels, code = code_tile(block[i * TILE : (i + 1) * TILE])
                levels_ref[pl.ds(wide * j + i * TILE, TILE), :] = levels
                codes.append(code)
    if first:
        row_id = lax.axis_index("row")
        levels_ref[pl.ds(ns, SCALES), :] = (
            jnp.concatenate(codes, axis=0).astype(jnp.int32).astype(I16)
        )
        out_copies = []
        for p in range(slots_ref.shape[0]):
            starts = [pl.multiple_of(pick * TILE, TILE) for pick in sent_tiles(slot_ref, p, row_id)]
            moves = [(start, j * TILE, TILE) for j, start in enumerate(starts)]
            for j, (start, place, size) in enumerate(moves + [(ns, SENT * TILE, SCALES)]):
                out_copies.append(
                    pltpu.make_async_copy(
                        levels_ref.at[pl.ds(start, size), :],
                        slots_ref.at[p, pl.ds(place, size), :],
                        out_sem.at[p * (SENT + 1) + j],
                    )
                )
        for copy in out_copies:
            copy.start()
        for copy in out_copies:
            copy.wait()


def solve(tiles, gathered, own, turned, kb, ancestor, slot_tiles=None):
    first = slot_tiles is not None
    blocks = gathered.shape[0]
    ns, width = own.shape
    k = kb // TILE
    outs = [
        jax.ShapeDtypeStruct((ns, width), F32),
        jax.ShapeDtypeStruct((kb, width), F32),
    ]
    out_specs = [VMEM_SPEC, VMEM_SPEC]
    parts = sum(len(column_parts(c, blocks, kb)) for c in range(blocks))
    scratch = [
        pltpu.VMEM((kb, ns), BF),
        pltpu.VMEM((ns, ns), BF),
        pltpu.VMEM((k,) + ancestor.shape[1:], I16),
        pltpu.VMEM((kb, kb), BF),
        pltpu.VMEM((kb, kb), BF),
        pltpu.VMEM((2 * TILE, ns), BF),
        pltpu.SemaphoreType.DMA((blocks,)),
        pltpu.SemaphoreType.DMA((k,)),
        pltpu.SemaphoreType.DMA((parts,)),
    ]
    operands = [tiles, gathered, own, turned, ancestor]
    in_specs = [SMEM_SPEC, HBM_SPEC, VMEM_SPEC, VMEM_SPEC, HBM_SPEC]
    if first:
        operands.append(slot_tiles)
        in_specs.append(SMEM_SPEC)
        count = slot_tiles.shape[0]
        outs.append(jax.ShapeDtypeStruct((count, SENT * TILE + SCALES, width), I16))
        out_specs.append(HBM_SPEC)
        scratch.append(pltpu.VMEM((ns + SCALES, width), I16))
        scratch.append(pltpu.SemaphoreType.DMA((count * (SENT + 1),)))
    return pl.pallas_call(
        functools.partial(solve_kernel, first, blocks, kb),
        out_shape=outs,
        in_specs=in_specs,
        out_specs=out_specs,
        scratch_shapes=scratch,
        compiler_params=pltpu.CompilerParams(vmem_limit_bytes=SOLVE_LIMIT),
        cost_estimate=pl.CostEstimate(
            flops=4 * ns * ns * width, transcendentals=0, bytes_accessed=14 << 20
        ),
        name="solve_first" if first else "solve_second",
    )(*operands)


def body(
    sigma_root,
    linv_one,
    panel_one,
    tiles_one,
    mask_one,
    linv_two,
    panel_two,
    tiles_two,
    mask_two,
    parent,
):
    leaf_id = lax.axis_index("leaf")
    kb = panel_one.shape[1]
    ns, width = linv_one.shape[1:]
    blocks = ns // TILE
    cut = (blocks - 1) * TILE // 2
    fold = [(i, blocks - 1 - i) for i in range(blocks // 2)]
    source = lax.dynamic_index_in_dim(parent, leaf_id, 0, keepdims=False)

    other_one = lax.ppermute(linv_one[0, :cut], "row", fold)
    coded_one = code(tiles_one, sigma_root)
    turned_one = turn(linv_one[0])
    packed_one = pack(blocks, mask_one[0], panel_one[0], linv_one[0], other_one)
    packed_one, coded_one, turned_one = lax.optimization_barrier(
        (packed_one, coded_one, turned_one)
    )
    gathered_one = lax.all_gather(packed_one, "row", axis=0)
    ancestor_one = lax.all_gather(coded_one, "row", axis=0)
    ancestor_one, later_two = lax.optimization_barrier((ancestor_one, linv_two[0]))
    other_two = lax.ppermute(later_two[:cut], "row", fold)
    turned_two = turn(later_two)
    packed_two = pack(blocks, mask_two[0], panel_two[0], later_two, other_two)
    gathered_one, packed_two = lax.optimization_barrier((gathered_one, packed_two))
    gathered_two = lax.all_gather(packed_two, "row", axis=0)
    sigma_first, cross_first, slots = solve(
        tiles_one, gathered_one, linv_one[0], turned_one, kb, ancestor_one, tiles_two
    )
    arrived = lax.all_to_all(slots, "leaf", split_axis=0, concat_axis=0, tiled=True)
    chosen = lax.dynamic_index_in_dim(arrived, source, 0, keepdims=False)
    ancestor_two = lax.all_gather(chosen, "row", axis=0)
    sigma_second, cross_second = solve(
        tiles_two, gathered_two, linv_two[0], turned_two, kb, ancestor_two
    )
    return (sigma_first[None], cross_first[None], sigma_second[None], cross_second[None])


def solution(mesh):
    return jax.shard_map(
        body,
        mesh=mesh,
        in_specs=(
            P(None, "row"),
            P("leaf", None, "row"),
            P("leaf", None, "row"),
            P(),
            P("leaf", None, "row"),
            P("leaf", None, "row"),
            P("leaf", None, "row"),
            P(),
            P("leaf", None, "row"),
            P(),
        ),
        out_specs=(
            P("leaf", None, "row"),
            P("leaf", None, "row"),
            P("leaf", None, "row"),
            P("leaf", None, "row"),
        ),
        check_vma=False,
    )
```

time: 195 us -> 177 us (0.908)
  waiting for transfers between devices: 106 us -> 57 us
  blocking collectives: 29.1 us -> 52.8 us
  starting transfers between devices: 6.62 us -> 16.7 us
  Pallas kernels: 30.9 us -> 26.3 us
    all_gather x1, waiting for transfers between devices: 83.4 us -> 13.5 us  [body(): gathered_one = lax.all_gather(packed_one, 'row', axis=0)]
    all_gather x1 -> x2, blocking collectives: 29.1 us -> 52.8 us  [the longest x1 28.7 us: body(): ancestor_one = lax.all_gather(coded_one, 'row', axis=0)]
    ppermute x0 -> x2, waiting for transfers between devices: none -> 21.6 us  [the longest x1 16.1 us: body(): other_two = lax.ppermute(later_two[:cut], 'row', fold)]
    ppermute x0 -> x2, starting transfers between devices: none -> 10.3 us  [the longest x1 8.89 us: body(): other_one = lax.ppermute(linv_one[0, :cut], 'row', fold)]
    pallas_call x2, Pallas kernels: 27.8 us -> 22.4 us  [solve(): pl.pallas_call(functools.partial(solve_kernel, first, blocks, kb), out_sh...]
    unnamed x20 -> x26, local copies, waits for them, and re-layouts: 4.63 us -> 5.34 us
  transfers between devices with their start and end apart: 3 -> 5, of which waited for: 2 -> 4; matrix products, arithmetic and copies ran while one was open for 1% -> 2% of each run, Pallas kernels for 8% -> 8%
where the time goes in v3:
time: 177 us
  waiting for transfers between devices  57 us (32%)
  blocking collectives  52.8 us (30%)
  Pallas kernels  26.3 us (15%)
  starting transfers between devices  16.7 us (9%)
  between operations  16.1 us (9%)
  local copies, waits for them, and re-layouts  7.78 us (4%)
    all_gather x1, blocking collectives, body(): ancestor_one = lax.all_gather(coded_one, 'row', axis=0)  28.7 us
    all_gather x1, blocking collectives, body(): ancestor_two = lax.all_gather(chosen, 'row', axis=0)  24.1 us
    pallas_call x2, Pallas kernels, solve(): pl.pallas_call(functools.partial(solve_kernel, first, blocks, kb), out_sh...  22.4 us
    all_to_all x1, waiting for transfers between devices, body(): lax.all_to_all(slots, 'leaf', split_axis=0, concat_axis=0, tiled=True)  21.9 us
    ppermute x1, waiting for transfers between devices, body(): other_two = lax.ppermute(later_two[:cut], 'row', fold)  16.1 us
    all_gather x1, waiting for transfers between devices, body(): gathered_one = lax.all_gather(packed_one, 'row', axis=0)  13.5 us
    ppermute x1, starting transfers between devices, body(): other_one = lax.ppermute(linv_one[0, :cut], 'row', fold)  8.89 us
    all_to_all x1, starting transfers between devices, body(): lax.all_to_all(slots, 'leaf', split_axis=0, concat_axis=0, tiled=True)  6.24 us
  transfers between devices with their start and end apart: 5, of which 4 were waited for; matrix products, arithmetic and copies ran while one was open for 2% of the time, Pallas kernels for 8%

profile of v3, /device:TPU:1, one launch (start us, length us, event | category | flops | bytes accessed | tf_op | source)
XLA Modules:
  0.0 176.7 jit_solution(5984219702368815261)
XLA Ops:
  7.2 1.0 slice_bitcast_fusion
  8.2 8.9 %collective-permute-start = (bf16[960,128]{1,0:T(8,128)(2,1)S(1)}, bf16[960,128]{1,0:T(8,128)(2,1)S(1)}, u32[]{:S(2)}, u32[]{:S(2)}) collective-permute-start(bf16[960,128]{1,0:T(8,128)(2,1)S(1)} %slice_bitcast_fusion), channel_id=1, source_target_pairs={{0,15},{1,14},{2,13},{3,12},{4,11},{5,10},{6,9},{7,8},{16,31},{17,... | collective-permute-start | bytes 737288 | tf_op jit(solution)/shard_map/ppermute | solution.py:331
  17.1 0.7 copy.20.mask_ref
  17.9 1.0 copy-done
  19.1 0.8 copy-done.3
  19.9 0.8 copy.23.tiles_ref
  20.7 1.2 copy-done.5
  21.9 0.7 code.1
  22.6 5.5 %collective-permute-done.other_ref = bf16[960,128]{1,0:T(8,128)(2,1)S(1)} collective-permute-done((bf16[960,128]{1,0:T(8,128)(2,1)S(1)}, bf16[960,128]{1,0:T(8,128)(2,1)S(1)}, u32[]{:S(2)}, u32[]{:S(2)}) %collective-permute-start) | collective-permute-done | bytes 245792 | tf_op jit(solution)/shard_map/ppermute | solution.py:331
  28.1 1.4 pack.2
  29.6 28.7 %all-gather.11 = s16[6400,128]{1,0:T(8,128)(2,1)} all-gather(s16[400,128]{1,0:T(8,128)(2,1)S(1)} %code.1), channel_id=3, replica_groups=mesh['leaf'=16,'row'=16] {'row'}, dimensions={0}, use_global_device_ids=true | all-gather | bytes 1740800 | tf_op jit(solution)/shard_map/all_gather | solution.py:339
  58.3 1.5 collective-permute-start.1
  59.9 16.1 %collective-permute-done.1.other_ref = bf16[960,128]{1,0:T(8,128)(2,1)S(1)} collective-permute-done((bf16[960,128]{1,0:T(8,128)(2,1)S(1)}, bf16[960,128]{1,0:T(8,128)(2,1)S(1)}, u32[]{:S(2)}, u32[]{:S(2)}) %collective-permute-start.1) | collective-permute-done | bytes 245792 | tf_op jit(solution)/shard_map/ppermute | solution.py:341
  76.0 1.3 pack.3
  77.4 13.5 %all-gather.8.cloned.1.call-done = bf16[25600,128]{1,0:T(8,128)(2,1)} async-done(((bf16[1600,128]{1,0:T(8,128)(2,1)}), bf16[25600,128]{1,0:T(8,128)(2,1)}) %all-gather.8.cloned.1.call-update) | async-done | bytes 6553616 | tf_op jit(solution)/shard_map/all_gather | solution.py:338
  90.8 0.7 copy.24.rest_0_.tiles_ref
  91.5 12.2 %solve_first.1 = (f32[2048,128]{1,0:T(8,128)}, f32[512,128]{1,0:T(8,128)}, s16[16,400,128]{2,1,0:T(8,128)(2,1)}) custom-call(s32[16,4]{1,0:T(8,128)} %copy-done.8, bf16[16,1600,128]{2,1,0:T(8,128)(2,1)} %bitcast.26, bf16[2048,128]{1,0:T(8,128)(2,1)} %bitcast.16, bf16[128,2048]{1,0:T(8,128)(2,1)} %copy-done.3, s16[16,400,128]{2,1,0:T(8,128)(2,1)} %bitcast.25, ...), custom_call_target="tpu_custom_call" | custom-call | flops 2147483648 | bytes 14680064 | tf_op jit(solution)/shard_map/solve_first/pallas_call | solution.py:297
  103.7 6.2 %all-to-all-start = ((s16[16,400,128]{2,1,0:T(8,128)(2,1)}), s16[16,400,128]{2,1,0:T(8,128)(2,1)S(1)}, u32[]{:S(2)}, u32[]{:S(2)}) async-start(s16[16,400,128]{2,1,0:T(8,128)(2,1)} %get-tuple-element.25), calls=%async_computation | async-start | bytes 3276800 | tf_op jit(solution)/shard_map/all_to_all | solution.py:349
  110.0 0.6 dynamic_slice.8
  112.5 0.2 turn.3.turned_ref
  112.7 0.8 copy-done.4
  113.5 21.9 %all-to-all-done = s16[16,400,128]{2,1,0:T(8,128)(2,1)S(1)} async-done(((s16[16,400,128]{2,1,0:T(8,128)(2,1)}), s16[16,400,128]{2,1,0:T(8,128)(2,1)S(1)}, u32[]{:S(2)}, u32[]{:S(2)}) %all-to-all-start) | async-done | bytes 1638432 | tf_op jit(solution)/shard_map/all_to_all | solution.py:349
  135.5 24.1 %all-gather.12.ancestor_ref = s16[16,400,128]{2,1,0:T(8,128)(2,1)} all-gather(s16[1,400,128]{2,1,0:T(8,128)(2,1)S(1)} %constant_dynamic-slice_fusion), channel_id=1, replica_groups=mesh['leaf'=16,'row'=16] {'row'}, dimensions={0}, use_global_device_ids=true | all-gather | bytes 1740800 | tf_op jit(solution)/shard_map/all_gather | solution.py:351
  159.6 10.3 %solve_second.1 = (f32[2048,128]{1,0:T(8,128)}, f32[512,128]{1,0:T(8,128)}) custom-call(s32[16,4]{1,0:T(8,128)} %copy.24.rest_0_.tiles_ref, bf16[16,1600,128]{2,1,0:T(8,128)(2,1)} %bitcast.27, bf16[2048,128]{1,0:T(8,128)(2,1)} %bitcast.19, bf16[128,2048]{1,0:T(8,128)(2,1)} %copy-done.4, s16[16,400,128]{2,1,0:T(8,128)(2,1)} %all-gather.12.ancestor_ref), custom_call_target="tpu_custom_call" | custom-call | flops 2147483648 | bytes 14680064 | tf_op jit(solution)/shard_map/solve_second/pallas_call | solution.py:297
  (29 shorter events, 0.5 us)
Async XLA Ops:
  7.2 20.9 %copy-start.6 = (bf16[1,512,128]{2,1,0:T(8,128)(2,1)S(1)}, bf16[1,512,128]{2,1,0:T(8,128)(2,1)}, u32[]{:S(2)}) copy-start(bf16[1,512,128]{2,1,0:T(8,128)(2,1)} %param.12) | copy-start | bytes 393220
  7.2 83.6 %all-gather.8.cloned.1.call-start = ((), (), s32[]{:S(2)}) async-start(), calls=%async_computation.1 | async-start | bytes 6963200 | tf_op jit(solution)/shard_map/all_gather | solution.py:338
  8.2 19.9 %collective-permute-start = (bf16[960,128]{1,0:T(8,128)(2,1)S(1)}, bf16[960,128]{1,0:T(8,128)(2,1)S(1)}, u32[]{:S(2)}, u32[]{:S(2)}) collective-permute-start(bf16[960,128]{1,0:T(8,128)(2,1)S(1)} %slice_bitcast_fusion), channel_id=1, source_target_pairs={{0,15},{1,14},{2,13},{3,12},{4,11},{5,10},{6,9},{7,8},{16,31},{17,... | collective-permute-start | bytes 737288 | tf_op jit(solution)/shard_map/ppermute | solution.py:331
  17.9 1.0 copy-start
  18.9 9.2 %copy-start.1 = (bf16[1,2048,128]{2,1,0:T(8,128)(2,1)S(1)}, bf16[1,2048,128]{2,1,0:T(8,128)(2,1)}, u32[]{:S(2)}) copy-start(bf16[1,2048,128]{2,1,0:T(8,128)(2,1)} %param.11) | copy-start | bytes 1572868
  19.1 0.8 copy-start.3
  20.7 1.2 copy-start.5
  21.9 36.4 %copy-start.8 = (s32[16,4]{1,0:T(8,128)}, s32[16,4]{1,0:T(8,128)S(1)}, u32[]{:S(2)}) copy-start(s32[16,4]{1,0:T(8,128)S(1)} %copy.23.tiles_ref) | copy-start | bytes 772
  28.1 30.2 %copy-start.2 = (bf16[1,2048,128]{2,1,0:T(8,128)(2,1)S(1)}, bf16[1,2048,128]{2,1,0:T(8,128)(2,1)}, u32[]{:S(2)}) copy-start(bf16[1,2048,128]{2,1,0:T(8,128)(2,1)} %param.15) | copy-start | bytes 1572868
  29.5 30.3 %copy-start.10 = (s32[1,4,1]{1,2,0:T(1,128)S(1)}, s32[1,4,1]{1,2,0:T(1,128)}, u32[]{:S(2)}) copy-start(s32[1,4,1]{1,2,0:T(1,128)} %param.18) | copy-start | bytes 52
  29.5 46.5 %copy-start.7 = (bf16[1,512,128]{2,1,0:T(8,128)(2,1)S(1)}, bf16[1,512,128]{2,1,0:T(8,128)(2,1)}, u32[]{:S(2)}) copy-start(bf16[1,512,128]{2,1,0:T(8,128)(2,1)} %param.16) | copy-start | bytes 393220
  29.5 61.3 %copy-start.9 = (s32[16,4]{0,1:T(4,128)S(1)}, s32[16,4]{0,1:T(4,128)}, u32[]{:S(2)}) copy-start(s32[16,4]{0,1:T(4,128)} %param.17) | copy-start | bytes 772
  29.5 130.1 %all-gather.10.cloned.1.call-start = ((), (), s32[]{:S(2)}) async-start(), calls=%async_computation.2 | async-start | bytes 6963200 | tf_op jit(solution)/shard_map/all_gather | solution.py:345
  58.3 17.7 %collective-permute-start.1 = (bf16[960,128]{1,0:T(8,128)(2,1)S(1)}, bf16[960,128]{1,0:T(8,128)(2,1)S(1)}, u32[]{:S(2)}, u32[]{:S(2)}) collective-permute-start(bf16[960,128]{1,0:T(8,128)(2,1)S(1)} %slice.7), channel_id=1, source_target_pairs={{0,15},{1,14},{2,13},{3,12},{4,11},{5,10},{6,9},{7,8},{16,31},{17,... | collective-permute-start | bytes 737288 | tf_op jit(solution)/shard_map/ppermute | solution.py:341
  103.7 6.3 %copy-start.11 = (s32[16]{0:T(128)S(1)}, s32[16]{0:T(128)}, u32[]{:S(2)}) copy-start(s32[16]{0:T(128)} %param.19) | copy-start | bytes 196
  103.7 31.8 %all-to-all-start = ((s16[16,400,128]{2,1,0:T(8,128)(2,1)}), s16[16,400,128]{2,1,0:T(8,128)(2,1)S(1)}, u32[]{:S(2)}, u32[]{:S(2)}) async-start(s16[16,400,128]{2,1,0:T(8,128)(2,1)} %get-tuple-element.25), calls=%async_computation | async-start | bytes 3276800 | tf_op jit(solution)/shard_map/all_to_all | solution.py:349
  112.7 0.8 copy-start.4
Sparse Core Ops, SparseCore 0:
  29.6 61.1 all-gather.7
  92.6 46.8 all-gather.9

commit v4 on v3

--- a/solution.py
+++ b/solution.py
@@ -158,24 +158,28 @@
 def solve_kernel(first, blocks, kb, tiles_ref, gath_ref, own_ref, turned_ref, ancestor_ref, *rest):
     if first:
         slot_ref, sigma_ref, cross_ref, slots_ref = rest[:4]
-        lm, lv, raw, sh, sl, mt, lm_sem, s_sem, lv_sem, levels_ref, out_sem = rest[4:]
+        rest = rest[4:]
+        levels_ref, picks_ref, out_sem = rest[-3:]
     else:
         sigma_ref, cross_ref = rest[:2]
-        lm, lv, raw, sh, sl, mt, lm_sem, s_sem, lv_sem = rest[2:]
+        rest = rest[2:]
+    lm, lv, own, turned, raw, sh, sl, mt, sg, cr, lm_sem, s_sem, lv_sem, own_sem, res_sem = rest[:15]
     ns = blocks * TILE
     wide = 2 * TILE
     pairs = blocks // 2
     k = kb // TILE
     leaf_id = lax.axis_index("leaf")
+    s_copies = [
+        pltpu.make_async_copy(ancestor_ref.at[tiles_ref[leaf_id, b]], raw.at[b], s_sem.at[b])
+        for b in range(k)
+    ]
+    own_copy = pltpu.make_async_copy(own_ref, own, own_sem.at[0])
+    turned_copy = pltpu.make_async_copy(turned_ref, turned, own_sem.at[1])
     lm_copies = [
         pltpu.make_async_copy(
             gath_ref.at[c, pl.ds(0, kb), :], lm.at[:, pl.ds(c * TILE, TILE)], lm_sem.at[c]
         )
         for c in range(blocks)
-    ]
-    s_copies = [
-        pltpu.make_async_copy(ancestor_ref.at[tiles_ref[leaf_id, b]], raw.at[b], s_sem.at[b])
-        for b in range(k)
     ]
     lv_copies = []
     for c in range(blocks):
@@ -187,10 +191,15 @@
                     lv_sem.at[len(lv_copies)],
                 )
             )
-    for copy in lm_copies + s_copies + lv_copies:
+    for copy in s_copies + [own_copy] + lm_copies + [turned_copy] + lv_copies:
         copy.start()
     for j in range(pairs):
         lv[pl.ds(wide * j, TILE), pl.ds(wide * j + TILE, TILE)] = jnp.zeros((TILE, TILE), BF)
+    if first:
+        row_id = lax.axis_index("row")
+        for p in range(slots_ref.shape[0]):
+            for j, pick in enumerate(sent_tiles(slot_ref, p, row_id)):
+                picks_ref[p * SENT + j] = pick
 
     for copy in s_copies:
         copy.wait()
@@ -211,55 +220,75 @@
                 high, low = split(values.T)
                 sh[pl.ds(b * TILE, TILE), pl.ds(a * TILE, TILE)] = high
                 sl[pl.ds(b * TILE, TILE), pl.ds(a * TILE, TILE)] = low
+    own_copy.wait()
     for copy in lm_copies:
         copy.wait()
-    upper_high, upper_low = split(dot(lm[...], own_ref[...]))
-    both = dot(sh[...], jnp.concatenate([upper_high, upper_low], axis=1))
-    cross = -(both[:, :TILE] + both[:, TILE:] + dot(sl[...], upper_high))
-    cross_ref[...] = cross
+    upper = jnp.concatenate(
+        [dot(lm[pl.ds(i * (kb // 2), kb // 2), :], own[...]) for i in range(2)], axis=0
+    )
+    upper_high, upper_low = split(upper)
+    upper_both = jnp.concatenate([upper_high, upper_low], axis=1)
+    crosses = []
+    for i in range(2):
+        rows = pl.ds(i * (kb // 2), kb // 2)
+        both = dot(sh[rows, :], upper_both)
+        crosses.append(-(both[:, :TILE] + both[:, TILE:] + dot(sl[rows, :], upper_high)))
+    cross = jnp.concatenate(crosses, axis=0)
+    cr[...] = cross
+    cross_copy = pltpu.make_async_copy(cr, cross_ref, own_sem.at[0])
+    cross_copy.start()
     cross_high, cross_low = split(cross.T)
     stacked = jnp.concatenate([cross_high, cross_low], axis=0)
+    turned_copy.wait()
+    for copy in lv_copies:
+        copy.wait()
     for j in range(pairs):
         rows = pl.ds(wide * j, wide)
         part = dot(stacked, lm[:, rows])
-        middle = turned_ref[:, rows].astype(F32) - (part[:TILE] + part[TILE:])
+        middle = turned[:, rows].astype(F32) - (part[:TILE] + part[TILE:])
         middle_high, middle_low = split(middle)
         mt[pl.ds(0, TILE), rows] = middle_high
         mt[pl.ds(TILE, TILE), rows] = middle_low
-    for copy in lv_copies:
-        copy.wait()
     codes = []
+    out_copies = []
     for j in range(pairs):
+        rows = pl.ds(wide * j, wide)
         rest_rows = pl.ds(wide * j, ns - wide * j)
-        total = dot(mt[:, rest_rows], lv[rest_rows, pl.ds(wide * j, wide)])
+        total = dot(mt[:, rest_rows], lv[rest_rows, rows])
         block = (total[:TILE] + total[TILE:]).T
-        sigma_ref[pl.ds(wide * j, wide), :] = block
+        sg[rows, :] = block
         if first:
             for i in range(2):
                 levels, code = code_tile(block[i * TILE : (i + 1) * TILE])
                 levels_ref[pl.ds(wide * j + i * TILE, TILE), :] = levels
                 codes.append(code)
+        else:
+            copy = pltpu.make_async_copy(sg.at[rows], sigma_ref.at[rows], res_sem.at[j])
+            copy.start()
+            out_copies.append(copy)
     if first:
-        row_id = lax.axis_index("row")
         levels_ref[pl.ds(ns, SCALES), :] = (
             jnp.concatenate(codes, axis=0).astype(jnp.int32).astype(I16)
         )
-        out_copies = []
         for p in range(slots_ref.shape[0]):
-            starts = [pl.multiple_of(pick * TILE, TILE) for pick in sent_tiles(slot_ref, p, row_id)]
+            starts = [
+                pl.multiple_of(picks_ref[p * SENT + j] * TILE, TILE) for j in range(SENT)
+            ]
             moves = [(start, j * TILE, TILE) for j, start in enumerate(starts)]
             for j, (start, place, size) in enumerate(moves + [(ns, SENT * TILE, SCALES)]):
-                out_copies.append(
-                    pltpu.make_async_copy(
-                        levels_ref.at[pl.ds(start, size), :],
-                        slots_ref.at[p, pl.ds(place, size), :],
-                        out_sem.at[p * (SENT + 1) + j],
-                    )
+                copy = pltpu.make_async_copy(
+                    levels_ref.at[pl.ds(start, size), :],
+                    slots_ref.at[p, pl.ds(place, size), :],
+                    out_sem.at[p * (SENT + 1) + j],
                 )
-        for copy in out_copies:
-            copy.start()
-        for copy in out_copies:
-            copy.wait()
+                copy.start()
+                out_copies.append(copy)
+        copy = pltpu.make_async_copy(sg, sigma_ref, res_sem.at[0])
+        copy.start()
+        out_copies.append(copy)
+    cross_copy.wait()
+    for copy in out_copies:
+        copy.wait()
 
 
 def solve(tiles, gathered, own, turned, kb, ancestor, slot_tiles=None):
@@ -271,34 +300,39 @@
         jax.ShapeDtypeStruct((ns, width), F32),
         jax.ShapeDtypeStruct((kb, width), F32),
     ]
-    out_specs = [VMEM_SPEC, VMEM_SPEC]
     parts = sum(len(column_parts(c, blocks, kb)) for c in range(blocks))
     scratch = [
         pltpu.VMEM((kb, ns), BF),
         pltpu.VMEM((ns, ns), BF),
+        pltpu.VMEM((ns, width), BF),
+        pltpu.VMEM((width, ns), BF),
         pltpu.VMEM((k,) + ancestor.shape[1:], I16),
         pltpu.VMEM((kb, kb), BF),
         pltpu.VMEM((kb, kb), BF),
         pltpu.VMEM((2 * TILE, ns), BF),
+        pltpu.VMEM((ns, width), F32),
+        pltpu.VMEM((kb, width), F32),
         pltpu.SemaphoreType.DMA((blocks,)),
         pltpu.SemaphoreType.DMA((k,)),
         pltpu.SemaphoreType.DMA((parts,)),
+        pltpu.SemaphoreType.DMA((2,)),
+        pltpu.SemaphoreType.DMA((blocks // 2,)),
     ]
     operands = [tiles, gathered, own, turned, ancestor]
-    in_specs = [SMEM_SPEC, HBM_SPEC, VMEM_SPEC, VMEM_SPEC, HBM_SPEC]
+    in_specs = [SMEM_SPEC, HBM_SPEC, HBM_SPEC, HBM_SPEC, HBM_SPEC]
     if first:
         operands.append(slot_tiles)
         in_specs.append(SMEM_SPEC)
         count = slot_tiles.shape[0]
         outs.append(jax.ShapeDtypeStruct((count, SENT * TILE + SCALES, width), I16))
-        out_specs.append(HBM_SPEC)
         scratch.append(pltpu.VMEM((ns + SCALES, width), I16))
+        scratch.append(pltpu.SMEM((count * SENT,), jnp.int32))
         scratch.append(pltpu.SemaphoreType.DMA((count * (SENT + 1),)))
     return pl.pallas_call(
         functools.partial(solve_kernel, first, blocks, kb),
         out_shape=outs,
         in_specs=in_specs,
-        out_specs=out_specs,
+        out_specs=[HBM_SPEC] * len(outs),
         scratch_shapes=scratch,
         compiler_params=pltpu.CompilerParams(vmem_limit_bytes=SOLVE_LIMIT),
         cost_estimate=pl.CostEstimate(
@@ -331,14 +365,15 @@
     other_one = lax.ppermute(linv_one[0, :cut], "row", fold)
     coded_one = code(tiles_one, sigma_root)
     turned_one = turn(linv_one[0])
+    other_one, later_two = lax.optimization_barrier((other_one, linv_two[0]))
     packed_one = pack(blocks, mask_one[0], panel_one[0], linv_one[0], other_one)
     packed_one, coded_one, turned_one = lax.optimization_barrier(
         (packed_one, coded_one, turned_one)
     )
     gathered_one = lax.all_gather(packed_one, "row", axis=0)
+    other_two = lax.ppermute(later_two[:cut], "row", fold)
     ancestor_one = lax.all_gather(coded_one, "row", axis=0)
-    ancestor_one, later_two = lax.optimization_barrier((ancestor_one, linv_two[0]))
-    other_two = lax.ppermute(later_two[:cut], "row", fold)
+    ancestor_one, other_two = lax.optimization_barrier((ancestor_one, other_two))
     turned_two = turn(later_two)
     packed_two = pack(blocks, mask_two[0], panel_two[0], later_two, other_two)
     gathered_one, packed_two = lax.optimization_barrier((gathered_one, packed_two))

time: 177 us -> 168 us (0.949)
  waiting for transfers between devices: 57 us -> 35.3 us
  blocking collectives: 52.8 us -> 64.1 us
  starting transfers between devices: 16.7 us -> 21.1 us
  Pallas kernels: 26.3 us -> 23.2 us
    ppermute x1, waiting for transfers between devices: 16.1 us -> 0.01 us  [body(): other_two = lax.ppermute(later_two[:cut], 'row', fold)]
    all_gather x1, blocking collectives: 28.7 us -> 41.6 us  [body(): ancestor_one = lax.all_gather(coded_one, 'row', axis=0)]
    all_gather x1, waiting for transfers between devices: 13.5 us -> 7.98 us  [body(): gathered_one = lax.all_gather(packed_one, 'row', axis=0)]
    ppermute x1, starting transfers between devices: 1.45 us -> 5.65 us  [body(): other_two = lax.ppermute(later_two[:cut], 'row', fold)]
    pallas_call x2, Pallas kernels: 22.4 us -> 19.4 us  [solve(): pl.pallas_call(functools.partial(solve_kernel, first, blocks, kb), out_sh...]
  transfers between devices with their start and end apart: 5 -> 5, of which waited for: 4 -> 3; matrix products, arithmetic and copies ran while one was open for 2% -> 2% of each run, Pallas kernels for 8% -> 8%
where the time goes in v4:
time: 168 us
  blocking collectives  64.1 us (38%)
  waiting for transfers between devices  35.3 us (21%)
  Pallas kernels  23.2 us (14%)
  starting transfers between devices  21.1 us (13%)
  between operations  16.1 us (10%)
  local copies, waits for them, and re-layouts  7.84 us (5%)
    all_gather x1, blocking collectives, body(): ancestor_one = lax.all_gather(coded_one, 'row', axis=0)  41.6 us
    all_gather x1, blocking collectives, body(): ancestor_two = lax.all_gather(chosen, 'row', axis=0)  22.5 us
    all_to_all x1, waiting for transfers between devices, body(): lax.all_to_all(slots, 'leaf', split_axis=0, concat_axis=0, tiled=True)  21.9 us
    pallas_call x2, Pallas kernels, solve(): pl.pallas_call(functools.partial(solve_kernel, first, blocks, kb), out_sh...  19.4 us
    ppermute x1, starting transfers between devices, body(): other_one = lax.ppermute(linv_one[0, :cut], 'row', fold)  8.89 us
    all_gather x1, waiting for transfers between devices, body(): gathered_one = lax.all_gather(packed_one, 'row', axis=0)  7.98 us
    all_to_all x1, starting transfers between devices, body(): lax.all_to_all(slots, 'leaf', split_axis=0, concat_axis=0, tiled=True)  6.54 us
    ppermute x1, starting transfers between devices, body(): other_two = lax.ppermute(later_two[:cut], 'row', fold)  5.65 us
  transfers between devices with their start and end apart: 5, of which 3 were waited for; matrix products, arithmetic and copies ran while one was open for 2% of the time, Pallas kernels for 8%

profile of v4, /device:TPU:1, one launch (start us, length us, event | category | flops | bytes accessed | tf_op | source)
XLA Modules:
  0.0 167.8 jit_solution(14349588111143539076)
XLA Ops:
  7.2 1.0 slice_bitcast_fusion
  8.2 8.9 %collective-permute-start = (bf16[960,128]{1,0:T(8,128)(2,1)S(1)}, bf16[960,128]{1,0:T(8,128)(2,1)S(1)}, u32[]{:S(2)}, u32[]{:S(2)}) collective-permute-start(bf16[960,128]{1,0:T(8,128)(2,1)S(1)} %slice_bitcast_fusion), channel_id=1, source_target_pairs={{0,15},{1,14},{2,13},{3,12},{4,11},{5,10},{6,9},{7,8},{16,31},{17,... | collective-permute-start | bytes 737288 | tf_op jit(solution)/shard_map/ppermute | solution.py:365
  17.1 0.7 copy.20.mask_ref
  17.9 1.0 copy-done
  18.9 0.2 turn.2.turned_ref
  19.1 0.8 copy-done.3
  19.9 0.8 copy.23.tiles_ref
  20.7 1.2 copy-done.5
  22.0 0.7 code.1
  22.7 5.4 %collective-permute-done.other_ref = bf16[960,128]{1,0:T(8,128)(2,1)S(1)} collective-permute-done((bf16[960,128]{1,0:T(8,128)(2,1)S(1)}, bf16[960,128]{1,0:T(8,128)(2,1)S(1)}, u32[]{:S(2)}, u32[]{:S(2)}) %collective-permute-start) | collective-permute-done | bytes 245792 | tf_op jit(solution)/shard_map/ppermute | solution.py:365
  28.1 1.4 pack.2
  29.7 5.6 %collective-permute-start.1 = (bf16[960,128]{1,0:T(8,128)(2,1)S(1)}, bf16[960,128]{1,0:T(8,128)(2,1)S(1)}, u32[]{:S(2)}, u32[]{:S(2)}) collective-permute-start(bf16[960,128]{1,0:T(8,128)(2,1)S(1)} %slice.7), channel_id=1, source_target_pairs={{0,15},{1,14},{2,13},{3,12},{4,11},{5,10},{6,9},{7,8},{16,31},{17,... | collective-permute-start | bytes 737288 | tf_op jit(solution)/shard_map/ppermute | solution.py:374
  35.3 41.6 %all-gather.11 = s16[6400,128]{1,0:T(8,128)(2,1)} all-gather(s16[400,128]{1,0:T(8,128)(2,1)S(1)} %code.1), channel_id=3, replica_groups=mesh['leaf'=16,'row'=16] {'row'}, dimensions={0}, use_global_device_ids=true | all-gather | bytes 1740800 | tf_op jit(solution)/shard_map/all_gather | solution.py:375
  77.0 1.4 pack.3
  78.3 8.0 %all-gather.8.cloned.1.call-done = bf16[25600,128]{1,0:T(8,128)(2,1)} async-done(((bf16[1600,128]{1,0:T(8,128)(2,1)}), bf16[25600,128]{1,0:T(8,128)(2,1)}) %all-gather.8.cloned.1.call-update) | async-done | bytes 6553616 | tf_op jit(solution)/shard_map/all_gather | solution.py:373
  86.4 0.7 copy.24.rest_0_.tiles_ref
  87.0 10.5 %solve_first.1 = (f32[2048,128]{1,0:T(8,128)}, f32[512,128]{1,0:T(8,128)}, s16[16,400,128]{2,1,0:T(8,128)(2,1)}) custom-call(s32[16,4]{1,0:T(8,128)} %copy-done.8, bf16[16,1600,128]{2,1,0:T(8,128)(2,1)} %bitcast.26, bf16[2048,128]{1,0:T(8,128)(2,1)} %bitcast.16, bf16[128,2048]{1,0:T(8,128)(2,1)} %copy-done.3, s16[16,400,128]{2,1,0:T(8,128)(2,1)} %bitcast.25, ...), custom_call_target="tpu_custom_call" | custom-call | flops 2147483648 | bytes 14680064 | tf_op jit(solution)/shard_map/solve_first/pallas_call | solution.py:331
  97.6 6.5 %all-to-all-start = ((s16[16,400,128]{2,1,0:T(8,128)(2,1)}), s16[16,400,128]{2,1,0:T(8,128)(2,1)S(1)}, u32[]{:S(2)}, u32[]{:S(2)}) async-start(s16[16,400,128]{2,1,0:T(8,128)(2,1)} %get-tuple-element.29), calls=%async_computation | async-start | bytes 3276800 | tf_op jit(solution)/shard_map/all_to_all | solution.py:384
  104.1 0.6 dynamic_slice.8
  106.7 0.2 turn.3.turned_ref
  106.9 0.8 copy-done.4
  107.7 21.9 %all-to-all-done = s16[16,400,128]{2,1,0:T(8,128)(2,1)S(1)} async-done(((s16[16,400,128]{2,1,0:T(8,128)(2,1)}), s16[16,400,128]{2,1,0:T(8,128)(2,1)S(1)}, u32[]{:S(2)}, u32[]{:S(2)}) %all-to-all-start) | async-done | bytes 1638432 | tf_op jit(solution)/shard_map/all_to_all | solution.py:384
  129.6 22.5 %all-gather.12.ancestor_ref = s16[16,400,128]{2,1,0:T(8,128)(2,1)} all-gather(s16[1,400,128]{2,1,0:T(8,128)(2,1)S(1)} %constant_dynamic-slice_fusion), channel_id=1, replica_groups=mesh['leaf'=16,'row'=16] {'row'}, dimensions={0}, use_global_device_ids=true | all-gather | bytes 1740800 | tf_op jit(solution)/shard_map/all_gather | solution.py:386
  152.1 8.8 %solve_second.1 = (f32[2048,128]{1,0:T(8,128)}, f32[512,128]{1,0:T(8,128)}) custom-call(s32[16,4]{1,0:T(8,128)} %copy.24.rest_0_.tiles_ref, bf16[16,1600,128]{2,1,0:T(8,128)(2,1)} %bitcast.27, bf16[2048,128]{1,0:T(8,128)(2,1)} %bitcast.19, bf16[128,2048]{1,0:T(8,128)(2,1)} %copy-done.4, s16[16,400,128]{2,1,0:T(8,128)(2,1)} %all-gather.12.ancestor_ref), custom_call_target="tpu_custom_call" | custom-call | flops 2147483648 | bytes 14680064 | tf_op jit(solution)/shard_map/solve_second/pallas_call | solution.py:331
  (29 shorter events, 0.3 us)
Async XLA Ops:
  7.2 20.9 %copy-start.6 = (bf16[1,512,128]{2,1,0:T(8,128)(2,1)S(1)}, bf16[1,512,128]{2,1,0:T(8,128)(2,1)}, u32[]{:S(2)}) copy-start(bf16[1,512,128]{2,1,0:T(8,128)(2,1)} %param.12) | copy-start | bytes 393220
  7.2 79.2 %all-gather.8.cloned.1.call-start = ((), (), s32[]{:S(2)}) async-start(), calls=%async_computation.1 | async-start | bytes 6963200 | tf_op jit(solution)/shard_map/all_gather | solution.py:373
  8.2 19.9 %collective-permute-start = (bf16[960,128]{1,0:T(8,128)(2,1)S(1)}, bf16[960,128]{1,0:T(8,128)(2,1)S(1)}, u32[]{:S(2)}, u32[]{:S(2)}) collective-permute-start(bf16[960,128]{1,0:T(8,128)(2,1)S(1)} %slice_bitcast_fusion), channel_id=1, source_target_pairs={{0,15},{1,14},{2,13},{3,12},{4,11},{5,10},{6,9},{7,8},{16,31},{17,... | collective-permute-start | bytes 737288 | tf_op jit(solution)/shard_map/ppermute | solution.py:365
  17.9 1.0 copy-start
  18.9 9.2 %copy-start.1 = (bf16[1,2048,128]{2,1,0:T(8,128)(2,1)S(1)}, bf16[1,2048,128]{2,1,0:T(8,128)(2,1)}, u32[]{:S(2)}) copy-start(bf16[1,2048,128]{2,1,0:T(8,128)(2,1)} %param.11) | copy-start | bytes 1572868
  19.1 0.8 copy-start.3
  19.9 9.7 %copy-start.2 = (bf16[1,2048,128]{2,1,0:T(8,128)(2,1)S(1)}, bf16[1,2048,128]{2,1,0:T(8,128)(2,1)}, u32[]{:S(2)}) copy-start(bf16[1,2048,128]{2,1,0:T(8,128)(2,1)} %param.15) | copy-start | bytes 1572868
  20.7 1.2 copy-start.5
  21.9 7.7 %copy-start.8 = (s32[16,4]{1,0:T(8,128)}, s32[16,4]{1,0:T(8,128)S(1)}, u32[]{:S(2)}) copy-start(s32[16,4]{1,0:T(8,128)S(1)} %copy.23.tiles_ref) | copy-start | bytes 772
  21.9 7.6 %copy-start.10 = (s32[1,4,1]{1,2,0:T(1,128)S(1)}, s32[1,4,1]{1,2,0:T(1,128)}, u32[]{:S(2)}) copy-start(s32[1,4,1]{1,2,0:T(1,128)} %param.18) | copy-start | bytes 52
  29.5 47.5 %copy-start.7 = (bf16[1,512,128]{2,1,0:T(8,128)(2,1)S(1)}, bf16[1,512,128]{2,1,0:T(8,128)(2,1)}, u32[]{:S(2)}) copy-start(bf16[1,512,128]{2,1,0:T(8,128)(2,1)} %param.16) | copy-start | bytes 393220
  29.5 122.6 %all-gather.10.cloned.1.call-start = ((), (), s32[]{:S(2)}) async-start(), calls=%async_computation.2 | async-start | bytes 6963200 | tf_op jit(solution)/shard_map/all_gather | solution.py:380
  29.7 56.7 %copy-start.9 = (s32[16,4]{0,1:T(4,128)S(1)}, s32[16,4]{0,1:T(4,128)}, u32[]{:S(2)}) copy-start(s32[16,4]{0,1:T(4,128)} %param.17) | copy-start | bytes 772
  29.7 47.3 %collective-permute-start.1 = (bf16[960,128]{1,0:T(8,128)(2,1)S(1)}, bf16[960,128]{1,0:T(8,128)(2,1)S(1)}, u32[]{:S(2)}, u32[]{:S(2)}) collective-permute-start(bf16[960,128]{1,0:T(8,128)(2,1)S(1)} %slice.7), channel_id=1, source_target_pairs={{0,15},{1,14},{2,13},{3,12},{4,11},{5,10},{6,9},{7,8},{16,31},{17,... | collective-permute-start | bytes 737288 | tf_op jit(solution)/shard_map/ppermute | solution.py:374
  97.6 6.6 %copy-start.11 = (s32[16]{0:T(128)S(1)}, s32[16]{0:T(128)}, u32[]{:S(2)}) copy-start(s32[16]{0:T(128)} %param.19) | copy-start | bytes 196
  97.6 32.1 %all-to-all-start = ((s16[16,400,128]{2,1,0:T(8,128)(2,1)}), s16[16,400,128]{2,1,0:T(8,128)(2,1)S(1)}, u32[]{:S(2)}, u32[]{:S(2)}) async-start(s16[16,400,128]{2,1,0:T(8,128)(2,1)} %get-tuple-element.29), calls=%async_computation | async-start | bytes 3276800 | tf_op jit(solution)/shard_map/all_to_all | solution.py:384
  106.9 0.8 copy-start.4
Sparse Core Ops, SparseCore 0:
  29.6 56.6 all-gather.7
  88.2 47.4 all-gather.9

commit v5 on v4

--- a/solution.py
+++ b/solution.py
@@ -17,6 +17,9 @@
 VMEM_LIMIT = 40 << 20
 SOLVE_LIMIT = 60 << 20
 SENT = 3
+HALF = TILE // 2
+PIECES = (TILE, TILE, HALF)
+DATA = sum(PIECES)
 SCALES = 16
 STEPS = 256.0
 TOP = 32512.0
@@ -31,7 +34,12 @@
     peak = jnp.max(jnp.abs(x), axis=0, keepdims=True)
     code = jnp.clip(jnp.ceil(jnp.log2(peak) * STEPS), -110.0 * STEPS, 127.0 * STEPS)
     levels = jnp.round(x * (TOP / jnp.exp2(code * (1.0 / STEPS))))
-    return levels.astype(jnp.int32).astype(I16), code
+    return levels.astype(jnp.int32), code
+
+
+def right_half(x):
+    lane = lax.broadcasted_iota(jnp.int32, (HALF, TILE), 1)
+    return jnp.where(lane < HALF, pltpu.roll(x[:HALF], HALF, 1), x[HALF:])
 
 
 def dot(a, b):
@@ -39,34 +47,36 @@
 
 
 def sent_tiles(tiles_ref, block, row_id):
-    count = tiles_ref.shape[1]
+    count = tiles_ref.shape[0]
     place = jnp.int32(0)
     for a in range(1, count):
-        place = jnp.where(tiles_ref[block, a] == row_id, jnp.int32(a), place)
+        place = jnp.where(tiles_ref[a, block] == row_id, jnp.int32(a), place)
     picks = []
     for j in range(SENT):
         index = place + j
-        picks.append(tiles_ref[block, jnp.where(index >= count, index - count, index)])
-    return picks
+        picks.append(tiles_ref[jnp.where(index >= count, index - count, index), block])
+    return picks, place < count // 2
 
 
 def code_kernel(tiles_ref, select_ref, out_ref):
-    picks = sent_tiles(tiles_ref, lax.axis_index("leaf"), lax.axis_index("row"))
+    picks, early = sent_tiles(tiles_ref, lax.axis_index("leaf"), lax.axis_index("row"))
     shape = (SCALES, select_ref.shape[1])
     row = lax.broadcasted_iota(jnp.int32, shape, 0)
     codes = jnp.zeros(shape, F32)
     for j in range(SENT):
         start = pl.multiple_of(picks[j] * TILE, TILE)
         levels, code = code_tile(select_ref[pl.ds(start, TILE), :])
-        out_ref[pl.ds(j * TILE, TILE), :] = levels
+        if PIECES[j] == HALF:
+            levels = jnp.where(early, right_half(levels), levels[:HALF])
+        out_ref[pl.ds(j * TILE, PIECES[j]), :] = levels.astype(I16)
         codes = jnp.where(row == picks[j], code, codes)
-    out_ref[pl.ds(SENT * TILE, SCALES), :] = codes.astype(jnp.int32).astype(I16)
+    out_ref[pl.ds(DATA, SCALES), :] = codes.astype(jnp.int32).astype(I16)
 
 
 def code(tiles, select):
     return pl.pallas_call(
         code_kernel,
-        out_shape=jax.ShapeDtypeStruct((SENT * TILE + SCALES, select.shape[1]), I16),
+        out_shape=jax.ShapeDtypeStruct((DATA + SCALES, select.shape[1]), I16),
         in_specs=[SMEM_SPEC, VMEM_SPEC],
         out_specs=VMEM_SPEC,
         compiler_params=pltpu.CompilerParams(vmem_limit_bytes=VMEM_LIMIT),
@@ -83,7 +93,7 @@
     row_id = lax.axis_index("row")
     for a in range(kb // TILE):
         rows = pl.ds(a * TILE, TILE)
-        weight = mask_ref[a, 0].astype(F32)
+        weight = mask_ref[a].astype(F32)
         out_ref[rows, :] = (panel_ref[rows, :].astype(F32) * weight).astype(BF)
 
     @pl.when(row_id < half)
@@ -170,7 +180,7 @@
     k = kb // TILE
     leaf_id = lax.axis_index("leaf")
     s_copies = [
-        pltpu.make_async_copy(ancestor_ref.at[tiles_ref[leaf_id, b]], raw.at[b], s_sem.at[b])
+        pltpu.make_async_copy(ancestor_ref.at[tiles_ref[b, leaf_id]], raw.at[b], s_sem.at[b])
         for b in range(k)
     ]
     own_copy = pltpu.make_async_copy(own_ref, own, own_sem.at[0])
@@ -198,28 +208,45 @@
     if first:
         row_id = lax.axis_index("row")
         for p in range(slots_ref.shape[0]):
-            for j, pick in enumerate(sent_tiles(slot_ref, p, row_id)):
-                picks_ref[p * SENT + j] = pick
+            picks, early = sent_tiles(slot_ref, p, row_id)
+            for j, pick in enumerate(picks):
+                start = pick * TILE
+                if PIECES[j] == HALF:
+                    start = jnp.where(early, ns + SCALES + pick * HALF, start)
+                picks_ref[p * SENT + j] = start
+
+    def store(a, b, values):
+        high, low = split(values)
+        sh[pl.ds(a * TILE, TILE), pl.ds(b * TILE, TILE)] = high
+        sl[pl.ds(a * TILE, TILE), pl.ds(b * TILE, TILE)] = low
 
     for copy in s_copies:
         copy.wait()
+    halves = []
     for b in range(k):
-        codes = raw[b, pl.ds(SENT * TILE, SCALES), :].astype(jnp.int32).astype(F32)
+        codes = raw[b, pl.ds(DATA, SCALES), :].astype(jnp.int32).astype(F32)
         code_row = lax.broadcasted_iota(jnp.int32, codes.shape, 0)
         for j in range(SENT):
             a = (b + j) % k
             code = jnp.sum(
-                jnp.where(code_row == tiles_ref[leaf_id, a], codes, 0.0), axis=0, keepdims=True
+                jnp.where(code_row == tiles_ref[a, leaf_id], codes, 0.0), axis=0, keepdims=True
             )
             scale = jnp.exp2(code * (1.0 / STEPS)) * (1.0 / TOP)
-            values = raw[b, pl.ds(j * TILE, TILE), :].astype(jnp.int32).astype(F32) * scale
-            high, low = split(values)
-            sh[pl.ds(a * TILE, TILE), pl.ds(b * TILE, TILE)] = high
-            sl[pl.ds(a * TILE, TILE), pl.ds(b * TILE, TILE)] = low
+            values = raw[b, pl.ds(j * TILE, PIECES[j]), :].astype(jnp.int32).astype(F32)
+            if j == 2:
+                if b < k // 2:
+                    values = jnp.concatenate([pltpu.roll(values, HALF, 1), values], axis=0)
+                halves.append(values * scale)
+                continue
+            values = values * scale
+            store(a, b, values)
             if j == 1:
-                high, low = split(values.T)
-                sh[pl.ds(b * TILE, TILE), pl.ds(a * TILE, TILE)] = high
-                sl[pl.ds(b * TILE, TILE), pl.ds(a * TILE, TILE)] = low
+                store(b, a, values.T)
+    for b in range(k // 2):
+        a = b + k // 2
+        values = jnp.concatenate([halves[a], halves[b].T[HALF:]], axis=0)
+        store(b, a, values)
+        store(a, b, values.T)
     own_copy.wait()
     for copy in lm_copies:
         copy.wait()
@@ -260,7 +287,10 @@
         if first:
             for i in range(2):
                 levels, code = code_tile(block[i * TILE : (i + 1) * TILE])
-                levels_ref[pl.ds(wide * j + i * TILE, TILE), :] = levels
+                levels_ref[pl.ds(wide * j + i * TILE, TILE), :] = levels.astype(I16)
+                levels_ref[pl.ds(ns + SCALES + (2 * j + i) * HALF, HALF), :] = right_half(
+                    levels
+                ).astype(I16)
                 codes.append(code)
         else:
             copy = pltpu.make_async_copy(sg.at[rows], sigma_ref.at[rows], res_sem.at[j])
@@ -271,11 +301,11 @@
             jnp.concatenate(codes, axis=0).astype(jnp.int32).astype(I16)
         )
         for p in range(slots_ref.shape[0]):
-            starts = [
-                pl.multiple_of(picks_ref[p * SENT + j] * TILE, TILE) for j in range(SENT)
+            moves = [
+                (pl.multiple_of(picks_ref[p * SENT + j], SCALES), j * TILE, PIECES[j])
+                for j in range(SENT)
             ]
-            moves = [(start, j * TILE, TILE) for j, start in enumerate(starts)]
-            for j, (start, place, size) in enumerate(moves + [(ns, SENT * TILE, SCALES)]):
+            for j, (start, place, size) in enumerate(moves + [(ns, DATA, SCALES)]):
                 copy = pltpu.make_async_copy(
                     levels_ref.at[pl.ds(start, size), :],
                     slots_ref.at[p, pl.ds(place, size), :],
@@ -323,9 +353,9 @@
     if first:
         operands.append(slot_tiles)
         in_specs.append(SMEM_SPEC)
-        count = slot_tiles.shape[0]
-        outs.append(jax.ShapeDtypeStruct((count, SENT * TILE + SCALES, width), I16))
-        scratch.append(pltpu.VMEM((ns + SCALES, width), I16))
+        count = slot_tiles.shape[1]
+        outs.append(jax.ShapeDtypeStruct((count, DATA + SCALES, width), I16))
+        scratch.append(pltpu.VMEM((ns + SCALES + ns // 2, width), I16))
         scratch.append(pltpu.SMEM((count * SENT,), jnp.int32))
         scratch.append(pltpu.SemaphoreType.DMA((count * (SENT + 1),)))
     return pl.pallas_call(
@@ -359,14 +389,16 @@
     ns, width = linv_one.shape[1:]
     blocks = ns // TILE
     cut = (blocks - 1) * TILE // 2
-    fold = [(i, blocks - 1 - i) for i in range(blocks // 2)]
+    fold = [(i, blocks - 1 - i) for i in range(blocks)]
+    tiles_one, tiles_two = tiles_one.T, tiles_two.T
+    mask_one, mask_two = mask_one[0, :, 0], mask_two[0, :, 0]
     source = lax.dynamic_index_in_dim(parent, leaf_id, 0, keepdims=False)
 
     other_one = lax.ppermute(linv_one[0, :cut], "row", fold)
     coded_one = code(tiles_one, sigma_root)
     turned_one = turn(linv_one[0])
     other_one, later_two = lax.optimization_barrier((other_one, linv_two[0]))
-    packed_one = pack(blocks, mask_one[0], panel_one[0], linv_one[0], other_one)
+    packed_one = pack(blocks, mask_one, panel_one[0], linv_one[0], other_one)
     packed_one, coded_one, turned_one = lax.optimization_barrier(
         (packed_one, coded_one, turned_one)
     )
@@ -375,7 +407,7 @@
     ancestor_one = lax.all_gather(coded_one, "row", axis=0)
     ancestor_one, other_two = lax.optimization_barrier((ancestor_one, other_two))
     turned_two = turn(later_two)
-    packed_two = pack(blocks, mask_two[0], panel_two[0], later_two, other_two)
+    packed_two = pack(blocks, mask_two, panel_two[0], later_two, other_two)
     gathered_one, packed_two = lax.optimization_barrier((gathered_one, packed_two))
     gathered_two = lax.all_gather(packed_two, "row", axis=0)
     sigma_first, cross_first, slots = solve(

time: 168 us -> 161 us (0.958)
  starting transfers between devices: 21.1 us -> 17.7 us
  blocking collectives: 64.1 us -> 61.4 us
  local copies, waits for them, and re-layouts: 7.84 us -> 5.54 us
    all_gather x1, blocking collectives: 41.6 us -> 37.1 us  [body(): ancestor_one = lax.all_gather(coded_one, 'row', axis=0)]
    all_to_all x1, waiting for transfers between devices: 21.9 us -> 17.9 us  [body(): lax.all_to_all(slots, 'leaf', split_axis=0, concat_axis=0, tiled=True)]
    all_gather x1, waiting for transfers between devices: 7.98 us -> 11.6 us  [body(): gathered_one = lax.all_gather(packed_one, 'row', axis=0)]
    ppermute x1, starting transfers between devices: 8.89 us -> 7.05 us  [body(): other_one = lax.ppermute(linv_one[0, :cut], 'row', fold)]
    ppermute x1, starting transfers between devices: 5.65 us -> 3.82 us  [body(): other_two = lax.ppermute(later_two[:cut], 'row', fold)]
    all_gather x1, blocking collectives: 22.5 us -> 24.3 us  [body(): ancestor_two = lax.all_gather(chosen, 'row', axis=0)]
    unnamed x26 -> x24, local copies, waits for them, and re-layouts: 5.4 us -> 3.93 us
  transfers between devices with their start and end apart: 5 -> 5, of which waited for: 3 -> 3; matrix products, arithmetic and copies ran while one was open for 2% -> 0% of each run, Pallas kernels for 8% -> 8%
where the time goes in v5:
time: 161 us; the launch traced here: 160 us
  blocking collectives  61.4 us (38%)
  waiting for transfers between devices  36.5 us (23%)
  Pallas kernels  22.9 us (14%)
  starting transfers between devices  17.7 us (11%)
  between operations  16.1 us (10%)
  local copies, waits for them, and re-layouts  5.54 us (3%)
    all_gather x1, blocking collectives, body(): ancestor_one = lax.all_gather(coded_one, 'row', axis=0)  37.1 us
    all_gather x1, blocking collectives, body(): ancestor_two = lax.all_gather(chosen, 'row', axis=0)  24.3 us
    pallas_call x2, Pallas kernels, solve(): pl.pallas_call(functools.partial(solve_kernel, first, blocks, kb), out_sh...  19.2 us
    all_to_all x1, waiting for transfers between devices, body(): lax.all_to_all(slots, 'leaf', split_axis=0, concat_axis=0, tiled=True)  17.9 us
    all_gather x1, waiting for transfers between devices, body(): gathered_one = lax.all_gather(packed_one, 'row', axis=0)  11.6 us
    ppermute x1, starting transfers between devices, body(): other_one = lax.ppermute(linv_one[0, :cut], 'row', fold)  7.05 us
    ppermute x1, waiting for transfers between devices, body(): other_one = lax.ppermute(linv_one[0, :cut], 'row', fold)  7.04 us
    all_to_all x1, starting transfers between devices, body(): lax.all_to_all(slots, 'leaf', split_axis=0, concat_axis=0, tiled=True)  6.73 us
  transfers between devices with their start and end apart: 5, of which 3 were waited for; matrix products, arithmetic and copies ran while one was open for 0% of the time, Pallas kernels for 8%

profile of v5, /device:TPU:1, one launch (start us, length us, event | category | flops | bytes accessed | tf_op | source)
XLA Modules:
  0.0 160.2 jit_solution(15327620532348320078)
XLA Ops:
  7.2 0.0 all-gather.8.cloned.1.call-start
  7.2 1.0 slice_bitcast_fusion
  8.2 7.1 %collective-permute-start = (bf16[960,128]{1,0:T(8,128)(2,1)S(1)}, bf16[960,128]{1,0:T(8,128)(2,1)S(1)}, u32[]{:S(2)}, u32[]{:S(2)}) collective-permute-start(bf16[960,128]{1,0:T(8,128)(2,1)S(1)} %slice_bitcast_fusion), channel_id=1, source_target_pairs={{0,15},{1,14},{2,13},{3,12},{4,11},{5,10},{6,9},{7,8},{8,7},{9,6},... | collective-permute-start | bytes 737288 | tf_op jit(solution)/shard_map/ppermute | solution.py:397
  15.3 1.0 copy-done
  16.3 0.2 turn.2.turned_ref
  16.6 0.8 copy-done.3
  17.3 1.2 copy-done.5
  18.6 0.7 code.1
  19.3 7.0 %collective-permute-done.other_ref = bf16[960,128]{1,0:T(8,128)(2,1)S(1)} collective-permute-done((bf16[960,128]{1,0:T(8,128)(2,1)S(1)}, bf16[960,128]{1,0:T(8,128)(2,1)S(1)}, u32[]{:S(2)}, u32[]{:S(2)}) %collective-permute-start) | collective-permute-done | bytes 245792 | tf_op jit(solution)/shard_map/ppermute | solution.py:397
  26.3 1.3 pack.2
  27.7 0.0 all-gather.8.cloned.1.call-update
  27.7 0.0 all-gather.10.cloned.1.call-start
  27.8 3.8 %collective-permute-start.1 = (bf16[960,128]{1,0:T(8,128)(2,1)S(1)}, bf16[960,128]{1,0:T(8,128)(2,1)S(1)}, u32[]{:S(2)}, u32[]{:S(2)}) collective-permute-start(bf16[960,128]{1,0:T(8,128)(2,1)S(1)} %slice.7), channel_id=1, source_target_pairs={{0,15},{1,14},{2,13},{3,12},{4,11},{5,10},{6,9},{7,8},{8,7},{9,6},... | collective-permute-start | bytes 737288 | tf_op jit(solution)/shard_map/ppermute | solution.py:406
  31.6 37.1 %all-gather.11 = s16[5376,128]{1,0:T(8,128)(2,1)} all-gather(s16[336,128]{1,0:T(8,128)(2,1)S(1)} %code.1), channel_id=3, replica_groups=mesh['leaf'=16,'row'=16] {'row'}, dimensions={0}, use_global_device_ids=true | all-gather | bytes 1462272 | tf_op jit(solution)/shard_map/all_gather | solution.py:407
  68.7 1.3 pack.3
  70.1 11.6 %all-gather.8.cloned.1.call-done = bf16[25600,128]{1,0:T(8,128)(2,1)} async-done(((bf16[1600,128]{1,0:T(8,128)(2,1)}), bf16[25600,128]{1,0:T(8,128)(2,1)}) %all-gather.8.cloned.1.call-update) | async-done | bytes 6553616 | tf_op jit(solution)/shard_map/all_gather | solution.py:405
  81.7 10.4 %solve_first.1 = (f32[2048,128]{1,0:T(8,128)}, f32[512,128]{1,0:T(8,128)}, s16[16,336,128]{2,1,0:T(8,128)(2,1)}) custom-call(s32[4,16]{1,0:T(4,128)} %bitcast.27, bf16[16,1600,128]{2,1,0:T(8,128)(2,1)} %bitcast.32, bf16[2048,128]{1,0:T(8,128)(2,1)} %bitcast.18, bf16[128,2048]{1,0:T(8,128)(2,1)} %copy-done.3, s16[16,336,128]{2,1,0:T(8,128)(2,1)} %bitcast.33, ...), custom_call_target="tpu_custom_call" | custom-call | flops 2147483648 | bytes 14680064 | tf_op jit(solution)/shard_map/solve_first/pallas_call | solution.py:361
  92.1 6.7 %all-to-all-start = ((s16[16,336,128]{2,1,0:T(8,128)(2,1)}), s16[16,336,128]{2,1,0:T(8,128)(2,1)S(1)}, u32[]{:S(2)}, u32[]{:S(2)}) async-start(s16[16,336,128]{2,1,0:T(8,128)(2,1)} %get-tuple-element.29), calls=%async_computation | async-start | bytes 2752512 | tf_op jit(solution)/shard_map/all_to_all | solution.py:416
  98.8 0.6 dynamic_slice.8
  101.4 0.2 turn.3.turned_ref
  101.6 0.8 copy-done.4
  102.4 17.9 %all-to-all-done = s16[16,336,128]{2,1,0:T(8,128)(2,1)S(1)} async-done(((s16[16,336,128]{2,1,0:T(8,128)(2,1)}), s16[16,336,128]{2,1,0:T(8,128)(2,1)S(1)}, u32[]{:S(2)}, u32[]{:S(2)}) %all-to-all-start) | async-done | bytes 1376288 | tf_op jit(solution)/shard_map/all_to_all | solution.py:416
  120.3 24.3 %all-gather.12.ancestor_ref = s16[16,336,128]{2,1,0:T(8,128)(2,1)} all-gather(s16[1,336,128]{2,1,0:T(8,128)(2,1)S(1)} %constant_dynamic-slice_fusion), channel_id=1, replica_groups=mesh['leaf'=16,'row'=16] {'row'}, dimensions={0}, use_global_device_ids=true | all-gather | bytes 1462272 | tf_op jit(solution)/shard_map/all_gather | solution.py:418
  144.6 8.8 %solve_second.1 = (f32[2048,128]{1,0:T(8,128)}, f32[512,128]{1,0:T(8,128)}) custom-call(s32[4,16]{1,0:T(4,128)} %bitcast.35, bf16[16,1600,128]{2,1,0:T(8,128)(2,1)} %bitcast.31, bf16[2048,128]{1,0:T(8,128)(2,1)} %bitcast.21, bf16[128,2048]{1,0:T(8,128)(2,1)} %copy-done.4, s16[16,336,128]{2,1,0:T(8,128)(2,1)} %all-gather.12.ancestor_ref), custom_call_target="tpu_custom_call" | custom-call | flops 2147483648 | bytes 14680064 | tf_op jit(solution)/shard_map/solve_second/pallas_call | solution.py:361
  (25 shorter events, 0.1 us)
Async XLA Ops:
  7.2 10.2 %copy-start.8 = (s32[16,4]{0,1:T(4,128)S(1)}, s32[16,4]{0,1:T(4,128)}, u32[]{:S(2)}) copy-start(s32[16,4]{0,1:T(4,128)} %param.13) | copy-start | bytes 772
  7.2 19.1 %copy-start.9 = (s32[1,4,1]{1,2,0:T(1,128)S(1)}, s32[1,4,1]{1,2,0:T(1,128)}, u32[]{:S(2)}) copy-start(s32[1,4,1]{1,2,0:T(1,128)} %param.14) | copy-start | bytes 52
  7.2 19.1 %copy-start.6 = (bf16[1,512,128]{2,1,0:T(8,128)(2,1)S(1)}, bf16[1,512,128]{2,1,0:T(8,128)(2,1)}, u32[]{:S(2)}) copy-start(bf16[1,512,128]{2,1,0:T(8,128)(2,1)} %param.12) | copy-start | bytes 393220
  7.2 74.5 %all-gather.8.cloned.1.call-start = ((), (), s32[]{:S(2)}) async-start(), calls=%async_computation.1 | async-start | bytes 6963200 | tf_op jit(solution)/shard_map/all_gather | solution.py:405
  8.2 18.1 %collective-permute-start = (bf16[960,128]{1,0:T(8,128)(2,1)S(1)}, bf16[960,128]{1,0:T(8,128)(2,1)S(1)}, u32[]{:S(2)}, u32[]{:S(2)}) collective-permute-start(bf16[960,128]{1,0:T(8,128)(2,1)S(1)} %slice_bitcast_fusion), channel_id=1, source_target_pairs={{0,15},{1,14},{2,13},{3,12},{4,11},{5,10},{6,9},{7,8},{8,7},{9,6},... | collective-permute-start | bytes 737288 | tf_op jit(solution)/shard_map/ppermute | solution.py:397
  15.3 1.0 copy-start
  16.3 10.0 %copy-start.1 = (bf16[1,2048,128]{2,1,0:T(8,128)(2,1)S(1)}, bf16[1,2048,128]{2,1,0:T(8,128)(2,1)}, u32[]{:S(2)}) copy-start(bf16[1,2048,128]{2,1,0:T(8,128)(2,1)} %param.11) | copy-start | bytes 1572868
  16.5 0.8 copy-start.3
  17.3 1.2 copy-start.5
  18.6 9.2 %copy-start.2 = (bf16[1,2048,128]{2,1,0:T(8,128)(2,1)S(1)}, bf16[1,2048,128]{2,1,0:T(8,128)(2,1)}, u32[]{:S(2)}) copy-start(bf16[1,2048,128]{2,1,0:T(8,128)(2,1)} %param.15) | copy-start | bytes 1572868
  27.7 41.1 %copy-start.7 = (bf16[1,512,128]{2,1,0:T(8,128)(2,1)S(1)}, bf16[1,512,128]{2,1,0:T(8,128)(2,1)}, u32[]{:S(2)}) copy-start(bf16[1,512,128]{2,1,0:T(8,128)(2,1)} %param.16) | copy-start | bytes 393220
  27.7 41.1 %copy-start.10 = (s32[1,4,1]{1,2,0:T(1,128)S(1)}, s32[1,4,1]{1,2,0:T(1,128)}, u32[]{:S(2)}) copy-start(s32[1,4,1]{1,2,0:T(1,128)} %param.18) | copy-start | bytes 52
  27.7 116.9 %all-gather.10.cloned.1.call-start = ((), (), s32[]{:S(2)}) async-start(), calls=%async_computation.2 | async-start | bytes 6963200 | tf_op jit(solution)/shard_map/all_gather | solution.py:412
  27.8 41.0 %collective-permute-start.1 = (bf16[960,128]{1,0:T(8,128)(2,1)S(1)}, bf16[960,128]{1,0:T(8,128)(2,1)S(1)}, u32[]{:S(2)}, u32[]{:S(2)}) collective-permute-start(bf16[960,128]{1,0:T(8,128)(2,1)S(1)} %slice.7), channel_id=1, source_target_pairs={{0,15},{1,14},{2,13},{3,12},{4,11},{5,10},{6,9},{7,8},{8,7},{9,6},... | collective-permute-start | bytes 737288 | tf_op jit(solution)/shard_map/ppermute | solution.py:406
  92.1 6.8 %copy-start.11 = (s32[16]{0:T(128)S(1)}, s32[16]{0:T(128)}, u32[]{:S(2)}) copy-start(s32[16]{0:T(128)} %param.19) | copy-start | bytes 196
  92.1 28.2 %all-to-all-start = ((s16[16,336,128]{2,1,0:T(8,128)(2,1)}), s16[16,336,128]{2,1,0:T(8,128)(2,1)S(1)}, u32[]{:S(2)}, u32[]{:S(2)}) async-start(s16[16,336,128]{2,1,0:T(8,128)(2,1)} %get-tuple-element.29), calls=%async_computation | async-start | bytes 2752512 | tf_op jit(solution)/shard_map/all_to_all | solution.py:416
  101.6 0.9 copy-start.4
Sparse Core Ops, SparseCore 0:
  27.8 53.8 all-gather.7
  83.5 48.7 all-gather.9

commit v6 on v5

--- a/solution.py
+++ b/solution.py
@@ -18,7 +18,8 @@
 SOLVE_LIMIT = 60 << 20
 SENT = 3
 HALF = TILE // 2
-PIECES = (TILE, TILE, HALF)
+PIECES = (HALF + HALF // 2, TILE, HALF)
+PLACES = (0, PIECES[0], PIECES[0] + PIECES[1])
 DATA = sum(PIECES)
 SCALES = 16
 STEPS = 256.0
@@ -38,8 +39,13 @@
 
 
 def right_half(x):
-    lane = lax.broadcasted_iota(jnp.int32, (HALF, TILE), 1)
-    return jnp.where(lane < HALF, pltpu.roll(x[:HALF], HALF, 1), x[HALF:])
+    rows = x.shape[0] // 2
+    lane = lax.broadcasted_iota(jnp.int32, (rows, TILE), 1)
+    return jnp.where(lane < HALF, pltpu.roll(x[:rows], HALF, 1), x[rows:])
+
+
+def own_tile(x):
+    return jnp.concatenate([x[:HALF], right_half(x[HALF:])], axis=0)
 
 
 def dot(a, b):
@@ -66,9 +72,11 @@
     for j in range(SENT):
         start = pl.multiple_of(picks[j] * TILE, TILE)
         levels, code = code_tile(select_ref[pl.ds(start, TILE), :])
-        if PIECES[j] == HALF:
+        if j == 0:
+            levels = own_tile(levels)
+        elif j == 2:
             levels = jnp.where(early, right_half(levels), levels[:HALF])
-        out_ref[pl.ds(j * TILE, PIECES[j]), :] = levels.astype(I16)
+        out_ref[pl.ds(PLACES[j], PIECES[j]), :] = levels.astype(I16)
         codes = jnp.where(row == picks[j], code, codes)
     out_ref[pl.ds(DATA, SCALES), :] = codes.astype(jnp.int32).astype(I16)
 
@@ -165,24 +173,27 @@
     return parts
 
 
-def solve_kernel(first, blocks, kb, tiles_ref, gath_ref, own_ref, turned_ref, ancestor_ref, *rest):
+def solve_kernel(first, blocks, kb, tiles_hbm, gath_ref, own_ref, turned_ref, ancestor_ref, *rest):
     if first:
-        slot_ref, sigma_ref, cross_ref, slots_ref = rest[:4]
+        slot_hbm, sigma_ref, cross_ref, slots_ref = rest[:4]
         rest = rest[4:]
-        levels_ref, picks_ref, out_sem = rest[-3:]
+        levels_ref, picks_ref, slot_ref, out_sem = rest[-4:]
     else:
         sigma_ref, cross_ref = rest[:2]
         rest = rest[2:]
-    lm, lv, own, turned, raw, sh, sl, mt, sg, cr, lm_sem, s_sem, lv_sem, own_sem, res_sem = rest[:15]
+    lm, lv, own, turned, raw, sh, sl, mt, sg, cr, lm_sem, s_sem, lv_sem, own_sem, res_sem, tiles_ref = (
+        rest[:16]
+    )
     ns = blocks * TILE
     wide = 2 * TILE
     pairs = blocks // 2
     k = kb // TILE
     leaf_id = lax.axis_index("leaf")
-    s_copies = [
-        pltpu.make_async_copy(ancestor_ref.at[tiles_ref[b, leaf_id]], raw.at[b], s_sem.at[b])
-        for b in range(k)
-    ]
+    tiles_copy = pltpu.make_async_copy(tiles_hbm, tiles_ref, own_sem.at[2])
+    tiles_copy.start()
+    if first:
+        slot_copy = pltpu.make_async_copy(slot_hbm, slot_ref, own_sem.at[3])
+        slot_copy.start()
     own_copy = pltpu.make_async_copy(own_ref, own, own_sem.at[0])
     turned_copy = pltpu.make_async_copy(turned_ref, turned, own_sem.at[1])
     lm_copies = [
@@ -201,18 +212,26 @@
                     lv_sem.at[len(lv_copies)],
                 )
             )
-    for copy in s_copies + [own_copy] + lm_copies + [turned_copy] + lv_copies:
+    for copy in [own_copy] + lm_copies:
+        copy.start()
+    tiles_copy.wait()
+    s_copies = [
+        pltpu.make_async_copy(ancestor_ref.at[tiles_ref[b, leaf_id]], raw.at[b], s_sem.at[b])
+        for b in range(k)
+    ]
+    for copy in s_copies + [turned_copy] + lv_copies:
         copy.start()
     for j in range(pairs):
         lv[pl.ds(wide * j, TILE), pl.ds(wide * j + TILE, TILE)] = jnp.zeros((TILE, TILE), BF)
     if first:
+        slot_copy.wait()
         row_id = lax.axis_index("row")
         for p in range(slots_ref.shape[0]):
             picks, early = sent_tiles(slot_ref, p, row_id)
             for j, pick in enumerate(picks):
                 start = pick * TILE
-                if PIECES[j] == HALF:
-                    start = jnp.where(early, ns + SCALES + pick * HALF, start)
+                if j == 2:
+                    start = jnp.where(early, ns + SCALES + PIECES[0] + pick * HALF, start)
                 picks_ref[p * SENT + j] = start
 
     def store(a, b, values):
@@ -223,6 +242,9 @@
     for copy in s_copies:
         copy.wait()
     halves = []
+    corner = (lax.broadcasted_iota(jnp.int32, (TILE, TILE), 0) >= HALF) & (
+        lax.broadcasted_iota(jnp.int32, (TILE, TILE), 1) < HALF
+    )
     for b in range(k):
         codes = raw[b, pl.ds(DATA, SCALES), :].astype(jnp.int32).astype(F32)
         code_row = lax.broadcasted_iota(jnp.int32, codes.shape, 0)
@@ -232,16 +254,20 @@
                 jnp.where(code_row == tiles_ref[a, leaf_id], codes, 0.0), axis=0, keepdims=True
             )
             scale = jnp.exp2(code * (1.0 / STEPS)) * (1.0 / TOP)
-            values = raw[b, pl.ds(j * TILE, PIECES[j]), :].astype(jnp.int32).astype(F32)
-            if j == 2:
+            values = raw[b, pl.ds(PLACES[j], PIECES[j]), :].astype(jnp.int32).astype(F32)
+            if j == 0:
+                low = values[HALF:]
+                values = jnp.concatenate([values[:HALF], pltpu.roll(low, HALF, 1), low], axis=0)
+                values = values * scale
+                store(a, b, jnp.where(corner, values.T, values))
+            elif j == 1:
+                values = values * scale
+                store(a, b, values)
+                store(b, a, values.T)
+            else:
                 if b < k // 2:
                     values = jnp.concatenate([pltpu.roll(values, HALF, 1), values], axis=0)
                 halves.append(values * scale)
-                continue
-            values = values * scale
-            store(a, b, values)
-            if j == 1:
-                store(b, a, values.T)
     for b in range(k // 2):
         a = b + k // 2
         values = jnp.concatenate([halves[a], halves[b].T[HALF:]], axis=0)
@@ -288,24 +314,28 @@
             for i in range(2):
                 levels, code = code_tile(block[i * TILE : (i + 1) * TILE])
                 levels_ref[pl.ds(wide * j + i * TILE, TILE), :] = levels.astype(I16)
-                levels_ref[pl.ds(ns + SCALES + (2 * j + i) * HALF, HALF), :] = right_half(
+                levels_ref[
+                    pl.ds(ns + SCALES + PIECES[0] + (2 * j + i) * HALF, HALF), :
+                ] = right_half(
                     levels
                 ).astype(I16)
                 codes.append(code)
-        else:
-            copy = pltpu.make_async_copy(sg.at[rows], sigma_ref.at[rows], res_sem.at[j])
-            copy.start()
-            out_copies.append(copy)
+        copy = pltpu.make_async_copy(sg.at[rows], sigma_ref.at[rows], res_sem.at[j])
+        copy.start()
+        out_copies.append(copy)
     if first:
+        own_start = pl.multiple_of(row_id * TILE, TILE)
+        levels = levels_ref[pl.ds(own_start, TILE), :].astype(jnp.int32)
+        levels_ref[pl.ds(ns + SCALES, PIECES[0]), :] = own_tile(levels).astype(I16)
         levels_ref[pl.ds(ns, SCALES), :] = (
             jnp.concatenate(codes, axis=0).astype(jnp.int32).astype(I16)
         )
         for p in range(slots_ref.shape[0]):
-            moves = [
-                (pl.multiple_of(picks_ref[p * SENT + j], SCALES), j * TILE, PIECES[j])
-                for j in range(SENT)
-            ]
-            for j, (start, place, size) in enumerate(moves + [(ns, DATA, SCALES)]):
+            moves = [(ns + SCALES, PLACES[0], PIECES[0]), (ns, DATA, SCALES)]
+            for j in range(1, SENT):
+                start = pl.multiple_of(picks_ref[p * SENT + j], SCALES)
+                moves.append((start, PLACES[j], PIECES[j]))
+            for j, (start, place, size) in enumerate(moves):
                 copy = pltpu.make_async_copy(
                     levels_ref.at[pl.ds(start, size), :],
                     slots_ref.at[p, pl.ds(place, size), :],
@@ -313,9 +343,6 @@
                 )
                 copy.start()
                 out_copies.append(copy)
-        copy = pltpu.make_async_copy(sg, sigma_ref, res_sem.at[0])
-        copy.start()
-        out_copies.append(copy)
     cross_copy.wait()
     for copy in out_copies:
         copy.wait()
@@ -345,18 +372,20 @@
         pltpu.SemaphoreType.DMA((blocks,)),
         pltpu.SemaphoreType.DMA((k,)),
         pltpu.SemaphoreType.DMA((parts,)),
-        pltpu.SemaphoreType.DMA((2,)),
+        pltpu.SemaphoreType.DMA((4,)),
         pltpu.SemaphoreType.DMA((blocks // 2,)),
+        pltpu.SMEM(tiles.shape, jnp.int32),
     ]
     operands = [tiles, gathered, own, turned, ancestor]
-    in_specs = [SMEM_SPEC, HBM_SPEC, HBM_SPEC, HBM_SPEC, HBM_SPEC]
+    in_specs = [HBM_SPEC] * 5
     if first:
         operands.append(slot_tiles)
-        in_specs.append(SMEM_SPEC)
+        in_specs.append(HBM_SPEC)
         count = slot_tiles.shape[1]
         outs.append(jax.ShapeDtypeStruct((count, DATA + SCALES, width), I16))
-        scratch.append(pltpu.VMEM((ns + SCALES + ns // 2, width), I16))
+        scratch.append(pltpu.VMEM((ns + SCALES + PIECES[0] + ns // 2, width), I16))
         scratch.append(pltpu.SMEM((count * SENT,), jnp.int32))
+        scratch.append(pltpu.SMEM(slot_tiles.shape, jnp.int32))
         scratch.append(pltpu.SemaphoreType.DMA((count * (SENT + 1),)))
     return pl.pallas_call(
         functools.partial(solve_kernel, first, blocks, kb),

time: 161 us -> 157 us (0.975)
    all_to_all x1, waiting for transfers between devices: 17.9 us -> 15.9 us  [body(): lax.all_to_all(slots, 'leaf', split_axis=0, concat_axis=0, tiled=True)]
where the time goes in v6:
time: 157 us
  blocking collectives  60.7 us (39%)
  waiting for transfers between devices  35.2 us (22%)
  Pallas kernels  21.7 us (14%)
  starting transfers between devices  17.5 us (11%)
  between operations  16.1 us (10%)
  local copies, waits for them, and re-layouts  5.52 us (4%)
    all_gather x1, blocking collectives, body(): ancestor_one = lax.all_gather(coded_one, 'row', axis=0)  36 us
    all_gather x1, blocking collectives, body(): ancestor_two = lax.all_gather(chosen, 'row', axis=0)  24.7 us
    pallas_call x2, Pallas kernels, solve(): pl.pallas_call(functools.partial(solve_kernel, first, blocks, kb), out_sh...  17.9 us
    all_to_all x1, waiting for transfers between devices, body(): lax.all_to_all(slots, 'leaf', split_axis=0, concat_axis=0, tiled=True)  15.9 us
    all_gather x1, waiting for transfers between devices, body(): gathered_one = lax.all_gather(packed_one, 'row', axis=0)  12.2 us
    ppermute x1, starting transfers between devices, body(): other_one = lax.ppermute(linv_one[0, :cut], 'row', fold)  7.05 us
    ppermute x1, waiting for transfers between devices, body(): other_one = lax.ppermute(linv_one[0, :cut], 'row', fold)  7.03 us
    all_to_all x1, starting transfers between devices, body(): lax.all_to_all(slots, 'leaf', split_axis=0, concat_axis=0, tiled=True)  6.54 us
  transfers between devices with their start and end apart: 5, of which 3 were waited for; matrix products, arithmetic and copies ran while one was open for 0% of the time, Pallas kernels for 8%

profile of v6, /device:TPU:1, one launch (start us, length us, event | category | flops | bytes accessed | tf_op | source)
XLA Modules:
  0.0 156.7 jit_solution(10974574535919955355)
XLA Ops:
  7.2 0.0 all-gather.8.cloned.1.call-start
  7.2 1.0 slice_bitcast_fusion
  8.2 7.1 %collective-permute-start = (bf16[960,128]{1,0:T(8,128)(2,1)S(1)}, bf16[960,128]{1,0:T(8,128)(2,1)S(1)}, u32[]{:S(2)}, u32[]{:S(2)}) collective-permute-start(bf16[960,128]{1,0:T(8,128)(2,1)S(1)} %slice_bitcast_fusion), channel_id=1, source_target_pairs={{0,15},{1,14},{2,13},{3,12},{4,11},{5,10},{6,9},{7,8},{8,7},{9,6},... | collective-permute-start | bytes 737288 | tf_op jit(solution)/shard_map/ppermute | solution.py:426
  15.3 1.0 copy-done
  16.3 0.2 turn.2.turned_ref
  16.6 0.8 copy-done.3
  17.3 1.2 copy-done.5
  18.6 0.7 code.1
  19.3 7.0 %collective-permute-done.other_ref = bf16[960,128]{1,0:T(8,128)(2,1)S(1)} collective-permute-done((bf16[960,128]{1,0:T(8,128)(2,1)S(1)}, bf16[960,128]{1,0:T(8,128)(2,1)S(1)}, u32[]{:S(2)}, u32[]{:S(2)}) %collective-permute-start) | collective-permute-done | bytes 245792 | tf_op jit(solution)/shard_map/ppermute | solution.py:426
  26.3 1.3 pack.2
  27.7 0.0 all-gather.8.cloned.1.call-update
  27.7 0.0 all-gather.10.cloned.1.call-start
  27.8 3.8 %collective-permute-start.1 = (bf16[960,128]{1,0:T(8,128)(2,1)S(1)}, bf16[960,128]{1,0:T(8,128)(2,1)S(1)}, u32[]{:S(2)}, u32[]{:S(2)}) collective-permute-start(bf16[960,128]{1,0:T(8,128)(2,1)S(1)} %slice.7), channel_id=1, source_target_pairs={{0,15},{1,14},{2,13},{3,12},{4,11},{5,10},{6,9},{7,8},{8,7},{9,6},... | collective-permute-start | bytes 737288 | tf_op jit(solution)/shard_map/ppermute | solution.py:435
  31.6 36.0 %all-gather.11 = s16[4864,128]{1,0:T(8,128)(2,1)} all-gather(s16[304,128]{1,0:T(8,128)(2,1)S(1)} %code.1), channel_id=3, replica_groups=mesh['leaf'=16,'row'=16] {'row'}, dimensions={0}, use_global_device_ids=true | all-gather | bytes 1323008 | tf_op jit(solution)/shard_map/all_gather | solution.py:436
  67.6 1.3 pack.3
  68.9 12.2 %all-gather.8.cloned.1.call-done = bf16[25600,128]{1,0:T(8,128)(2,1)} async-done(((bf16[1600,128]{1,0:T(8,128)(2,1)}), bf16[25600,128]{1,0:T(8,128)(2,1)}) %all-gather.8.cloned.1.call-update) | async-done | bytes 6553616 | tf_op jit(solution)/shard_map/all_gather | solution.py:434
  81.1 9.5 %solve_first.1 = (f32[2048,128]{1,0:T(8,128)}, f32[512,128]{1,0:T(8,128)}, s16[16,304,128]{2,1,0:T(8,128)(2,1)}) custom-call(s32[4,16]{1,0:T(4,128)} %bitcast.27, bf16[16,1600,128]{2,1,0:T(8,128)(2,1)} %bitcast.32, bf16[2048,128]{1,0:T(8,128)(2,1)} %bitcast.18, bf16[128,2048]{1,0:T(8,128)(2,1)} %copy-done.3, s16[16,304,128]{2,1,0:T(8,128)(2,1)} %bitcast.33, ...), custom_call_target="tpu_custom_call" | custom-call | flops 2147483648 | bytes 14680064 | tf_op jit(solution)/shard_map/solve_first/pallas_call | solution.py:390
  90.7 6.5 %all-to-all-start = ((s16[16,304,128]{2,1,0:T(8,128)(2,1)}), s16[16,304,128]{2,1,0:T(8,128)(2,1)S(1)}, u32[]{:S(2)}, u32[]{:S(2)}) async-start(s16[16,304,128]{2,1,0:T(8,128)(2,1)} %get-tuple-element.29), calls=%async_computation | async-start | bytes 2490368 | tf_op jit(solution)/shard_map/all_to_all | solution.py:445
  97.3 0.6 dynamic_slice.8
  99.8 0.2 turn.3.turned_ref
  100.0 0.8 copy-done.4
  100.8 15.9 %all-to-all-done = s16[16,304,128]{2,1,0:T(8,128)(2,1)S(1)} async-done(((s16[16,304,128]{2,1,0:T(8,128)(2,1)}), s16[16,304,128]{2,1,0:T(8,128)(2,1)S(1)}, u32[]{:S(2)}, u32[]{:S(2)}) %all-to-all-start) | async-done | bytes 1245216 | tf_op jit(solution)/shard_map/all_to_all | solution.py:445
  116.8 24.7 %all-gather.12.ancestor_ref = s16[16,304,128]{2,1,0:T(8,128)(2,1)} all-gather(s16[1,304,128]{2,1,0:T(8,128)(2,1)S(1)} %constant_dynamic-slice_fusion), channel_id=1, replica_groups=mesh['leaf'=16,'row'=16] {'row'}, dimensions={0}, use_global_device_ids=true | all-gather | bytes 1323008 | tf_op jit(solution)/shard_map/all_gather | solution.py:447
  141.5 8.3 %solve_second.1 = (f32[2048,128]{1,0:T(8,128)}, f32[512,128]{1,0:T(8,128)}) custom-call(s32[4,16]{1,0:T(4,128)} %bitcast.35, bf16[16,1600,128]{2,1,0:T(8,128)(2,1)} %bitcast.31, bf16[2048,128]{1,0:T(8,128)(2,1)} %bitcast.21, bf16[128,2048]{1,0:T(8,128)(2,1)} %copy-done.4, s16[16,304,128]{2,1,0:T(8,128)(2,1)} %all-gather.12.ancestor_ref), custom_call_target="tpu_custom_call" | custom-call | flops 2147483648 | bytes 14680064 | tf_op jit(solution)/shard_map/solve_second/pallas_call | solution.py:390
  (25 shorter events, 0.1 us)
Async XLA Ops:
  7.2 10.2 %copy-start.8 = (s32[16,4]{0,1:T(4,128)S(1)}, s32[16,4]{0,1:T(4,128)}, u32[]{:S(2)}) copy-start(s32[16,4]{0,1:T(4,128)} %param.13) | copy-start | bytes 772
  7.2 19.1 %copy-start.9 = (s32[1,4,1]{1,2,0:T(1,128)S(1)}, s32[1,4,1]{1,2,0:T(1,128)}, u32[]{:S(2)}) copy-start(s32[1,4,1]{1,2,0:T(1,128)} %param.14) | copy-start | bytes 52
  7.2 19.1 %copy-start.6 = (bf16[1,512,128]{2,1,0:T(8,128)(2,1)S(1)}, bf16[1,512,128]{2,1,0:T(8,128)(2,1)}, u32[]{:S(2)}) copy-start(bf16[1,512,128]{2,1,0:T(8,128)(2,1)} %param.12) | copy-start | bytes 393220
  7.2 73.9 %all-gather.8.cloned.1.call-start = ((), (), s32[]{:S(2)}) async-start(), calls=%async_computation.1 | async-start | bytes 6963200 | tf_op jit(solution)/shard_map/all_gather | solution.py:434
  8.2 18.1 %collective-permute-start = (bf16[960,128]{1,0:T(8,128)(2,1)S(1)}, bf16[960,128]{1,0:T(8,128)(2,1)S(1)}, u32[]{:S(2)}, u32[]{:S(2)}) collective-permute-start(bf16[960,128]{1,0:T(8,128)(2,1)S(1)} %slice_bitcast_fusion), channel_id=1, source_target_pairs={{0,15},{1,14},{2,13},{3,12},{4,11},{5,10},{6,9},{7,8},{8,7},{9,6},... | collective-permute-start | bytes 737288 | tf_op jit(solution)/shard_map/ppermute | solution.py:426
  15.3 1.0 copy-start
  16.3 10.0 %copy-start.1 = (bf16[1,2048,128]{2,1,0:T(8,128)(2,1)S(1)}, bf16[1,2048,128]{2,1,0:T(8,128)(2,1)}, u32[]{:S(2)}) copy-start(bf16[1,2048,128]{2,1,0:T(8,128)(2,1)} %param.11) | copy-start | bytes 1572868
  16.5 0.8 copy-start.3
  17.3 1.2 copy-start.5
  18.6 9.2 %copy-start.2 = (bf16[1,2048,128]{2,1,0:T(8,128)(2,1)S(1)}, bf16[1,2048,128]{2,1,0:T(8,128)(2,1)}, u32[]{:S(2)}) copy-start(bf16[1,2048,128]{2,1,0:T(8,128)(2,1)} %param.15) | copy-start | bytes 1572868
  27.7 39.9 %copy-start.7 = (bf16[1,512,128]{2,1,0:T(8,128)(2,1)S(1)}, bf16[1,512,128]{2,1,0:T(8,128)(2,1)}, u32[]{:S(2)}) copy-start(bf16[1,512,128]{2,1,0:T(8,128)(2,1)} %param.16) | copy-start | bytes 393220
  27.7 39.9 %copy-start.10 = (s32[1,4,1]{1,2,0:T(1,128)S(1)}, s32[1,4,1]{1,2,0:T(1,128)}, u32[]{:S(2)}) copy-start(s32[1,4,1]{1,2,0:T(1,128)} %param.18) | copy-start | bytes 52
  27.7 113.8 %all-gather.10.cloned.1.call-start = ((), (), s32[]{:S(2)}) async-start(), calls=%async_computation.2 | async-start | bytes 6963200 | tf_op jit(solution)/shard_map/all_gather | solution.py:441
  27.8 39.8 %collective-permute-start.1 = (bf16[960,128]{1,0:T(8,128)(2,1)S(1)}, bf16[960,128]{1,0:T(8,128)(2,1)S(1)}, u32[]{:S(2)}, u32[]{:S(2)}) collective-permute-start(bf16[960,128]{1,0:T(8,128)(2,1)S(1)} %slice.7), channel_id=1, source_target_pairs={{0,15},{1,14},{2,13},{3,12},{4,11},{5,10},{6,9},{7,8},{8,7},{9,6},... | collective-permute-start | bytes 737288 | tf_op jit(solution)/shard_map/ppermute | solution.py:435
  90.7 6.6 %copy-start.11 = (s32[16]{0:T(128)S(1)}, s32[16]{0:T(128)}, u32[]{:S(2)}) copy-start(s32[16]{0:T(128)} %param.19) | copy-start | bytes 196
  90.7 26.1 %all-to-all-start = ((s16[16,304,128]{2,1,0:T(8,128)(2,1)}), s16[16,304,128]{2,1,0:T(8,128)(2,1)S(1)}, u32[]{:S(2)}, u32[]{:S(2)}) async-start(s16[16,304,128]{2,1,0:T(8,128)(2,1)} %get-tuple-element.29), calls=%async_computation | async-start | bytes 2490368 | tf_op jit(solution)/shard_map/all_to_all | solution.py:445
  100.0 0.8 copy-start.4
Sparse Core Ops, SparseCore 0:
  27.8 53.2 all-gather.7
  82.9 49.7 all-gather.9

commit v7 on v6

--- a/solution.py
+++ b/solution.py
@@ -239,6 +239,16 @@
         sh[pl.ds(a * TILE, TILE), pl.ds(b * TILE, TILE)] = high
         sl[pl.ds(a * TILE, TILE), pl.ds(b * TILE, TILE)] = low
 
+    own_copy.wait()
+    uppers = [jnp.zeros((kb // 2, TILE), F32) for _ in range(2)]
+    for i in range(4):
+        for copy in lm_copies[i * 4 : (i + 1) * 4]:
+            copy.wait()
+        rows = pl.ds(i * 4 * TILE, 4 * TILE)
+        for m in range(2):
+            part = pl.ds(m * (kb // 2), kb // 2)
+            uppers[m] = uppers[m] + dot(lm[part, rows], own[rows, :])
+    upper = jnp.concatenate(uppers, axis=0)
     for copy in s_copies:
         copy.wait()
     halves = []
@@ -273,12 +283,6 @@
         values = jnp.concatenate([halves[a], halves[b].T[HALF:]], axis=0)
         store(b, a, values)
         store(a, b, values.T)
-    own_copy.wait()
-    for copy in lm_copies:
-        copy.wait()
-    upper = jnp.concatenate(
-        [dot(lm[pl.ds(i * (kb // 2), kb // 2), :], own[...]) for i in range(2)], axis=0
-    )
     upper_high, upper_low = split(upper)
     upper_both = jnp.concatenate([upper_high, upper_low], axis=1)
     crosses = []
@@ -437,7 +441,6 @@
     ancestor_one, other_two = lax.optimization_barrier((ancestor_one, other_two))
     turned_two = turn(later_two)
     packed_two = pack(blocks, mask_two, panel_two[0], later_two, other_two)
-    gathered_one, packed_two = lax.optimization_barrier((gathered_one, packed_two))
     gathered_two = lax.all_gather(packed_two, "row", axis=0)
     sigma_first, cross_first, slots = solve(
         tiles_one, gathered_one, linv_one[0], turned_one, kb, ancestor_one, tiles_two

time: 157 us -> 156 us (level)
  transfers between devices with their start and end apart: 5 -> 5, of which waited for: 3 -> 3; matrix products, arithmetic and copies ran while one was open for 0% -> 0% of each run, Pallas kernels for 8% -> 7%
where the time goes in v7:
time: 156 us
  blocking collectives  61.4 us (39%)
  waiting for transfers between devices  35.2 us (23%)
  Pallas kernels  20.2 us (13%)
  starting transfers between devices  17.5 us (11%)
  between operations  16.1 us (10%)
  local copies, waits for them, and re-layouts  5.52 us (4%)
    all_gather x1, blocking collectives, body(): ancestor_one = lax.all_gather(coded_one, 'row', axis=0)  36 us
    all_gather x1, blocking collectives, body(): ancestor_two = lax.all_gather(chosen, 'row', axis=0)  25.4 us
    pallas_call x2, Pallas kernels, solve(): pl.pallas_call(functools.partial(solve_kernel, first, blocks, kb), out_sh...  16.5 us
    all_to_all x1, waiting for transfers between devices, body(): lax.all_to_all(slots, 'leaf', split_axis=0, concat_axis=0, tiled=True)  15.9 us
    all_gather x1, waiting for transfers between devices, body(): gathered_one = lax.all_gather(packed_one, 'row', axis=0)  12.2 us
    ppermute x1, starting transfers between devices, body(): other_one = lax.ppermute(linv_one[0, :cut], 'row', fold)  7.05 us
    ppermute x1, waiting for transfers between devices, body(): other_one = lax.ppermute(linv_one[0, :cut], 'row', fold)  7.03 us
    all_to_all x1, starting transfers between devices, body(): lax.all_to_all(slots, 'leaf', split_axis=0, concat_axis=0, tiled=True)  6.54 us
  transfers between devices with their start and end apart: 5, of which 3 were waited for; matrix products, arithmetic and copies ran while one was open for 0% of the time, Pallas kernels for 7%

profile of v7, /device:TPU:1, one launch (start us, length us, event | category | flops | bytes accessed | tf_op | source)
XLA Modules:
  0.0 156.0 jit_solution(2374639603478884455)
XLA Ops:
  7.2 0.0 all-gather.8.cloned.1.call-start
  7.2 1.0 slice_bitcast_fusion
  8.2 7.1 %collective-permute-start = (bf16[960,128]{1,0:T(8,128)(2,1)S(1)}, bf16[960,128]{1,0:T(8,128)(2,1)S(1)}, u32[]{:S(2)}, u32[]{:S(2)}) collective-permute-start(bf16[960,128]{1,0:T(8,128)(2,1)S(1)} %slice_bitcast_fusion), channel_id=1, source_target_pairs={{0,15},{1,14},{2,13},{3,12},{4,11},{5,10},{6,9},{7,8},{8,7},{9,6},... | collective-permute-start | bytes 737288 | tf_op jit(solution)/shard_map/ppermute | solution.py:430
  15.3 1.0 copy-done
  16.3 0.2 turn.2.turned_ref
  16.6 0.8 copy-done.3
  17.3 1.2 copy-done.5
  18.6 0.7 code.1
  19.3 7.0 %collective-permute-done.other_ref = bf16[960,128]{1,0:T(8,128)(2,1)S(1)} collective-permute-done((bf16[960,128]{1,0:T(8,128)(2,1)S(1)}, bf16[960,128]{1,0:T(8,128)(2,1)S(1)}, u32[]{:S(2)}, u32[]{:S(2)}) %collective-permute-start) | collective-permute-done | bytes 245792 | tf_op jit(solution)/shard_map/ppermute | solution.py:430
  26.3 1.3 pack.2
  27.7 0.0 all-gather.8.cloned.1.call-update
  27.7 0.0 all-gather.10.cloned.1.call-start
  27.8 3.8 %collective-permute-start.1 = (bf16[960,128]{1,0:T(8,128)(2,1)S(1)}, bf16[960,128]{1,0:T(8,128)(2,1)S(1)}, u32[]{:S(2)}, u32[]{:S(2)}) collective-permute-start(bf16[960,128]{1,0:T(8,128)(2,1)S(1)} %slice.7), channel_id=1, source_target_pairs={{0,15},{1,14},{2,13},{3,12},{4,11},{5,10},{6,9},{7,8},{8,7},{9,6},... | collective-permute-start | bytes 737288 | tf_op jit(solution)/shard_map/ppermute | solution.py:439
  31.6 36.0 %all-gather.11 = s16[4864,128]{1,0:T(8,128)(2,1)} all-gather(s16[304,128]{1,0:T(8,128)(2,1)S(1)} %code.1), channel_id=3, replica_groups=mesh['leaf'=16,'row'=16] {'row'}, dimensions={0}, use_global_device_ids=true | all-gather | bytes 1323008 | tf_op jit(solution)/shard_map/all_gather | solution.py:440
  67.6 1.3 pack.3
  68.9 12.2 %all-gather.8.cloned.1.call-done = bf16[25600,128]{1,0:T(8,128)(2,1)} async-done(((bf16[1600,128]{1,0:T(8,128)(2,1)}), bf16[25600,128]{1,0:T(8,128)(2,1)}) %all-gather.8.cloned.1.call-update) | async-done | bytes 6553616 | tf_op jit(solution)/shard_map/all_gather | solution.py:438
  81.1 8.8 %solve_first.1 = (f32[2048,128]{1,0:T(8,128)}, f32[512,128]{1,0:T(8,128)}, s16[16,304,128]{2,1,0:T(8,128)(2,1)}) custom-call(s32[4,16]{1,0:T(4,128)} %bitcast.27, bf16[16,1600,128]{2,1,0:T(8,128)(2,1)} %bitcast.32, bf16[2048,128]{1,0:T(8,128)(2,1)} %bitcast.18, bf16[128,2048]{1,0:T(8,128)(2,1)} %copy-done.3, s16[16,304,128]{2,1,0:T(8,128)(2,1)} %bitcast.33, ...), custom_call_target="tpu_custom_call" | custom-call | flops 2147483648 | bytes 14680064 | tf_op jit(solution)/shard_map/solve_first/pallas_call | solution.py:394
  90.0 6.5 %all-to-all-start = ((s16[16,304,128]{2,1,0:T(8,128)(2,1)}), s16[16,304,128]{2,1,0:T(8,128)(2,1)S(1)}, u32[]{:S(2)}, u32[]{:S(2)}) async-start(s16[16,304,128]{2,1,0:T(8,128)(2,1)} %get-tuple-element.25), calls=%async_computation | async-start | bytes 2490368 | tf_op jit(solution)/shard_map/all_to_all | solution.py:448
  96.5 0.6 dynamic_slice.8
  99.0 0.2 turn.3.turned_ref
  99.3 0.8 copy-done.4
  100.1 15.9 %all-to-all-done = s16[16,304,128]{2,1,0:T(8,128)(2,1)S(1)} async-done(((s16[16,304,128]{2,1,0:T(8,128)(2,1)}), s16[16,304,128]{2,1,0:T(8,128)(2,1)S(1)}, u32[]{:S(2)}, u32[]{:S(2)}) %all-to-all-start) | async-done | bytes 1245216 | tf_op jit(solution)/shard_map/all_to_all | solution.py:448
  116.1 25.4 %all-gather.12.ancestor_ref = s16[16,304,128]{2,1,0:T(8,128)(2,1)} all-gather(s16[1,304,128]{2,1,0:T(8,128)(2,1)S(1)} %constant_dynamic-slice_fusion), channel_id=1, replica_groups=mesh['leaf'=16,'row'=16] {'row'}, dimensions={0}, use_global_device_ids=true | all-gather | bytes 1323008 | tf_op jit(solution)/shard_map/all_gather | solution.py:450
  141.5 7.6 %solve_second.1 = (f32[2048,128]{1,0:T(8,128)}, f32[512,128]{1,0:T(8,128)}) custom-call(s32[4,16]{1,0:T(4,128)} %bitcast.35, bf16[16,1600,128]{2,1,0:T(8,128)(2,1)} %bitcast.31, bf16[2048,128]{1,0:T(8,128)(2,1)} %bitcast.21, bf16[128,2048]{1,0:T(8,128)(2,1)} %copy-done.4, s16[16,304,128]{2,1,0:T(8,128)(2,1)} %all-gather.12.ancestor_ref), custom_call_target="tpu_custom_call" | custom-call | flops 2147483648 | bytes 14680064 | tf_op jit(solution)/shard_map/solve_second/pallas_call | solution.py:394
  (25 shorter events, 0.1 us)
Async XLA Ops:
  7.2 10.2 %copy-start.8 = (s32[16,4]{0,1:T(4,128)S(1)}, s32[16,4]{0,1:T(4,128)}, u32[]{:S(2)}) copy-start(s32[16,4]{0,1:T(4,128)} %param.13) | copy-start | bytes 772
  7.2 19.1 %copy-start.9 = (s32[1,4,1]{1,2,0:T(1,128)S(1)}, s32[1,4,1]{1,2,0:T(1,128)}, u32[]{:S(2)}) copy-start(s32[1,4,1]{1,2,0:T(1,128)} %param.14) | copy-start | bytes 52
  7.2 19.1 %copy-start.6 = (bf16[1,512,128]{2,1,0:T(8,128)(2,1)S(1)}, bf16[1,512,128]{2,1,0:T(8,128)(2,1)}, u32[]{:S(2)}) copy-start(bf16[1,512,128]{2,1,0:T(8,128)(2,1)} %param.12) | copy-start | bytes 393220
  7.2 73.9 %all-gather.8.cloned.1.call-start = ((), (), s32[]{:S(2)}) async-start(), calls=%async_computation.1 | async-start | bytes 6963200 | tf_op jit(solution)/shard_map/all_gather | solution.py:438
  8.2 18.1 %collective-permute-start = (bf16[960,128]{1,0:T(8,128)(2,1)S(1)}, bf16[960,128]{1,0:T(8,128)(2,1)S(1)}, u32[]{:S(2)}, u32[]{:S(2)}) collective-permute-start(bf16[960,128]{1,0:T(8,128)(2,1)S(1)} %slice_bitcast_fusion), channel_id=1, source_target_pairs={{0,15},{1,14},{2,13},{3,12},{4,11},{5,10},{6,9},{7,8},{8,7},{9,6},... | collective-permute-start | bytes 737288 | tf_op jit(solution)/shard_map/ppermute | solution.py:430
  15.3 1.0 copy-start
  16.3 10.0 %copy-start.1 = (bf16[1,2048,128]{2,1,0:T(8,128)(2,1)S(1)}, bf16[1,2048,128]{2,1,0:T(8,128)(2,1)}, u32[]{:S(2)}) copy-start(bf16[1,2048,128]{2,1,0:T(8,128)(2,1)} %param.11) | copy-start | bytes 1572868
  16.5 0.8 copy-start.3
  17.3 1.2 copy-start.5
  18.6 9.2 %copy-start.2 = (bf16[1,2048,128]{2,1,0:T(8,128)(2,1)S(1)}, bf16[1,2048,128]{2,1,0:T(8,128)(2,1)}, u32[]{:S(2)}) copy-start(bf16[1,2048,128]{2,1,0:T(8,128)(2,1)} %param.15) | copy-start | bytes 1572868
  27.7 39.9 %copy-start.7 = (bf16[1,512,128]{2,1,0:T(8,128)(2,1)S(1)}, bf16[1,512,128]{2,1,0:T(8,128)(2,1)}, u32[]{:S(2)}) copy-start(bf16[1,512,128]{2,1,0:T(8,128)(2,1)} %param.16) | copy-start | bytes 393220
  27.7 39.9 %copy-start.10 = (s32[1,4,1]{1,2,0:T(1,128)S(1)}, s32[1,4,1]{1,2,0:T(1,128)}, u32[]{:S(2)}) copy-start(s32[1,4,1]{1,2,0:T(1,128)} %param.18) | copy-start | bytes 52
  27.7 113.8 %all-gather.10.cloned.1.call-start = ((), (), s32[]{:S(2)}) async-start(), calls=%async_computation.2 | async-start | bytes 6963200 | tf_op jit(solution)/shard_map/all_gather | solution.py:444
  27.8 39.8 %collective-permute-start.1 = (bf16[960,128]{1,0:T(8,128)(2,1)S(1)}, bf16[960,128]{1,0:T(8,128)(2,1)S(1)}, u32[]{:S(2)}, u32[]{:S(2)}) collective-permute-start(bf16[960,128]{1,0:T(8,128)(2,1)S(1)} %slice.7), channel_id=1, source_target_pairs={{0,15},{1,14},{2,13},{3,12},{4,11},{5,10},{6,9},{7,8},{8,7},{9,6},... | collective-permute-start | bytes 737288 | tf_op jit(solution)/shard_map/ppermute | solution.py:439
  89.9 6.6 %copy-start.11 = (s32[16]{0:T(128)S(1)}, s32[16]{0:T(128)}, u32[]{:S(2)}) copy-start(s32[16]{0:T(128)} %param.19) | copy-start | bytes 196
  90.0 26.1 %all-to-all-start = ((s16[16,304,128]{2,1,0:T(8,128)(2,1)}), s16[16,304,128]{2,1,0:T(8,128)(2,1)S(1)}, u32[]{:S(2)}, u32[]{:S(2)}) async-start(s16[16,304,128]{2,1,0:T(8,128)(2,1)} %get-tuple-element.25), calls=%async_computation | async-start | bytes 2490368 | tf_op jit(solution)/shard_map/all_to_all | solution.py:448
  99.3 0.8 copy-start.4
Sparse Core Ops, SparseCore 0:
  27.8 53.2 all-gather.7
  82.9 50.1 all-gather.9

commit v8 on v7

--- a/solution.py
+++ b/solution.py
@@ -32,7 +32,7 @@
 
 
 def code_tile(x):
-    peak = jnp.max(jnp.abs(x), axis=0, keepdims=True)
+    peak = jnp.maximum(jnp.max(jnp.abs(x), axis=0, keepdims=True), 2.0**-110)
     code = jnp.clip(jnp.ceil(jnp.log2(peak) * STEPS), -110.0 * STEPS, 127.0 * STEPS)
     levels = jnp.round(x * (TOP / jnp.exp2(code * (1.0 / STEPS))))
     return levels.astype(jnp.int32), code
@@ -93,16 +93,13 @@
     )(tiles, select)
 
 
-def pack_kernel(blocks, mask_ref, panel_ref, linv_ref, other_ref, out_ref):
+def pack_kernel(blocks, panel_ref, linv_ref, other_ref, out_ref):
     kb = panel_ref.shape[0]
     ns = linv_ref.shape[0]
     cut = other_ref.shape[0]
     half = blocks // 2
     row_id = lax.axis_index("row")
-    for a in range(kb // TILE):
-        rows = pl.ds(a * TILE, TILE)
-        weight = mask_ref[a].astype(F32)
-        out_ref[rows, :] = (panel_ref[rows, :].astype(F32) * weight).astype(BF)
+    out_ref[pl.ds(0, kb), :] = panel_ref[...]
 
     @pl.when(row_id < half)
     def _():
@@ -121,42 +118,49 @@
         out_ref[pl.ds(kb + cut, TILE), :] = linv_ref[pl.ds(ns - TILE, TILE), :]
 
 
-def turn_kernel(linv_ref, turned_ref):
+def ready_kernel(mask_ref, panel_ref, linv_ref, masked_ref, turned_ref):
+    for a in range(panel_ref.shape[0] // TILE):
+        rows = pl.ds(a * TILE, TILE)
+        weight = mask_ref[a].astype(F32)
+        masked_ref[rows, :] = (panel_ref[rows, :].astype(F32) * weight).astype(BF)
     for c in range(linv_ref.shape[0] // TILE):
         rows = pl.ds(c * TILE, TILE)
         turned_ref[:, rows] = linv_ref[rows, :].astype(F32).T.astype(BF)
 
 
-def turn(linv):
+def ready(mask, panel, linv):
     ns, width = linv.shape
     return pl.pallas_call(
-        turn_kernel,
-        out_shape=jax.ShapeDtypeStruct((width, ns), BF),
-        in_specs=[VMEM_SPEC],
-        out_specs=VMEM_SPEC,
+        ready_kernel,
+        out_shape=[
+            jax.ShapeDtypeStruct(panel.shape, BF),
+            jax.ShapeDtypeStruct((width, ns), BF),
+        ],
+        in_specs=[SMEM_SPEC, VMEM_SPEC, VMEM_SPEC],
+        out_specs=[VMEM_SPEC, VMEM_SPEC],
         compiler_params=pltpu.CompilerParams(vmem_limit_bytes=VMEM_LIMIT),
         cost_estimate=pl.CostEstimate(
             flops=0, transcendentals=0, bytes_accessed=2 * 2 * ns * width
         ),
-        name="turn",
-    )(linv)
-
-
-def pack(blocks, mask, panel, linv, other):
+        name="ready",
+    )(mask, panel, linv)
+
+
+def pack(blocks, panel, linv, other):
     kb, width = panel.shape
     ns = linv.shape[0]
     rows = kb + ns - other.shape[0]
     return pl.pallas_call(
         functools.partial(pack_kernel, blocks),
         out_shape=jax.ShapeDtypeStruct((rows, width), BF),
-        in_specs=[SMEM_SPEC, VMEM_SPEC, VMEM_SPEC, VMEM_SPEC],
+        in_specs=[VMEM_SPEC, VMEM_SPEC, VMEM_SPEC],
         out_specs=VMEM_SPEC,
         compiler_params=pltpu.CompilerParams(vmem_limit_bytes=VMEM_LIMIT),
         cost_estimate=pl.CostEstimate(
             flops=0, transcendentals=0, bytes_accessed=2 * 2 * rows * width
         ),
         name="pack",
-    )(mask, panel, linv, other)
+    )(panel, linv, other)
 
 
 def column_parts(c, blocks, kb):
@@ -429,9 +433,9 @@
 
     other_one = lax.ppermute(linv_one[0, :cut], "row", fold)
     coded_one = code(tiles_one, sigma_root)
-    turned_one = turn(linv_one[0])
+    masked_one, turned_one = ready(mask_one, panel_one[0], linv_one[0])
     other_one, later_two = lax.optimization_barrier((other_one, linv_two[0]))
-    packed_one = pack(blocks, mask_one, panel_one[0], linv_one[0], other_one)
+    packed_one = pack(blocks, masked_one, linv_one[0], other_one)
     packed_one, coded_one, turned_one = lax.optimization_barrier(
         (packed_one, coded_one, turned_one)
     )
@@ -439,8 +443,8 @@
     other_two = lax.ppermute(later_two[:cut], "row", fold)
     ancestor_one = lax.all_gather(coded_one, "row", axis=0)
     ancestor_one, other_two = lax.optimization_barrier((ancestor_one, other_two))
-    turned_two = turn(later_two)
-    packed_two = pack(blocks, mask_two, panel_two[0], later_two, other_two)
+    masked_two, turned_two = ready(mask_two, panel_two[0], later_two)
+    packed_two = pack(blocks, masked_two, later_two, other_two)
     gathered_two = lax.all_gather(packed_two, "row", axis=0)
     sigma_first, cross_first, slots = solve(
         tiles_one, gathered_one, linv_one[0], turned_one, kb, ancestor_one, tiles_two

time: 156 us -> 156 us (level)
  waiting for transfers between devices: 35.2 us -> 32.4 us
  local copies, waits for them, and re-layouts: 5.52 us -> 7.71 us
    ppermute x1, waiting for transfers between devices: 7.03 us -> 4.25 us  [body(): other_one = lax.ppermute(linv_one[0, :cut], 'row', fold)]
    unnamed x24, local copies, waits for them, and re-layouts: 3.92 us -> 6.14 us
  transfers between devices with their start and end apart: 5 -> 5, of which waited for: 3 -> 3; matrix products, arithmetic and copies ran while one was open for 0% -> 0% of each run, Pallas kernels for 7% -> 8%
where the time goes in v8:
time: 156 us; the launch traced here: 155 us
  blocking collectives  61.4 us (39%)
  waiting for transfers between devices  32.4 us (21%)
  Pallas kernels  20.2 us (13%)
  starting transfers between devices  17.5 us (11%)
  between operations  16.1 us (10%)
  local copies, waits for them, and re-layouts  7.71 us (5%)
    all_gather x1, blocking collectives, body(): ancestor_one = lax.all_gather(coded_one, 'row', axis=0)  36 us
    all_gather x1, blocking collectives, body(): ancestor_two = lax.all_gather(chosen, 'row', axis=0)  25.4 us
    all_to_all x1, waiting for transfers between devices, body(): lax.all_to_all(slots, 'leaf', split_axis=0, concat_axis=0, tiled=True)  17 us
    pallas_call x2, Pallas kernels, solve(): pl.pallas_call(functools.partial(solve_kernel, first, blocks, kb), out_sh...  16.5 us
    all_gather x1, waiting for transfers between devices, body(): gathered_one = lax.all_gather(packed_one, 'row', axis=0)  11.1 us
    ppermute x1, starting transfers between devices, body(): other_one = lax.ppermute(linv_one[0, :cut], 'row', fold)  7.05 us
    all_to_all x1, starting transfers between devices, body(): lax.all_to_all(slots, 'leaf', split_axis=0, concat_axis=0, tiled=True)  6.54 us
    unnamed x24, local copies, waits for them, and re-layouts  6.14 us
  transfers between devices with their start and end apart: 5, of which 3 were waited for; matrix products, arithmetic and copies ran while one was open for 0% of the time, Pallas kernels for 8%

profile of v8, /device:TPU:1, one launch (start us, length us, event | category | flops | bytes accessed | tf_op | source)
XLA Modules:
  0.0 155.4 jit_solution(15634891754278338611)
XLA Ops:
  7.2 1.0 slice_bitcast_fusion
  8.2 7.1 %collective-permute-start = (bf16[960,128]{1,0:T(8,128)(2,1)S(1)}, bf16[960,128]{1,0:T(8,128)(2,1)S(1)}, u32[]{:S(2)}, u32[]{:S(2)}) collective-permute-start(bf16[960,128]{1,0:T(8,128)(2,1)S(1)} %slice_bitcast_fusion), channel_id=1, source_target_pairs={{0,15},{1,14},{2,13},{3,12},{4,11},{5,10},{6,9},{7,8},{8,7},{9,6},... | collective-permute-start | bytes 737288 | tf_op jit(solution)/shard_map/ppermute | solution.py:434
  15.2 1.0 copy-done
  16.3 0.9 copy-done.6
  17.2 0.7 copy-done.9
  17.8 0.7 ready.2
  18.6 0.8 copy-done.5
  19.4 1.2 copy-done.3
  20.6 0.7 copy-done.8
  21.3 0.7 code.1
  22.0 4.2 %collective-permute-done.other_ref = bf16[960,128]{1,0:T(8,128)(2,1)S(1)} collective-permute-done((bf16[960,128]{1,0:T(8,128)(2,1)S(1)}, bf16[960,128]{1,0:T(8,128)(2,1)S(1)}, u32[]{:S(2)}, u32[]{:S(2)}) %collective-permute-start) | collective-permute-done | bytes 245792 | tf_op jit(solution)/shard_map/ppermute | solution.py:434
  26.3 0.8 pack.2
  27.2 3.8 %collective-permute-start.1 = (bf16[960,128]{1,0:T(8,128)(2,1)S(1)}, bf16[960,128]{1,0:T(8,128)(2,1)S(1)}, u32[]{:S(2)}, u32[]{:S(2)}) collective-permute-start(bf16[960,128]{1,0:T(8,128)(2,1)S(1)} %slice.7), channel_id=1, source_target_pairs={{0,15},{1,14},{2,13},{3,12},{4,11},{5,10},{6,9},{7,8},{8,7},{9,6},... | collective-permute-start | bytes 737288 | tf_op jit(solution)/shard_map/ppermute | solution.py:443
  31.0 36.0 %all-gather.11 = s16[4864,128]{1,0:T(8,128)(2,1)} all-gather(s16[304,128]{1,0:T(8,128)(2,1)S(1)} %code.1), channel_id=3, replica_groups=mesh['leaf'=16,'row'=16] {'row'}, dimensions={0}, use_global_device_ids=true | all-gather | bytes 1323008 | tf_op jit(solution)/shard_map/all_gather | solution.py:444
  66.9 0.7 ready.3
  67.7 0.8 copy-done.4
  68.5 0.8 pack.3
  69.3 11.1 %all-gather.8.cloned.1.call-done = bf16[25600,128]{1,0:T(8,128)(2,1)} async-done(((bf16[1600,128]{1,0:T(8,128)(2,1)}), bf16[25600,128]{1,0:T(8,128)(2,1)}) %all-gather.8.cloned.1.call-update) | async-done | bytes 6553616 | tf_op jit(solution)/shard_map/all_gather | solution.py:442
  80.5 8.8 %solve_first.1 = (f32[2048,128]{1,0:T(8,128)}, f32[512,128]{1,0:T(8,128)}, s16[16,304,128]{2,1,0:T(8,128)(2,1)}) custom-call(s32[4,16]{1,0:T(4,128)} %bitcast.27, bf16[16,1600,128]{2,1,0:T(8,128)(2,1)} %bitcast.32, bf16[2048,128]{1,0:T(8,128)(2,1)} %bitcast.18, bf16[128,2048]{1,0:T(8,128)(2,1)} %copy-done.5, s16[16,304,128]{2,1,0:T(8,128)(2,1)} %bitcast.33, ...), custom_call_target="tpu_custom_call" | custom-call | flops 2147483648 | bytes 14680064 | tf_op jit(solution)/shard_map/solve_first/pallas_call | solution.py:398
  89.3 6.5 %all-to-all-start = ((s16[16,304,128]{2,1,0:T(8,128)(2,1)}), s16[16,304,128]{2,1,0:T(8,128)(2,1)S(1)}, u32[]{:S(2)}, u32[]{:S(2)}) async-start(s16[16,304,128]{2,1,0:T(8,128)(2,1)} %get-tuple-element.33), calls=%async_computation | async-start | bytes 2490368 | tf_op jit(solution)/shard_map/all_to_all | solution.py:452
  95.9 0.6 dynamic_slice.8
  98.4 17.0 %all-to-all-done = s16[16,304,128]{2,1,0:T(8,128)(2,1)S(1)} async-done(((s16[16,304,128]{2,1,0:T(8,128)(2,1)}), s16[16,304,128]{2,1,0:T(8,128)(2,1)S(1)}, u32[]{:S(2)}, u32[]{:S(2)}) %all-to-all-start) | async-done | bytes 1245216 | tf_op jit(solution)/shard_map/all_to_all | solution.py:452
  115.4 25.4 %all-gather.12.ancestor_ref = s16[16,304,128]{2,1,0:T(8,128)(2,1)} all-gather(s16[1,304,128]{2,1,0:T(8,128)(2,1)S(1)} %constant_dynamic-slice_fusion), channel_id=1, replica_groups=mesh['leaf'=16,'row'=16] {'row'}, dimensions={0}, use_global_device_ids=true | all-gather | bytes 1323008 | tf_op jit(solution)/shard_map/all_gather | solution.py:454
  140.9 7.6 %solve_second.1 = (f32[2048,128]{1,0:T(8,128)}, f32[512,128]{1,0:T(8,128)}) custom-call(s32[4,16]{1,0:T(4,128)} %bitcast.35, bf16[16,1600,128]{2,1,0:T(8,128)(2,1)} %bitcast.31, bf16[2048,128]{1,0:T(8,128)(2,1)} %bitcast.21, bf16[128,2048]{1,0:T(8,128)(2,1)} %copy-done.4, s16[16,304,128]{2,1,0:T(8,128)(2,1)} %all-gather.12.ancestor_ref), custom_call_target="tpu_custom_call" | custom-call | flops 2147483648 | bytes 14680064 | tf_op jit(solution)/shard_map/solve_second/pallas_call | solution.py:398
  (25 shorter events, 0.2 us)
Async XLA Ops:
  7.2 73.3 %all-gather.8.cloned.1.call-start = ((), (), s32[]{:S(2)}) async-start(), calls=%async_computation.1 | async-start | bytes 6963200 | tf_op jit(solution)/shard_map/all_gather | solution.py:442
  8.2 18.1 %collective-permute-start = (bf16[960,128]{1,0:T(8,128)(2,1)S(1)}, bf16[960,128]{1,0:T(8,128)(2,1)S(1)}, u32[]{:S(2)}, u32[]{:S(2)}) collective-permute-start(bf16[960,128]{1,0:T(8,128)(2,1)S(1)} %slice_bitcast_fusion), channel_id=1, source_target_pairs={{0,15},{1,14},{2,13},{3,12},{4,11},{5,10},{6,9},{7,8},{8,7},{9,6},... | collective-permute-start | bytes 737288 | tf_op jit(solution)/shard_map/ppermute | solution.py:434
  15.2 1.0 copy-start
  16.3 0.9 copy-start.6
  17.2 0.7 copy-start.9
  17.8 8.4 %copy-start.1 = (bf16[1,2048,128]{2,1,0:T(8,128)(2,1)S(1)}, bf16[1,2048,128]{2,1,0:T(8,128)(2,1)}, u32[]{:S(2)}) copy-start(bf16[1,2048,128]{2,1,0:T(8,128)(2,1)} %param.11) | copy-start | bytes 1572868
  18.6 0.8 copy-start.5
  19.4 1.2 copy-start.3
  20.6 0.7 copy-start.8
  21.3 5.8 %copy-start.2 = (bf16[1,2048,128]{2,1,0:T(8,128)(2,1)S(1)}, bf16[1,2048,128]{2,1,0:T(8,128)(2,1)}, u32[]{:S(2)}) copy-start(bf16[1,2048,128]{2,1,0:T(8,128)(2,1)} %param.15) | copy-start | bytes 1572868
  27.0 39.9 %copy-start.7 = (bf16[1,512,128]{2,1,0:T(8,128)(2,1)S(1)}, bf16[1,512,128]{2,1,0:T(8,128)(2,1)}, u32[]{:S(2)}) copy-start(bf16[1,512,128]{2,1,0:T(8,128)(2,1)} %param.16) | copy-start | bytes 393220
  27.0 39.9 %copy-start.10 = (s32[1,4,1]{1,2,0:T(1,128)S(1)}, s32[1,4,1]{1,2,0:T(1,128)}, u32[]{:S(2)}) copy-start(s32[1,4,1]{1,2,0:T(1,128)} %param.18) | copy-start | bytes 52
  27.1 113.8 %all-gather.10.cloned.1.call-start = ((), (), s32[]{:S(2)}) async-start(), calls=%async_computation.2 | async-start | bytes 6963200 | tf_op jit(solution)/shard_map/all_gather | solution.py:448
  27.2 41.4 %collective-permute-start.1 = (bf16[960,128]{1,0:T(8,128)(2,1)S(1)}, bf16[960,128]{1,0:T(8,128)(2,1)S(1)}, u32[]{:S(2)}, u32[]{:S(2)}) collective-permute-start(bf16[960,128]{1,0:T(8,128)(2,1)S(1)} %slice.7), channel_id=1, source_target_pairs={{0,15},{1,14},{2,13},{3,12},{4,11},{5,10},{6,9},{7,8},{8,7},{9,6},... | collective-permute-start | bytes 737288 | tf_op jit(solution)/shard_map/ppermute | solution.py:443
  67.7 0.8 copy-start.4
  89.3 6.6 %copy-start.11 = (s32[16]{0:T(128)S(1)}, s32[16]{0:T(128)}, u32[]{:S(2)}) copy-start(s32[16]{0:T(128)} %param.19) | copy-start | bytes 196
  89.3 26.1 %all-to-all-start = ((s16[16,304,128]{2,1,0:T(8,128)(2,1)}), s16[16,304,128]{2,1,0:T(8,128)(2,1)S(1)}, u32[]{:S(2)}, u32[]{:S(2)}) async-start(s16[16,304,128]{2,1,0:T(8,128)(2,1)} %get-tuple-element.33), calls=%async_computation | async-start | bytes 2490368 | tf_op jit(solution)/shard_map/all_to_all | solution.py:452
Sparse Core Ops, SparseCore 0:
  27.2 53.2 all-gather.7
  82.3 50.1 all-gather.9

commit v9 on v8

--- a/solution.py
+++ b/solution.py
@@ -245,10 +245,10 @@
 
     own_copy.wait()
     uppers = [jnp.zeros((kb // 2, TILE), F32) for _ in range(2)]
-    for i in range(4):
-        for copy in lm_copies[i * 4 : (i + 1) * 4]:
+    for i in range(8):
+        for copy in lm_copies[i * 2 : (i + 1) * 2]:
             copy.wait()
-        rows = pl.ds(i * 4 * TILE, 4 * TILE)
+        rows = pl.ds(i * 2 * TILE, 2 * TILE)
         for m in range(2):
             part = pl.ds(m * (kb // 2), kb // 2)
             uppers[m] = uppers[m] + dot(lm[part, rows], own[rows, :])

time: 156 us -> 156 us (level)
  no operation moved by 1% of the time
where the time goes in v9:
time: 156 us; the launch traced here: 155 us
  blocking collectives  61.4 us (39%)
  waiting for transfers between devices  32.5 us (21%)
  Pallas kernels  20.2 us (13%)
  starting transfers between devices  17.5 us (11%)
  between operations  16.1 us (10%)
  local copies, waits for them, and re-layouts  7.71 us (5%)
    all_gather x1, blocking collectives, body(): ancestor_one = lax.all_gather(coded_one, 'row', axis=0)  36 us
    all_gather x1, blocking collectives, body(): ancestor_two = lax.all_gather(chosen, 'row', axis=0)  25.4 us
    all_to_all x1, waiting for transfers between devices, body(): lax.all_to_all(slots, 'leaf', split_axis=0, concat_axis=0, tiled=True)  17 us
    pallas_call x2, Pallas kernels, solve(): pl.pallas_call(functools.partial(solve_kernel, first, blocks, kb), out_sh...  16.5 us
    all_gather x1, waiting for transfers between devices, body(): gathered_one = lax.all_gather(packed_one, 'row', axis=0)  11.1 us
    ppermute x1, starting transfers between devices, body(): other_one = lax.ppermute(linv_one[0, :cut], 'row', fold)  7.05 us
    all_to_all x1, starting transfers between devices, body(): lax.all_to_all(slots, 'leaf', split_axis=0, concat_axis=0, tiled=True)  6.54 us
    unnamed x24, local copies, waits for them, and re-layouts  6.14 us
  transfers between devices with their start and end apart: 5, of which 3 were waited for; matrix products, arithmetic and copies ran while one was open for 0% of the time, Pallas kernels for 8%

profile of v9, /device:TPU:1, one launch (start us, length us, event | category | flops | bytes accessed | tf_op | source)
XLA Modules:
  0.0 155.4 jit_solution(15621712450235445031)
XLA Ops:
  7.2 1.0 slice_bitcast_fusion
  8.2 7.1 %collective-permute-start = (bf16[960,128]{1,0:T(8,128)(2,1)S(1)}, bf16[960,128]{1,0:T(8,128)(2,1)S(1)}, u32[]{:S(2)}, u32[]{:S(2)}) collective-permute-start(bf16[960,128]{1,0:T(8,128)(2,1)S(1)} %slice_bitcast_fusion), channel_id=1, source_target_pairs={{0,15},{1,14},{2,13},{3,12},{4,11},{5,10},{6,9},{7,8},{8,7},{9,6},... | collective-permute-start | bytes 737288 | tf_op jit(solution)/shard_map/ppermute | solution.py:434
  15.2 1.0 copy-done
  16.3 0.9 copy-done.6
  17.2 0.7 copy-done.9
  17.8 0.7 ready.2
  18.6 0.8 copy-done.5
  19.4 1.2 copy-done.3
  20.6 0.7 copy-done.8
  21.3 0.7 code.1
  22.0 4.2 %collective-permute-done.other_ref = bf16[960,128]{1,0:T(8,128)(2,1)S(1)} collective-permute-done((bf16[960,128]{1,0:T(8,128)(2,1)S(1)}, bf16[960,128]{1,0:T(8,128)(2,1)S(1)}, u32[]{:S(2)}, u32[]{:S(2)}) %collective-permute-start) | collective-permute-done | bytes 245792 | tf_op jit(solution)/shard_map/ppermute | solution.py:434
  26.3 0.8 pack.2
  27.2 3.8 %collective-permute-start.1 = (bf16[960,128]{1,0:T(8,128)(2,1)S(1)}, bf16[960,128]{1,0:T(8,128)(2,1)S(1)}, u32[]{:S(2)}, u32[]{:S(2)}) collective-permute-start(bf16[960,128]{1,0:T(8,128)(2,1)S(1)} %slice.7), channel_id=1, source_target_pairs={{0,15},{1,14},{2,13},{3,12},{4,11},{5,10},{6,9},{7,8},{8,7},{9,6},... | collective-permute-start | bytes 737288 | tf_op jit(solution)/shard_map/ppermute | solution.py:443
  31.0 36.0 %all-gather.11 = s16[4864,128]{1,0:T(8,128)(2,1)} all-gather(s16[304,128]{1,0:T(8,128)(2,1)S(1)} %code.1), channel_id=3, replica_groups=mesh['leaf'=16,'row'=16] {'row'}, dimensions={0}, use_global_device_ids=true | all-gather | bytes 1323008 | tf_op jit(solution)/shard_map/all_gather | solution.py:444
  66.9 0.7 ready.3
  67.7 0.8 copy-done.4
  68.5 0.8 pack.3
  69.3 11.1 %all-gather.8.cloned.1.call-done = bf16[25600,128]{1,0:T(8,128)(2,1)} async-done(((bf16[1600,128]{1,0:T(8,128)(2,1)}), bf16[25600,128]{1,0:T(8,128)(2,1)}) %all-gather.8.cloned.1.call-update) | async-done | bytes 6553616 | tf_op jit(solution)/shard_map/all_gather | solution.py:442
  80.5 8.8 %solve_first.1 = (f32[2048,128]{1,0:T(8,128)}, f32[512,128]{1,0:T(8,128)}, s16[16,304,128]{2,1,0:T(8,128)(2,1)}) custom-call(s32[4,16]{1,0:T(4,128)} %bitcast.27, bf16[16,1600,128]{2,1,0:T(8,128)(2,1)} %bitcast.32, bf16[2048,128]{1,0:T(8,128)(2,1)} %bitcast.18, bf16[128,2048]{1,0:T(8,128)(2,1)} %copy-done.5, s16[16,304,128]{2,1,0:T(8,128)(2,1)} %bitcast.33, ...), custom_call_target="tpu_custom_call" | custom-call | flops 2147483648 | bytes 14680064 | tf_op jit(solution)/shard_map/solve_first/pallas_call | solution.py:398
  89.3 6.5 %all-to-all-start = ((s16[16,304,128]{2,1,0:T(8,128)(2,1)}), s16[16,304,128]{2,1,0:T(8,128)(2,1)S(1)}, u32[]{:S(2)}, u32[]{:S(2)}) async-start(s16[16,304,128]{2,1,0:T(8,128)(2,1)} %get-tuple-element.33), calls=%async_computation | async-start | bytes 2490368 | tf_op jit(solution)/shard_map/all_to_all | solution.py:452
  95.9 0.6 dynamic_slice.8
  98.4 17.0 %all-to-all-done = s16[16,304,128]{2,1,0:T(8,128)(2,1)S(1)} async-done(((s16[16,304,128]{2,1,0:T(8,128)(2,1)}), s16[16,304,128]{2,1,0:T(8,128)(2,1)S(1)}, u32[]{:S(2)}, u32[]{:S(2)}) %all-to-all-start) | async-done | bytes 1245216 | tf_op jit(solution)/shard_map/all_to_all | solution.py:452
  115.5 25.4 %all-gather.12.ancestor_ref = s16[16,304,128]{2,1,0:T(8,128)(2,1)} all-gather(s16[1,304,128]{2,1,0:T(8,128)(2,1)S(1)} %constant_dynamic-slice_fusion), channel_id=1, replica_groups=mesh['leaf'=16,'row'=16] {'row'}, dimensions={0}, use_global_device_ids=true | all-gather | bytes 1323008 | tf_op jit(solution)/shard_map/all_gather | solution.py:454
  140.9 7.6 %solve_second.1 = (f32[2048,128]{1,0:T(8,128)}, f32[512,128]{1,0:T(8,128)}) custom-call(s32[4,16]{1,0:T(4,128)} %bitcast.35, bf16[16,1600,128]{2,1,0:T(8,128)(2,1)} %bitcast.31, bf16[2048,128]{1,0:T(8,128)(2,1)} %bitcast.21, bf16[128,2048]{1,0:T(8,128)(2,1)} %copy-done.4, s16[16,304,128]{2,1,0:T(8,128)(2,1)} %all-gather.12.ancestor_ref), custom_call_target="tpu_custom_call" | custom-call | flops 2147483648 | bytes 14680064 | tf_op jit(solution)/shard_map/solve_second/pallas_call | solution.py:398
  (25 shorter events, 0.2 us)
Async XLA Ops:
  7.2 73.3 %all-gather.8.cloned.1.call-start = ((), (), s32[]{:S(2)}) async-start(), calls=%async_computation.1 | async-start | bytes 6963200 | tf_op jit(solution)/shard_map/all_gather | solution.py:442
  8.2 18.1 %collective-permute-start = (bf16[960,128]{1,0:T(8,128)(2,1)S(1)}, bf16[960,128]{1,0:T(8,128)(2,1)S(1)}, u32[]{:S(2)}, u32[]{:S(2)}) collective-permute-start(bf16[960,128]{1,0:T(8,128)(2,1)S(1)} %slice_bitcast_fusion), channel_id=1, source_target_pairs={{0,15},{1,14},{2,13},{3,12},{4,11},{5,10},{6,9},{7,8},{8,7},{9,6},... | collective-permute-start | bytes 737288 | tf_op jit(solution)/shard_map/ppermute | solution.py:434
  15.2 1.0 copy-start
  16.3 0.9 copy-start.6
  17.2 0.7 copy-start.9
  17.8 8.4 %copy-start.1 = (bf16[1,2048,128]{2,1,0:T(8,128)(2,1)S(1)}, bf16[1,2048,128]{2,1,0:T(8,128)(2,1)}, u32[]{:S(2)}) copy-start(bf16[1,2048,128]{2,1,0:T(8,128)(2,1)} %param.11) | copy-start | bytes 1572868
  18.6 0.8 copy-start.5
  19.4 1.2 copy-start.3
  20.6 0.7 copy-start.8
  21.3 5.8 %copy-start.2 = (bf16[1,2048,128]{2,1,0:T(8,128)(2,1)S(1)}, bf16[1,2048,128]{2,1,0:T(8,128)(2,1)}, u32[]{:S(2)}) copy-start(bf16[1,2048,128]{2,1,0:T(8,128)(2,1)} %param.15) | copy-start | bytes 1572868
  27.0 39.9 %copy-start.7 = (bf16[1,512,128]{2,1,0:T(8,128)(2,1)S(1)}, bf16[1,512,128]{2,1,0:T(8,128)(2,1)}, u32[]{:S(2)}) copy-start(bf16[1,512,128]{2,1,0:T(8,128)(2,1)} %param.16) | copy-start | bytes 393220
  27.0 39.9 %copy-start.10 = (s32[1,4,1]{1,2,0:T(1,128)S(1)}, s32[1,4,1]{1,2,0:T(1,128)}, u32[]{:S(2)}) copy-start(s32[1,4,1]{1,2,0:T(1,128)} %param.18) | copy-start | bytes 52
  27.1 113.8 %all-gather.10.cloned.1.call-start = ((), (), s32[]{:S(2)}) async-start(), calls=%async_computation.2 | async-start | bytes 6963200 | tf_op jit(solution)/shard_map/all_gather | solution.py:448
  27.2 41.4 %collective-permute-start.1 = (bf16[960,128]{1,0:T(8,128)(2,1)S(1)}, bf16[960,128]{1,0:T(8,128)(2,1)S(1)}, u32[]{:S(2)}, u32[]{:S(2)}) collective-permute-start(bf16[960,128]{1,0:T(8,128)(2,1)S(1)} %slice.7), channel_id=1, source_target_pairs={{0,15},{1,14},{2,13},{3,12},{4,11},{5,10},{6,9},{7,8},{8,7},{9,6},... | collective-permute-start | bytes 737288 | tf_op jit(solution)/shard_map/ppermute | solution.py:443
  67.7 0.8 copy-start.4
  89.3 6.6 %copy-start.11 = (s32[16]{0:T(128)S(1)}, s32[16]{0:T(128)}, u32[]{:S(2)}) copy-start(s32[16]{0:T(128)} %param.19) | copy-start | bytes 196
  89.3 26.1 %all-to-all-start = ((s16[16,304,128]{2,1,0:T(8,128)(2,1)}), s16[16,304,128]{2,1,0:T(8,128)(2,1)S(1)}, u32[]{:S(2)}, u32[]{:S(2)}) async-start(s16[16,304,128]{2,1,0:T(8,128)(2,1)} %get-tuple-element.33), calls=%async_computation | async-start | bytes 2490368 | tf_op jit(solution)/shard_map/all_to_all | solution.py:452
Sparse Core Ops, SparseCore 0:
  27.2 53.2 all-gather.7
  82.3 50.1 all-gather.9
